TPU v7x, 32 devices: a whole 2x2x4 slice. The times are simulated.
32 devices in a mesh: dp: 16 (over z, y, x), fsdp: 2 (over core).
Axes of the slice: x: 2, y: 2, z: 4, core: 2. Of those that a mesh axis runs over, the one named last changes fastest.
Arguments:
- hidden_in: bfloat16 [32, 704, 1024], P(('dp', 'fsdp')), may hold values from -6 to 6
- cluster_lengths: int32 [32, 8], P(('dp', 'fsdp')), may hold values from 1 to 192, 704 in all within a row
- norm_gain: bfloat16 [1024], P('fsdp'), may hold values from 0.099609375 to 1.8984375
- in_proj: bfloat16 [1024, 4096], P('fsdp'), may hold values from -0.1875 to 0.1875
- conv_weight: bfloat16 [4, 2048], P(None, 'fsdp'), may hold values from -3 to 3
- conv_bias: bfloat16 [2048], P('fsdp'), may hold values from -3 to 3
- x_proj: bfloat16 [2048, 96], P('fsdp'), may hold values from -0.125 to 0.125
- dt_proj: bfloat16 [64, 2048], P(None, 'fsdp'), may hold values from -0.75 to 0.75
- dt_bias: bfloat16 [2048], P('fsdp'), may hold values from -6 to -2.5
- a_log: bfloat16 [16, 2048], P(None, 'fsdp'), may hold values from 0 to 2.765625
- skip_gain: bfloat16 [2048], P('fsdp'), may hold values from 0.5 to 1.5
- out_proj: bfloat16 [2048, 1024], P('fsdp'), may hold values from -0.125 to 0.125
- out_grad: bfloat16 [32, 704, 1024], P(('dp', 'fsdp')), may hold values from -6 to 6
Outputs:
- layer_out: bfloat16 [32, 704, 1024], P(('dp', 'fsdp'))
- input_grad: float32 [32, 704, 1024], P(('dp', 'fsdp'))
- grad_norm_gain: float32 [1024], P('fsdp')
- grad_in_proj: float32 [1024, 4096], P('fsdp')
- grad_conv_weight: float32 [4, 2048], P(None, 'fsdp')
- grad_conv_bias: float32 [2048], P('fsdp')
- grad_x_proj: float32 [2048, 96], P('fsdp')
- grad_dt_proj: float32 [64, 2048], P(None, 'fsdp')
- grad_dt_bias: float32 [2048], P('fsdp')
- grad_a_log: float32 [16, 2048], P(None, 'fsdp')
- grad_skip_gain: float32 [2048], P('fsdp')
- grad_out_proj: float32 [2048, 1024], P('fsdp')
Inputs may be any that keep to these rules, and one draw needn't show every extreme that they name: `cluster_lengths`: each row lists the 8 cluster lengths of one context; they sum to 704, and each context's longest cluster has exactly 192 tokens.
All inputs are finite; a program needn't handle non-finite values.
Results may differ from a plain program's by a relative error of at most 0.011.
Values may be sent and summed in bfloat16 or wider, within the bound.
A program may use at most 256 MiB of HBM per device.

v0:
```python
import functools
import math

import jax
import jax.numpy as jnp
from jax import lax
from jax.experimental import pallas as pl
from jax.experimental.pallas import tpu as pltpu
from jax.sharding import PartitionSpec as P

CHUNK = 64
WIDTH = 4
norm_eps = 1e-05

def bits_of(size):
    return size.bit_length() - 1


ORDERS = ((0, 1, 2, 3), (1, 2, 0, 3), (2, 0, 1, 3))


class Reduction:
    def __init__(self, outer, inner, shapes, parts):
        self.outer_bits, self.inner_bits = bits_of(outer), bits_of(inner)
        self.blocks, self.inner = outer * inner, inner
        self.shapes = [(self.blocks, s[0] // self.blocks, s[1]) for s in shapes]
        self.stages = self.outer_bits + self.inner_bits
        self.steps = self.stages + self.inner_bits
        self.pieces = []
        for i, s in enumerate(shapes):
            at = 0
            for columns, order in parts[i]:
                order = [b for b in order if b < self.inner_bits] + list(range(len(order), self.inner_bits))
                self.pieces.append((i, pl.ds(at, columns), order))
                at += columns
            assert at == s[1]

    def axis_bit(self, piece, stage):
        if stage < self.outer_bits:
            return "fsdp", self.outer_bits - 1 - stage
        return "dp", self.pieces[piece][2][stage - self.outer_bits]

    def mine(self, piece, stage):
        axis, bit = self.axis_bit(piece, stage)
        return (lax.axis_index(axis) // (1 << bit)) % 2

    def partner(self, axis, bit):
        here = lax.axis_index(axis)
        return {axis: here + (1 << bit) - (here // (1 << bit)) % 2 * (2 << bit)}

    def barrier(self):
        sem = pltpu.get_barrier_semaphore()
        for axis, bits in (("fsdp", self.outer_bits), ("dp", self.inner_bits)):
            for bit in range(bits):
                pl.semaphore_signal(sem, inc=1, device_id=self.partner(axis, bit), device_id_type=pl.DeviceIdType.MESH)
        pl.semaphore_wait(sem, self.stages)

    def low(self, piece, stage):
        low = 0
        for s in range(1, stage):
            low = low + self.mine(piece, s) * (self.blocks >> (s + 1))
        return low

    def place(self, piece, stages):
        at = 0
        for j in range(stages):
            at = at + self.mine(piece, self.outer_bits + j) * (1 << (self.inner_bits - 1 - j))
        return at

    def bind(self, given, out, scratch):
        n = len(self.shapes)
        self.given, self.out = given, out
        self.work, self.inbox, self.result = scratch[:n], scratch[n : 2 * n], scratch[2 * n : 3 * n]
        self.send, self.recv, self.near = scratch[3 * n :]

    def scratch(self):
        b16, k = jnp.bfloat16, len(self.pieces)
        return (
            [pltpu.VMEM((b // 2, r, c), b16) for b, r, c in self.shapes]
            + [pltpu.VMEM((b, r, c), b16) for b, r, c in self.shapes]
            + [pltpu.VMEM((self.inner, r, c), b16) for b, r, c in self.shapes]
            + [pltpu.SemaphoreType.DMA((k, self.steps)), pltpu.SemaphoreType.DMA((k, self.steps)), pltpu.SemaphoreType.DMA((k,))]
        )

    def copy(self, piece, step):
        i, columns, _ = self.pieces[piece]
        if step < self.stages:
            stage = step
            half = self.blocks >> (step + 1)
            other = (1 - self.mine(piece, step)) * half
            if step == 0:
                source = self.given[i].at[pl.ds(other, half), :, columns]
            else:
                source = self.work[i].at[pl.ds(self.low(piece, step) + other, half), :, columns]
            target = self.inbox[i].at[pl.ds(self.blocks - 2 * half, half), :, columns]
        else:
            stage = self.steps - 1 - step + self.outer_bits
            j = stage - self.outer_bits
            many = 1 << (self.inner_bits - 1 - j)
            source = target = self.result[i].at[pl.ds(self.place(piece, j + 1), many), :, columns]
        return pltpu.make_async_remote_copy(
            src_ref=source,
            dst_ref=target,
            send_sem=self.send.at[piece, step],
            recv_sem=self.recv.at[piece, step],
            device_id=self.partner(*self.axis_bit(piece, stage)),
            device_id_type=pl.DeviceIdType.MESH,
        )

    def own(self, piece):
        i, columns, _ = self.pieces[piece]
        half = self.blocks // 2
        source = self.given[i].at[pl.ds(self.mine(piece, 0) * half, half), :, columns]
        return pltpu.make_async_copy(source, self.work[i].at[:, :, columns], self.near.at[piece])

    def leave(self, piece):
        i, columns, _ = self.pieces[piece]
        return pltpu.make_async_copy(self.result[i].at[:, :, columns], self.out[i].at[:, :, columns], self.near.at[piece])

    def add(self, piece, stage):
        i, columns, _ = self.pieces[piece]
        work, inbox, result = self.work[i], self.inbox[i], self.result[i]
        half = self.blocks >> (stage + 1)
        arrived = self.blocks - 2 * half
        base = 0 if stage == 0 else self.low(piece, stage) + self.mine(piece, stage) * half

        @pl.loop(0, half)
        def _(k):
            new = work[base + k, :, columns].astype(jnp.float32) + inbox[arrived + k, :, columns].astype(jnp.float32)
            if stage == self.stages - 1:
                result[self.place(piece, self.inner_bits), :, columns] = new.astype(jnp.bfloat16)
            else:
                work[base + k, :, columns] = new.astype(jnp.bfloat16)

    def begin(self):
        self.barrier()
        for p in range(len(self.pieces)):
            self.copy(p, 0).start()
        for p in range(len(self.pieces)):
            self.own(p).start()

    def finish(self, step):
        for p in range(len(self.pieces)):
            if step == 0:
                self.own(p).wait()
            self.copy(p, step).wait()
            if step < self.stages:
                self.add(p, step)
            if step + 1 < self.steps:
                self.copy(p, step + 1).start()
            else:
                self.leave(p).start()
        if step + 1 == self.steps:
            for p in range(len(self.pieces)):
                self.leave(p).wait()

    def times(self, count):
        heavy = (2.0, 1.3)
        there = [heavy[j] if j < len(heavy) else 1.0 for j in range(self.inner_bits)]
        loads = [1.2] * self.outer_bits + there + there[::-1]
        total, at, out = sum(loads), 0.0, []
        for load in loads[:-1]:
            at += load
            out.append(max(1, min(count - 1, round(at / total * count))))
        return out


def reduce_kernel(*refs, plan):
    n = len(plan.shapes)
    plan.bind(refs[:n], refs[n : 2 * n], refs[2 * n :])
    plan.begin()
    for step in range(plan.steps):
        plan.finish(step)


def reduction_of(arrays, parts):
    plan = Reduction(lax.axis_size("fsdp"), lax.axis_size("dp"), [a.shape for a in arrays], parts)
    shaped = [a.reshape(s) for a, s in zip(arrays, plan.shapes)]
    out = [jax.ShapeDtypeStruct((plan.inner,) + s[1:], jnp.bfloat16) for s in plan.shapes]
    return plan, shaped, out


def reduce_all(arrays, parts, ident):
    plan, shaped, out = reduction_of(arrays, parts)
    anywhere = pl.BlockSpec(memory_space=pl.ANY)
    out = pl.pallas_call(
        functools.partial(reduce_kernel, plan=plan),
        out_shape=out,
        in_specs=[anywhere] * len(arrays),
        out_specs=[anywhere] * len(arrays),
        scratch_shapes=plan.scratch(),
        compiler_params=pltpu.CompilerParams(collective_id=ident, has_side_effects=True, vmem_limit_bytes=56 << 20),
        name="reduce_all",
    )(*shaped)
    return [o.reshape(-1, o.shape[-1]) for o in out]


BIG = 1e30
LN2 = math.log(2.0)
LOG2E = 1.0 / LN2
TAPS, SHIFT, DT_BIAS, SKIP = 0, 4, 5, 6


def rows_of(ref, tile, row, width):
    return [ref[tile + j, pl.ds(row, 8, stride=0), :] for j in range(width)]


def by_eights(ref, tile):
    total = ref[tile, pl.ds(0, 8, stride=8), :]
    for s in range(1, 8):
        total = total + ref[tile, pl.ds(s, 8, stride=8), :]
    return total


def folded(x):
    total = x[:8]
    for s in range(8, x.shape[0], 8):
        total = total + x[s : s + 8]
    return total


def spread(proj, first, wide, states):
    for t in range(proj.shape[1]):
        wide[pl.ds(t * states, states), :] = jnp.broadcast_to(proj[first : first + states, t : t + 1], (states, 128))


def forward_kernel(
    upper_ref, z_ref, dg_ref, off_ref, par_ref, xp_ref, dtw_ref, a_ref,
    u_ref, ds_ref, dt_ref, sg_ref, dy_ref, gated_ref, gate_ref, proj_ref, wide_b, wide_c, bound_ref, skip_ref,
    hs, ext, u16, dtm, dtu, ys, ybuf, *, width
):
    f32, bf16 = jnp.float32, jnp.bfloat16
    rows, inner = upper_ref.shape
    states, rank = a_ref.shape[0], dtw_ref.shape[0]
    tiles = inner // 128

    @pl.when(pl.program_id(0) == 0)
    def _():
        hs[...] = jnp.zeros_like(hs)
        skip_ref[...] = jnp.zeros_like(skip_ref)
        ext[pl.ds(0, 8), :] = jnp.zeros((8, inner), f32)

    bound_ref[0] = hs[...]

    @pl.loop(0, tiles, unroll=True)
    def _(k):
        lanes = pl.ds(pl.multiple_of(k * 128, 128), 128)
        now = upper_ref[:, lanes]
        ext[pl.ds(8, rows), lanes] = now
        conv = par_ref[SHIFT : SHIFT + 1, lanes] + par_ref[TAPS + 3 : TAPS + 4, lanes] * now
        for lag in range(1, 4):
            before = ext[pl.ds(8 - lag, rows), lanes]
            conv = conv + par_ref[TAPS + 3 - lag : TAPS + 4 - lag, lanes] * jnp.where(off_ref[...] >= lag, before, 0.0)
        sig = jax.nn.sigmoid(conv)
        act = conv * sig
        u_ref[:, lanes] = act
        u16[:, lanes] = act.astype(bf16)
        ds_ref[:, lanes] = sig * (1.0 + conv * (1.0 - sig))
        ext[pl.ds(0, 8), lanes] = now[rows - 8 :]

    proj = lax.dot_general(xp_ref[...], u16[...], (((1,), (1,)), ((), ())), preferred_element_type=f32)
    proj_ref[0] = proj
    spread(proj, rank, wide_b, states)
    spread(proj, rank + states, wide_c, states)
    rank16 = proj[:rank].astype(bf16)

    @pl.loop(0, tiles // 2, unroll=True)
    def _(k):
        pair = pl.ds(pl.multiple_of(k * 256, 256), 256)
        pre = lax.dot_general(rank16, dtw_ref[:, pair], (((0,), (0,)), ((), ())), preferred_element_type=f32)
        pre = pre + par_ref[DT_BIAS : DT_BIAS + 1, pair]
        small = jnp.exp(-jnp.abs(pre))
        delta = jnp.maximum(pre, 0.0) + jnp.log1p(small)
        dt_ref[:, pair] = delta
        sg_ref[:, pair] = jnp.where(pre >= 0, 1.0, small) / (1.0 + small)
        grown = delta * u_ref[:, pair]
        for j in range(2):
            part = slice(128 * j, 128 * j + 128)
            dtm[2 * k + j] = jnp.where(off_ref[...] > 0, delta[:, part], BIG)
            dtu[2 * k + j] = grown[:, part]

    @pl.loop(0, tiles // width)
    def _(cb):
        tile = cb * width
        base = pl.multiple_of(cb * 128 * width, 128 * width)
        rate = [[a_ref[pl.ds(8 * s, 8), pl.ds(base + 128 * j, 128)] for s in range(2)] for j in range(width)]

        def body(g, h):
            h = [list(p) for p in zip(h[:width], h[width:])]
            r0 = pl.multiple_of(g * 8, 8)
            for t in range(8):
                d = rows_of(dtm, tile, r0 + t, width)
                x = rows_of(dtu, tile, r0 + t, width)
                bt = [wide_b[pl.ds((r0 + t) * 16 + 8 * s, 8), :] for s in range(2)]
                ct = [wide_c[pl.ds((r0 + t) * 16 + 8 * s, 8), :] for s in range(2)]
                for j in range(width):
                    for s in range(2):
                        h[j][s] = jnp.exp2(d[j] * rate[j][s]) * h[j][s] + x[j] * bt[s]
                    ybuf[j, pl.ds(t * 8, 8), :] = ct[0] * h[j][0] + ct[1] * h[j][1]
            for j in range(width):
                ys[tile + j, pl.ds(r0, 8), :] = by_eights(ybuf, j)
            return tuple(p[0] for p in h) + tuple(p[1] for p in h)

        h = tuple(hs[pl.ds(8 * s, 8), pl.ds(base + 128 * j, 128)] for s in range(2) for j in range(width))
        h = lax.fori_loop(0, rows // 8, body, h, unroll=4)
        for s in range(2):
            for j in range(width):
                hs[pl.ds(8 * s, 8), pl.ds(base + 128 * j, 128)] = h[s * width + j]

    @pl.loop(0, tiles, unroll=True)
    def _(k):
        lanes = pl.ds(pl.multiple_of(k * 128, 128), 128)
        act, z, dg = u_ref[:, lanes], z_ref[:, lanes], dg_ref[:, lanes]
        full = ys[k] + par_ref[SKIP : SKIP + 1, lanes] * act
        sig = jax.nn.sigmoid(z)
        silu = z * sig
        gated_ref[:, lanes] = (full * silu).astype(bf16)
        dy = dg * silu
        dy_ref[:, lanes] = dy
        gate_ref[:, lanes] = (dg * full * sig * (1.0 + z * (1.0 - sig))).astype(bf16)
        skip_ref[:, lanes] = skip_ref[:, lanes] + folded(dy * act)


def scan_forward(both, d_gated, offset, params, xp, dtw, rate, chunk, width):
    T, DI = d_gated.shape
    n, states, cols = T // chunk, rate.shape[0], xp.shape[0]
    f32, bf16 = jnp.float32, jnp.bfloat16
    row = pl.BlockSpec((chunk, DI), lambda i: (i, 0))
    whole = lambda a: pl.BlockSpec(a.shape, lambda i: (0, 0))
    flat = lambda d: jax.ShapeDtypeStruct((T, DI), d)
    tile = lambda d: pltpu.VMEM((DI // 128, chunk, 128), d)
    return pl.pallas_call(
        functools.partial(forward_kernel, width=width),
        grid=(n,),
        in_specs=[row, pl.BlockSpec((chunk, DI), lambda i: (i, 1)), row, pl.BlockSpec((chunk, 128), lambda i: (i, 0))]
        + [whole(a) for a in (params, xp, dtw, rate)],
        out_specs=[row] * 7
        + [
            pl.BlockSpec((1, cols, chunk), lambda i: (i, 0, 0)),
            pl.BlockSpec((chunk * states, 128), lambda i: (i, 0)),
            pl.BlockSpec((chunk * states, 128), lambda i: (i, 0)),
            pl.BlockSpec((1, states, DI), lambda i: (i, 0, 0)),
            pl.BlockSpec((8, DI), lambda i: (0, 0)),
        ],
        out_shape=[flat(f32)] * 5
        + [flat(bf16)] * 2
        + [
            jax.ShapeDtypeStruct((n, cols, chunk), f32),
            jax.ShapeDtypeStruct((T * states, 128), f32),
            jax.ShapeDtypeStruct((T * states, 128), f32),
            jax.ShapeDtypeStruct((n, states, DI), f32),
            jax.ShapeDtypeStruct((8, DI), f32),
        ],
        scratch_shapes=[
            pltpu.VMEM((states, DI), f32),
            pltpu.VMEM((chunk + 8, DI), f32),
            pltpu.VMEM((chunk, DI), bf16),
            tile(f32),
            tile(f32),
            tile(f32),
            pltpu.VMEM((width, 64, 128), f32),
        ],
        compiler_params=pltpu.CompilerParams(dimension_semantics=("arbitrary",), vmem_limit_bytes=48 << 20),
        name="scan_forward",
    )(both, both, d_gated, offset, params, xp, dtw, rate)


def backward_kernel(
    u_ref, ds_ref, dt_ref, sg_ref, dy_ref, upper_ref, off_ref, proj_ref, wide_b, wide_c, bound_ref, par_ref, xp_ref, dtw_ref, a_ref,
    *rest, width, plan, total
):
    f32, bf16 = jnp.float32, jnp.bfloat16
    n = len(plan.shapes)
    given, rest = rest[:n], rest[n:]
    (du_ref, ga_ref, gdt_ref, gx_ref, sum_ref), out, rest = rest[:5], rest[5 : 5 + n], rest[5 + n :]
    ws, dtm, dtu, dyb, hbuf, sbuf, qbuf, dd, di, u16, dt16, ext, off_ext, wide_db, wide_dc, cols_ref = rest[:16]
    plan.bind(given, out, rest[16:])
    rows, inner = u_ref.shape
    states, rank = a_ref.shape[0], dtw_ref.shape[0]
    tiles = inner // 128
    times = plan.times(total // rows)

    @pl.when(pl.program_id(0) == 0)
    def _():
        for ref in (ws, ga_ref, gdt_ref, gx_ref, sum_ref):
            ref[...] = jnp.zeros_like(ref)
        ext[pl.ds(rows, 8), :] = jnp.zeros((8, inner), f32)
        off_ext[pl.ds(rows, 8), :] = jnp.full((8, 128), -1, jnp.int32)
        plan.begin()

    for at in sorted(set(times)):
        @pl.when(pl.program_id(0) == at)
        def _():
            for step in range(plan.steps - 1):
                if times[step] == at:
                    plan.finish(step)

    proj = proj_ref[0]
    wide_db[...] = jnp.zeros_like(wide_db)
    wide_dc[...] = jnp.zeros_like(wide_dc)

    @pl.loop(0, tiles // width)
    def _(cb):
        tile = cb * width
        base = pl.multiple_of(cb * 128 * width, 128 * width)
        for j in range(width):
            lanes = pl.ds(base + 128 * j, 128)
            d, act = dt_ref[:, lanes], u_ref[:, lanes]
            dtm[j] = jnp.where(off_ref[...] > 0, d, BIG)
            dtu[j] = d * act
            dyb[j] = dy_ref[:, lanes]
            u16[:, lanes] = act.astype(bf16)
        rate = [[a_ref[pl.ds(8 * s, 8), pl.ds(base + 128 * j, 128)] for s in range(2)] for j in range(width)]

        def again(g, h):
            h = [list(p) for p in zip(h[:width], h[width:])]
            r0 = pl.multiple_of(g * 8, 8)
            for t in range(8):
                d = rows_of(dtm, 0, r0 + t, width)
                x = rows_of(dtu, 0, r0 + t, width)
                bt = [wide_b[pl.ds((r0 + t) * 16 + 8 * s, 8), :] for s in range(2)]
                for j in range(width):
                    for s in range(2):
                        hbuf[pl.ds((r0 + t) * 16 + 8 * s, 8), pl.ds(128 * j, 128)] = h[j][s]
                        h[j][s] = jnp.exp2(d[j] * rate[j][s]) * h[j][s] + x[j] * bt[s]
            return tuple(p[0] for p in h) + tuple(p[1] for p in h)

        h = tuple(bound_ref[0, pl.ds(8 * s, 8), pl.ds(base + 128 * j, 128)] for s in range(2) for j in range(width))
        h = lax.fori_loop(0, rows // 8, again, h)
        for s in range(2):
            for j in range(width):
                hbuf[pl.ds(rows * 16 + 8 * s, 8), pl.ds(128 * j, 128)] = h[s * width + j]

        def body(k, carry):
            r0 = pl.multiple_of((rows // 8 - 1 - k) * 8, 8)
            w = [[carry[s * width + j] for s in range(2)] for j in range(width)]
            ga = [[carry[2 * width + s * width + j] for s in range(2)] for j in range(width)]
            newer = [[hbuf[pl.ds((r0 + 8) * 16 + 8 * s, 8), pl.ds(128 * j, 128)] for s in range(2)] for j in range(width)]
            for t in range(7, -1, -1):
                d = rows_of(dtm, 0, r0 + t, width)
                x = rows_of(dtu, 0, r0 + t, width)
                v = rows_of(dyb, 0, r0 + t, width)
                bt = [wide_b[pl.ds((r0 + t) * 16 + 8 * s, 8), :] for s in range(2)]
                ct = [wide_c[pl.ds((r0 + t) * 16 + 8 * s, 8), :] for s in range(2)]
                db = [None, None]
                dc = [None, None]
                for j in range(width):
                    qs, ss = None, None
                    for s in range(2):
                        later = newer[j][s]
                        prior = hbuf[pl.ds((r0 + t) * 16 + 8 * s, 8), pl.ds(128 * j, 128)]
                        newer[j][s] = prior
                        g = ct[s] * v[j] + w[j][s]
                        w[j][s] = jnp.exp2(d[j] * rate[j][s]) * g
                        q = w[j][s] * prior
                        ga[j][s] = ga[j][s] + q * d[j]
                        qa = q * rate[j][s]
                        sb = g * bt[s]
                        qs = qa if qs is None else qs + qa
                        ss = sb if ss is None else ss + sb
                        gx = g * x[j]
                        vh = v[j] * later
                        db[s] = gx if db[s] is None else db[s] + gx
                        dc[s] = vh if dc[s] is None else dc[s] + vh
                    qbuf[j, pl.ds(t * 8, 8), :] = qs
                    sbuf[j, pl.ds(t * 8, 8), :] = ss
                for s in range(2):
                    here = pl.ds((r0 + t) * 16 + 8 * s, 8)
                    wide_db[here, :] = wide_db[here, :] + db[s]
                    wide_dc[here, :] = wide_dc[here, :] + dc[s]
            for j in range(width):
                lanes = pl.ds(base + 128 * j, 128)
                here = pl.ds(r0, 8)
                s8 = by_eights(sbuf, j)
                dd[here, lanes] = LN2 * by_eights(qbuf, j) + u_ref[here, lanes] * s8
                di[here, lanes] = dt_ref[here, lanes] * s8
            return tuple(w[j][s] for s in range(2) for j in range(width)) + tuple(
                ga[j][s] for s in range(2) for j in range(width)
            )

        held = [(r, pl.ds(8 * s, 8), pl.ds(base + 128 * j, 128)) for r in (ws, ga_ref) for s in range(2) for j in range(width)]
        end = lax.fori_loop(0, rows // 8, body, tuple(r[a, b] for r, a, b in held))
        for (r, a, b), value in zip(held, end):
            r[a, b] = value

    for i, ref in enumerate((wide_db, wide_dc)):
        for k in range(states):
            cols_ref[pl.ds(i * rows, rows), pl.ds(128 * k, 128)] = ref[pl.ds(k, rows, stride=states), :].astype(bf16)
    owner = lax.broadcasted_iota(jnp.int32, (states, states * 128), 1) // 128
    picks = jnp.where(owner == lax.broadcasted_iota(jnp.int32, (states, states * 128), 0), 1.0, 0.0).astype(bf16)
    d_bc = lax.dot_general(picks, cols_ref[...], (((1,), (1,)), ((), ())), preferred_element_type=f32)

    @pl.loop(0, tiles, unroll=True)
    def _(k):
        lanes = pl.ds(pl.multiple_of(k * 128, 128), 128)
        low = (dd[:, lanes] * sg_ref[:, lanes]).astype(bf16)
        dt16[:, lanes] = low
        sum_ref[pl.ds(40, 8), lanes] = sum_ref[pl.ds(40, 8), lanes] + folded(low.astype(f32))

    rank16 = proj[:rank].astype(bf16)
    d_rank = lax.dot_general(dtw_ref[...], dt16[...], (((1,), (1,)), ((), ())), preferred_element_type=f32)
    proj16 = jnp.concatenate([d_rank, d_bc[:, :rows], d_bc[:, rows:]], axis=0).astype(bf16)
    off_ext[pl.ds(0, rows), :] = off_ref[...]

    @pl.loop(0, tiles // 2, unroll=True)
    def _(k):
        pair = pl.ds(pl.multiple_of(k * 256, 256), 256)
        dot = lambda a, b, c: lax.dot_general(a, b, ((c, (0,)), ((), ())), preferred_element_type=f32)
        gdt_ref[:, pair] = gdt_ref[:, pair] + dot(rank16, dt16[:, pair], (1,))
        gx_ref[:, pair] = gx_ref[:, pair] + dot(proj16, u16[:, pair], (1,))
        inner_grad = dot(proj16, xp_ref[:, pair], (0,)) + di[:, pair] + dy_ref[:, pair] * par_ref[SKIP : SKIP + 1, pair]
        ext[pl.ds(0, rows), pair] = inner_grad * ds_ref[:, pair]
        for j in range(2):
            lanes = pl.ds(pl.multiple_of(k * 256 + 128 * j, 128), 128)
            now, above = ext[pl.ds(0, rows), lanes], upper_ref[:, lanes]
            grad = par_ref[TAPS + 3 : TAPS + 4, lanes] * now
            sums = [now, now * above]
            for lag in range(1, 4):
                after = jnp.where(off_ext[pl.ds(lag, rows), :] >= lag, ext[pl.ds(lag, rows), lanes], 0.0)
                grad = grad + par_ref[TAPS + 3 - lag : TAPS + 4 - lag, lanes] * after
                sums.append(after * above)
            du_ref[:, lanes] = grad.astype(bf16)
            for at, value in zip((32, 24, 16, 8, 0), sums):
                sum_ref[pl.ds(at, 8), lanes] = sum_ref[pl.ds(at, 8), lanes] + folded(value)
            ext[pl.ds(rows, 8), lanes] = now[:8]

    off_ext[pl.ds(rows, 8), :] = off_ref[pl.ds(0, 8), :]

    @pl.when(pl.program_id(0) == pl.num_programs(0) - 1)
    def _():
        plan.finish(plan.steps - 1)


def scan_backward(saved, both, offset, proj, wide_b, wide_c, bound, params, xp, dtw, rate, chunk, width, grads, parts):
    T, DI = saved[0].shape
    n, states, cols, rank = T // chunk, rate.shape[0], xp.shape[0], dtw.shape[0]
    f32, bf16 = jnp.float32, jnp.bfloat16
    row = pl.BlockSpec((chunk, DI), lambda i: (n - 1 - i, 0))
    whole = lambda a: pl.BlockSpec(a.shape, lambda i: (0, 0))
    anywhere = pl.BlockSpec(memory_space=pl.ANY)
    plan, shaped, summed = reduction_of(grads, parts)
    sums = [jax.ShapeDtypeStruct((r, DI), f32) for r in (states, rank, cols, 48)]
    pieces = pltpu.VMEM((width, chunk, 128), f32)
    eights = pltpu.VMEM((width, 64, 128), f32)
    tall = pltpu.VMEM((chunk * states, 128), f32)
    out = pl.pallas_call(
        functools.partial(backward_kernel, width=width, plan=plan, total=T),
        grid=(n,),
        in_specs=[row] * 6
        + [
            pl.BlockSpec((chunk, 128), lambda i: (n - 1 - i, 0)),
            pl.BlockSpec((1, cols, chunk), lambda i: (n - 1 - i, 0, 0)),
            pl.BlockSpec((chunk * states, 128), lambda i: (n - 1 - i, 0)),
            pl.BlockSpec((chunk * states, 128), lambda i: (n - 1 - i, 0)),
            pl.BlockSpec((1, states, DI), lambda i: (n - 1 - i, 0, 0)),
        ]
        + [whole(a) for a in (params, xp, dtw, rate)]
        + [anywhere] * len(grads),
        out_specs=[row] + [whole(a) for a in sums] + [anywhere] * len(grads),
        out_shape=[jax.ShapeDtypeStruct((T, DI), bf16)] + sums + summed,
        scratch_shapes=[
            pltpu.VMEM((states, DI), f32),
            pieces,
            pieces,
            pieces,
            pltpu.VMEM((chunk * states + states, 128 * width), f32),
            eights,
            eights,
            pltpu.VMEM((chunk, DI), f32),
            pltpu.VMEM((chunk, DI), f32),
            pltpu.VMEM((chunk, DI), bf16),
            pltpu.VMEM((chunk, DI), bf16),
            pltpu.VMEM((chunk + 8, DI), f32),
            pltpu.VMEM((chunk + 8, 128), jnp.int32),
            tall,
            tall,
            pltpu.VMEM((2 * chunk, states * 128), bf16),
        ]
        + plan.scratch(),
        compiler_params=pltpu.CompilerParams(
            dimension_semantics=("arbitrary",), collective_id=0, has_side_effects=True, vmem_limit_bytes=56 << 20
        ),
        name="scan_backward",
    )(*saved, both, offset, proj, wide_b, wide_c, bound, params, xp, dtw, rate, *shaped)
    return out[:5], [o.reshape(-1, o.shape[-1]) for o in out[5:]]


def cluster_offsets(lengths, total_len):
    count = lengths.shape[1]
    ahead = jnp.arange(count)[:, None] < jnp.arange(count)[None, :]
    start_points = jnp.sum(jnp.where(ahead[None], lengths[:, :, None], 0), axis=1, dtype=jnp.int32)
    end_points = start_points + lengths
    where_at = jnp.arange(total_len, dtype=jnp.int32)
    inside = (where_at[None, None, :] >= start_points[:, :, None]) & (
        where_at[None, None, :] < end_points[:, :, None]
    )
    first_spot = jnp.sum(jnp.where(inside, start_points[:, :, None], 0), axis=1, dtype=jnp.int32)
    return where_at[None, :] - first_spot


def rms_piece(inputs, gain_vec):
    mean_sq = jnp.mean(inputs * inputs, axis=-1, keepdims=True)
    return inputs * lax.rsqrt(mean_sq + norm_eps) * gain_vec


def dot32(left, right, contract):
    return lax.dot_general(left, right, (contract, ((), ())), preferred_element_type=jnp.float32)


def thirds(columns, times=1):
    wide = columns // times // 1024 * 384
    return list(zip((wide, wide, columns // times - 2 * wide) * times, ORDERS * times))


def shards(
    hidden_in,
    cluster_lengths,
    norm_gain,
    in_proj,
    conv_weight,
    conv_bias,
    x_proj,
    dt_proj,
    dt_bias,
    a_log,
    skip_gain,
    out_proj,
    out_grad,
):
    f32, bf16 = jnp.float32, jnp.bfloat16
    w_in = lax.all_gather(in_proj, "fsdp", axis=0, tiled=True)
    w_out = lax.all_gather(out_proj, "fsdp", axis=0, tiled=True)
    w_x = lax.all_gather(x_proj, "fsdp", axis=0, tiled=True)
    w_gain = lax.all_gather(norm_gain, "fsdp", axis=0, tiled=True)
    taps = conv_weight.shape[0]
    rank_dim = dt_proj.shape[0]
    state_dim = a_log.shape[0]
    packed = jnp.concatenate(
        [dt_proj, a_log, conv_weight, conv_bias[None], dt_bias[None], skip_gain[None]], axis=0
    )
    packed = lax.all_gather(packed, "fsdp", axis=1, tiled=True)
    w_dt = packed[:rank_dim]
    w_alog = packed[rank_dim : rank_dim + state_dim].astype(f32)
    rest = packed[rank_dim + state_dim :].astype(f32)

    contexts_here, total_len, model_dim = hidden_in.shape
    inner_dim = packed.shape[1]
    rows = contexts_here * total_len
    offsets = cluster_offsets(cluster_lengths, total_len).reshape(rows)
    offset = jnp.broadcast_to(offsets[:, None], (rows, 128))
    inputs = hidden_in.reshape(rows, model_dim).astype(f32)
    grad_rows = out_grad.reshape(rows, model_dim)
    gain_full = w_gain.astype(f32)
    normed16 = rms_piece(inputs, gain_full).astype(bf16)
    both = dot32(normed16, w_in, ((1,), (0,)))
    decay_rate = -jnp.exp(w_alog)
    rate2 = decay_rate * LOG2E
    params = jnp.pad(rest, ((0, 8 - rest.shape[0]), (0, 0)))
    xp = w_x.T
    d_gated = dot32(grad_rows, w_out, ((1,), (1,)))
    *saved, gated16, gate16, proj, b_wide, c_wide, boundary, skip_sums = scan_forward(
        both, d_gated, offset, params, xp, w_dt, rate2, CHUNK, WIDTH
    )
    g_w_out = dot32(gated16, grad_rows, ((0,), (0,))).astype(bf16)
    g_w_gate = dot32(normed16, gate16, ((0,), (0,))).astype(bf16)
    (upper16, rate_sum, g_w_dt, g_w_x, sums), (t_out, t_gate) = scan_backward(
        saved, both, offset, proj, b_wide, c_wide, boundary, params, xp, w_dt, rate2, CHUNK, WIDTH,
        [g_w_out, g_w_gate], [thirds(model_dim), thirds(inner_dim)],
    )
    layer_out = (inputs + dot32(gated16, w_out, ((1,), (0,)))).astype(bf16)
    g_w_upper = dot32(normed16, upper16, ((0,), (0,))).astype(bf16)
    d_normed = dot32(upper16, w_in[:, :inner_dim], ((1,), (1,))) + dot32(
        gate16, w_in[:, inner_dim:], ((1,), (1,))
    )
    _, norm_pull = jax.vjp(rms_piece, inputs, gain_full)
    d_inputs, g_gain = norm_pull(d_normed)
    input_grad = grad_rows.astype(f32) + d_inputs

    parts = lax.axis_size("fsdp")
    gain_row = jnp.pad(
        g_gain.reshape(parts, model_dim // parts), ((0, 0), (0, (inner_dim - model_dim) // parts))
    ).reshape(1, inner_dim)
    row_sums = jnp.concatenate([sums, skip_sums]).reshape(7, 8, inner_dim).sum(axis=1)
    small = jnp.concatenate([g_w_x, g_w_dt, rate_sum * decay_rate, row_sums, gain_row], axis=0)
    spare = -small.shape[0] % (16 * lax.axis_size("dp"))
    small = jnp.pad(small, ((0, spare), (0, 0))).astype(bf16)
    small = small.reshape(-1, parts, inner_dim // parts).transpose(1, 0, 2).reshape(-1, inner_dim // parts)
    t_upper, t_small = reduce_all(
        [g_w_upper, small], [thirds(inner_dim, 2), [(inner_dim // parts, ORDERS[2])]], 1
    )
    t_small = t_small.astype(f32)
    t_in = jnp.concatenate([t_upper, t_gate], axis=1).astype(f32)
    t_out = t_out.astype(f32)
    columns = rank_dim + 2 * state_dim
    at = 0
    picked = []
    for size in (columns, rank_dim, state_dim, taps, 1, 1, 1, 1):
        picked.append(t_small[at : at + size])
        at += size
    t_x, t_dt, t_alog, t_conv, t_b_conv, t_b_dt, t_skip, t_gain = picked
    return (
        layer_out.reshape(hidden_in.shape),
        input_grad.reshape(hidden_in.shape),
        t_gain[0, : model_dim // parts],
        t_in,
        t_conv,
        t_b_conv[0],
        t_x.T,
        t_dt,
        t_b_dt[0],
        t_alog,
        t_skip[0],
        t_out,
    )


def solution(mesh):
    placed = (
        P(("dp", "fsdp"), None, None),
        P(("dp", "fsdp"), None),
        P("fsdp"),
        P("fsdp", None),
        P(None, "fsdp"),
        P("fsdp"),
        P("fsdp", None),
        P(None, "fsdp"),
        P("fsdp"),
        P(None, "fsdp"),
        P("fsdp"),
        P("fsdp", None),
        P(("dp", "fsdp"), None, None),
    )
    return jax.shard_map(
        shards,
        mesh=mesh,
        in_specs=placed,
        out_specs=(
            P(("dp", "fsdp"), None, None),
            P(("dp", "fsdp"), None, None),
            P("fsdp"),
            P("fsdp", None),
            P(None, "fsdp"),
            P("fsdp"),
            P("fsdp", None),
            P(None, "fsdp"),
            P("fsdp"),
            P(None, "fsdp"),
            P("fsdp"),
            P("fsdp", None),
        ),
        check_vma=False,
    )
```

profile of v0, /device:TPU:0, one launch (start us, length us, event | category | flops | bytes accessed | tf_op | source)
XLA Modules:
  0.0 367.1 jit_solution(14978692601416647456)
XLA Ops:
  8.9 2.1 all_gather.18
  11.1 1.8 all-gather
  13.0 2.1 all_gather.19
  15.7 10.3 %all-gather.6.cloned.1.call-done = bf16[2048,1024]{1,0:T(8,128)(2,1)} async-done(((bf16[1024,1024]{1,0:T(8,128)(2,1)}), bf16[2048,1024]{1,0:T(8,128)(2,1)}) %all-gather.6.cloned.1.call-update) | async-done | bytes 4194320 | tf_op jit(solution)/shard_map/all_gather | solution.py:632
  26.0 8.3 %fusion.18.dg_ref = f32[704,2048]{1,0:T(8,128)} fusion(bf16[2048,1024]{1,0:T(8,128)(2,1)} %all-gather.6.cloned.1.call-done, bf16[1,704,1024]{2,1,0:T(8,128)(2,1)} %param.25), kind=kOutput, calls=%fused_computation.27 | convolution fusion | flops 2952790016 | bytes 11403264 | tf_op jit(solution)/shard_map/dot_general | solution.py:607
  34.4 14.3 %all-gather.4.cloned.1.call-done = bf16[1024,4096]{1,0:T(8,128)(2,1)} async-done(((bf16[512,4096]{1,0:T(8,128)(2,1)}), bf16[1024,4096]{1,0:T(8,128)(2,1)}) %all-gather.4.cloned.1.call-update) | async-done | bytes 8388624 | tf_op jit(solution)/shard_map/all_gather | solution.py:631
  48.6 12.4 %fusion.27.upper_ref.z_ref = f32[704,4096]{1,0:T(8,128)} fusion(bf16[1024,4096]{1,0:T(8,128)(2,1)} %all-gather.4.cloned.1.call-done, bf16[1,704,1024]{2,1,0:T(8,128)(2,1)S(1)} %copy-done.9, f32[1024]{0:T(1024)S(1)} %bitcast.88, f32[704]{0:T(1024)S(1)} %fusion.23), kind=kOutput, calls=%fused_computation.50 | convolution fusion | flops 5908463616 | bytes 21371648 | tf_op jit(solution)/shard_map/dot_general | solution.py:607
  61.2 49.5 %scan_forward.1 = (f32[704,2048]{1,0:T(8,128)}, f32[704,2048]{1,0:T(8,128)}, f32[704,2048]{1,0:T(8,128)}, f32[704,2048]{1,0:T(8,128)}, f32[704,2048]{1,0:T(8,128...) custom-call(f32[704,4096]{1,0:T(8,128)} %fusion.27.upper_ref.z_ref, ...), custom_call_target="tpu_custom_call" | custom-call | tf_op jit(solution)/shard_map/scan_forward/pallas_call | solution.py:332
  110.8 8.9 %convolution_convert_fusion.1 = bf16[1024,2048]{1,0:T(8,128)(2,1)} fusion(bf16[704,2048]{1,0:T(8,128)(2,1)} %get-tuple-element.43, bf16[1,704,1024]{2,1,0:T(8,128)(2,1)S(1)} %copy-done.9, f32[1024]{0:T(1024)S(1)} %bitcast.89, f32[704]{0:T(1024)S(1)} %fusion.23), kind=kOutput, calls=%fused_computation.12 | convolution fusion | flops 2957770752 | bytes 8526592 | tf_op jit(solution)/shard_map/dot_general | solution.py:607
  119.7 5.0 %convolution_convert_fusion.2 = bf16[2048,1024]{1,0:T(8,128)(2,1)} fusion(bf16[704,2048]{1,0:T(8,128)(2,1)S(1)} %get-tuple-element.33, bf16[1,704,1024]{2,1,0:T(8,128)(2,1)S(1)} %copy-done.14), kind=kOutput, calls=%fused_computation.13 | convolution fusion | flops 2954887168 | bytes 8519680 | tf_op jit(solution)/shard_map/dot_general | solution.py:607
  124.7 132.1 %scan_backward.1 = (bf16[704,2048]{1,0:T(8,128)(2,1)}, f32[16,2048]{1,0:T(8,128)}, f32[64,2048]{1,0:T(8,128)}, f32[96,2048]{1,0:T(8,128)}, f32[48,2048]{1,0:T(8,...) custom-call(f32[704,2048]{1,0:T(8,128)} %get-tuple-element.34.u_ref, ...), custom_call_target="tpu_custom_call" | custom-call | tf_op jit(solution)/shard_map/scan_backward/pallas_call | solution.py:546
  256.9 7.5 %convolution_convert_fusion = bf16[1024,2048]{1,0:T(8,128)(2,1)} fusion(bf16[704,2048]{1,0:T(8,128)(2,1)} %get-tuple-element.44, bf16[1,704,1024]{2,1,0:T(8,128)(2,1)S(1)} %copy-done.9, f32[1024]{0:T(1024)S(1)} %bitcast.90, f32[704]{0:T(1024)S(1)} %fusion.23), kind=kOutput, calls=%fused_computation.11 | convolution fusion | flops 2957770752 | bytes 8526592 | tf_op jit(solution)/shard_map/dot_general | solution.py:607
  264.4 5.2 %fusion = f32[704,1024]{1,0:T(8,128)S(1)} fusion(bf16[704,2048]{1,0:T(8,128)(2,1)S(1)} %copy-done.28, bf16[1024,4096]{1,0:T(8,128)(2,1)} %all-gather.4.cloned.1.call-done), kind=kOutput, calls=%fused_computation.6 | convolution fusion | flops 2952790016 | bytes 9961472 | tf_op jit(solution)/shard_map/dot_general | solution.py:607
  269.6 5.2 %fusion.7 = (bf16[1024]{0:T(1024)(128)(2,1)S(1)}, f32[704]{0:T(1024)S(1)}, f32[704,1024]{1,0:T(8,128)}) fusion(bf16[1,704,1024]{2,1,0:T(8,128)(2,1)S(1)} %copy-done.9, f32[704]{0:T(1024)S(1)} %fusion.23, f32[1024]{0:T(1024)S(1)} %bitcast.91, f32[704,1024]{1,0:T(8,128)S(1)} %fusion, bf16[704,2048]{1,0:T(8,128)(2,1)S(1)} %copy-done.29, ...), kind=kOutput, calls=%fused_computation.17 | convolution fusion | flops 2958555392 | bytes 14299904 | tf_op jit(solution)/shard_map/dot_general | solution.py:607
  274.9 1.1 convert.26
  276.5 1.1 copy.31
  277.5 59.1 %reduce_all.1 = (bf16[16,32,2048]{2,1,0:T(8,128)(2,1)}, bf16[16,16,1024]{2,1,0:T(8,128)(2,1)}) custom-call(bf16[32,32,2048]{2,1,0:T(8,128)(2,1)} %bitcast.77, bf16[32,16,1024]{2,1,0:T(8,128)(2,1)} %bitcast.78), custom_call_target="tpu_custom_call" | custom-call | tf_op jit(solution)/shard_map/reduce_all/pallas_call | solution.py:186
  336.7 1.6 slice.75
  338.3 1.7 slice.74
  340.0 1.2 convert_element_type.63
  343.6 2.7 bitcast_convert_fusion
  347.3 2.4 fusion.9
  350.6 5.0 %maximum_convert_fusion = f32[512,4096]{1,0:T(8,128)} fusion(bf16[512,2048]{1,0:T(8,128)(2,1)S(1)} %bitcast.80, bf16[512,2048]{1,0:T(8,128)(2,1)S(1)} %bitcast.81), kind=kLoop, calls=%fused_computation.10 | loop fusion | flops 8388608 | bytes 12582912 | tf_op jit(solution)/shard_map/convert_element_type | solution.py:692
  356.1 4.2 %fusion.16 = bf16[1,704,1024]{2,1,0:T(8,128)(2,1)} fusion(bf16[704,2048]{1,0:T(8,128)(2,1)S(1)} %copy-done.8, bf16[2048,1024]{1,0:T(8,128)(2,1)S(1)} %copy-done.27, bf16[1,704,1024]{2,1,0:T(8,128)(2,1)S(1)} %copy-done.9), kind=kOutput, calls=%fused_computation.25 | convolution fusion | flops 2954952704 | bytes 9961472 | tf_op jit(solution)/shard_map/dot_general | solution.py:607
  (101 shorter events, 7.7 us)
Async XLA Ops:
  7.2 18.8 %all-gather.6.cloned.1.call-start = ((), (), s32[]{:S(2)}) async-start(), calls=%async_computation.1 | async-start | bytes 6291456 | tf_op jit(solution)/shard_map/all_gather | solution.py:632
  8.0 5.0 %copy-start.18 = (bf16[1024,96]{0,1:T(8,128)(2,1)S(1)}, bf16[1024,96]{0,1:T(8,128)(2,1)}, u32[]{:S(2)}) copy-start(bf16[1024,96]{0,1:T(8,128)(2,1)} %param.19) | copy-start | bytes 589828
  8.0 7.1 %copy-start.30 = (s32[1,8]{1,0:T(1,128)S(1)}, s32[1,8]{1,0:T(1,128)}, u32[]{:S(2)}) copy-start(s32[1,8]{1,0:T(1,128)} %param.14) | copy-start | bytes 100
  8.0 7.2 %copy-start.9 = (bf16[1,704,1024]{2,1,0:T(8,128)(2,1)S(1)}, bf16[1,704,1024]{2,1,0:T(8,128)(2,1)}, u32[]{:S(2)}) copy-start(bf16[1,704,1024]{2,1,0:T(8,128)(2,1)} %param.13) | copy-start | bytes 4325380
  8.0 40.6 %all-gather.4.cloned.1.call-start = ((), (), s32[]{:S(2)}) async-start(), calls=%async_computation | async-start | bytes 12582912 | tf_op jit(solution)/shard_map/all_gather | solution.py:631
  11.1 50.1 %copy-start.2 = (bf16[64,2048]{1,0:T(8,128)(2,1)}, bf16[64,2048]{1,0:T(8,128)(2,1)S(1)}, u32[]{:S(2)}) copy-start(bf16[64,2048]{1,0:T(8,128)(2,1)S(1)} %slice.67.dtw_ref) | copy-start | bytes 786436
  15.1 46.1 %copy-start = (bf16[2048,96]{0,1:T(8,128)(2,1)}, bf16[2048,96]{0,1:T(8,128)(2,1)S(1)}, u32[]{:S(2)}) copy-start(bf16[2048,96]{0,1:T(8,128)(2,1)S(1)} %all_gather.19) | copy-start | bytes 1179652
  15.6 45.6 %copy-start.5 = (f32[8,2048]{1,0:T(8,128)}, f32[8,2048]{1,0:T(8,128)S(1)}, u32[]{:S(2)}) copy-start(f32[8,2048]{1,0:T(8,128)S(1)} %pad_convert_fusion.par_ref) | copy-start | bytes 196612
  15.7 45.5 %copy-start.4 = (f32[16,2048]{1,0:T(8,128)}, f32[16,2048]{1,0:T(8,128)S(1)}, u32[]{:S(2)}) copy-start(f32[16,2048]{1,0:T(8,128)S(1)} %fusion.21.a_ref) | copy-start | bytes 393220
  61.2 49.6 %copy-start.1 = (s32[704,128]{1,0:T(8,128)}, s32[704,128]{1,0:T(8,128)S(1)}, u32[]{:S(2)}) copy-start(s32[704,128]{1,0:T(8,128)S(1)} %broadcast_in_dim.35.off_ref) | copy-start | bytes 1081348
  110.7 8.9 %copy-start.3 = (f32[11,16,2048]{2,1,0:T(8,128)}, f32[11,16,2048]{2,1,0:T(8,128)S(1)}, u32[]{:S(2)}) copy-start(f32[11,16,2048]{2,1,0:T(8,128)S(1)} %get-tuple-element.42.bound_ref) | copy-start | bytes 4325380
  110.8 8.9 %copy-start.6 = (f32[11,96,64]{2,1,0:T(8,128)}, f32[11,96,64]{2,1,0:T(8,128)S(1)}, u32[]{:S(2)}) copy-start(f32[11,96,64]{2,1,0:T(8,128)S(1)} %get-tuple-element.39.proj_ref) | copy-start | bytes 811012
  110.8 8.9 %copy-start.7 = (bf16[704,2048]{1,0:T(8,128)(2,1)}, bf16[704,2048]{1,0:T(8,128)(2,1)S(1)}, u32[]{:S(2)}) copy-start(bf16[704,2048]{1,0:T(8,128)(2,1)S(1)} %get-tuple-element.33) | copy-start | bytes 8650756
  110.8 8.9 %copy-start.14 = (bf16[1,704,1024]{2,1,0:T(8,128)(2,1)S(1)}, bf16[1,704,1024]{2,1,0:T(8,128)(2,1)}, u32[]{:S(2)}) copy-start(bf16[1,704,1024]{2,1,0:T(8,128)(2,1)} %param.25) | copy-start | bytes 4325380
  256.9 7.5 %copy-start.28 = (bf16[704,2048]{1,0:T(8,128)(2,1)S(1)}, bf16[704,2048]{1,0:T(8,128)(2,1)}, u32[]{:S(2)}) copy-start(bf16[704,2048]{1,0:T(8,128)(2,1)} %get-tuple-element.43) | copy-start | bytes 8650756
  256.9 12.7 %slice-start = ((s8[8388608]{0:T(1024)(128)(4,1)}), s8[4194304]{0:T(1024)(128)(4,1)S(1)}, s32[]{:S(2)}) async-start(s8[8388608]{0:T(1024)(128)(4,1)} %bitcast.97), calls=%async_computation.2 | async-start | bytes 8388608
  264.4 5.2 %slice-start.1 = ((s8[8388608]{0:T(1024)(128)(4,1)}), s8[4194304]{0:T(1024)(128)(4,1)S(1)}, s32[]{:S(2)}) async-start(s8[8388608]{0:T(1024)(128)(4,1)} %bitcast.97), calls=%async_computation.3 | async-start | bytes 8388608
  264.4 5.2 %copy-start.29 = (bf16[704,2048]{1,0:T(8,128)(2,1)S(1)}, bf16[704,2048]{1,0:T(8,128)(2,1)}, u32[]{:S(2)}) copy-start(bf16[704,2048]{1,0:T(8,128)(2,1)} %get-tuple-element.44) | copy-start | bytes 8650756
  269.6 5.2 %copy-start.19 = (f32[16,2048]{1,0:T(8,128)S(1)}, f32[16,2048]{1,0:T(8,128)}, u32[]{:S(2)}) copy-start(f32[16,2048]{1,0:T(8,128)} %get-tuple-element.47) | copy-start | bytes 393220
  269.6 5.3 %copy-start.16 = (f32[96,2048]{1,0:T(8,128)S(1)}, f32[96,2048]{1,0:T(8,128)}, u32[]{:S(2)}) copy-start(f32[96,2048]{1,0:T(8,128)} %get-tuple-element.45) | copy-start | bytes 2359300
  269.6 6.4 %copy-start.17 = (f32[48,2048]{1,0:T(8,128)S(1)}, f32[48,2048]{1,0:T(8,128)}, u32[]{:S(2)}) copy-start(f32[48,2048]{1,0:T(8,128)} %get-tuple-element.48) | copy-start | bytes 1179652
  277.5 66.1 %copy-start.11 = (bf16[16,64,1024]{2,1,0:T(8,128)(2,1)S(1)}, bf16[16,64,1024]{2,1,0:T(8,128)(2,1)}, u32[]{:S(2)}) copy-start(bf16[16,64,1024]{2,1,0:T(8,128)(2,1)} %get-tuple-element.53) | copy-start | bytes 6291460
  350.6 5.0 %copy-start.8 = (bf16[704,2048]{1,0:T(8,128)(2,1)S(1)}, bf16[704,2048]{1,0:T(8,128)(2,1)}, u32[]{:S(2)}) copy-start(bf16[704,2048]{1,0:T(8,128)(2,1)} %copy-done.7) | copy-start | bytes 8650756
  350.6 5.5 %copy-start.27 = (bf16[2048,1024]{1,0:T(8,128)(2,1)S(1)}, bf16[2048,1024]{1,0:T(8,128)(2,1)}, u32[]{:S(2)}) copy-start(bf16[2048,1024]{1,0:T(8,128)(2,1)} %all-gather.6.cloned.1.call-done) | copy-start | bytes 12582916
  (11 other events, 24.9 us)
Sparse Core Ops, SparseCore 0:
  9.6 16.3 all-gather.5
  27.6 21.0 all-gather.3
where the time goes:
time: 368 us; the launch traced here: 367 us
  Pallas kernels  241 us (65%)
  matrix products  56.7 us (15%)
  waiting for transfers between devices  26 us (7%)
  between operations  14.6 us (4%)
  other arithmetic  13.1 us (4%)
  local copies, waits for them, and re-layouts  9.86 us (3%)
  blocking collectives  6.07 us (2%)
    pallas_call x1, Pallas kernels, scan_backward(): pl.pallas_call(functools.partial(backward_kernel, width=width, plan=plan,...  132 us
    pallas_call x1, Pallas kernels, reduce_all(): pl.pallas_call(functools.partial(reduce_kernel, plan=plan), out_shape=out...  59.1 us
    dot_general x8, matrix products, dot32(): lax.dot_general(left, right, (contract, ((), ())), preferred_element_type...  56.7 us
    pallas_call x1, Pallas kernels, scan_forward(): pl.pallas_call(functools.partial(forward_kernel, width=width), grid=(n,),...  49.5 us
    all_gather x1, waiting for transfers between devices, shards(): w_in = lax.all_gather(in_proj, 'fsdp', axis=0, tiled=True)  14.3 us
    all_gather x1, waiting for transfers between devices, shards(): w_out = lax.all_gather(out_proj, 'fsdp', axis=0, tiled=True)  10.3 us
  transfers between devices with their start and end apart: 2, of which 2 were waited for; matrix products, arithmetic and copies ran while one was open for 2% of the time, Pallas kernels for 0%

commit v1 on v0

--- a/solution.py
+++ b/solution.py
@@ -155,9 +155,9 @@
                 self.leave(p).wait()
 
     def times(self, count):
-        heavy = (2.0, 1.3)
-        there = [heavy[j] if j < len(heavy) else 1.0 for j in range(self.inner_bits)]
-        loads = [1.2] * self.outer_bits + there + there[::-1]
+        heavy = (18.0, 10.0, 6.5, 14.0)
+        there = [heavy[min(j, 3)] for j in range(self.inner_bits)]
+        loads = [11.0] * self.outer_bits + there + there[::-1]
         total, at, out = sum(loads), 0.0, []
         for load in loads[:-1]:
             at += load
@@ -193,6 +193,165 @@
         name="reduce_all",
     )(*shaped)
     return [o.reshape(-1, o.shape[-1]) for o in out]
+
+
+class Exchange:
+    def __init__(self, size):
+        self.size = size
+
+    def owner(self, turn):
+        return (lax.axis_index("fsdp") + self.size - turn) % self.size
+
+    def peer(self, turn):
+        return {"fsdp": (lax.axis_index("fsdp") + turn) % self.size}
+
+    def barrier(self):
+        sem = pltpu.get_barrier_semaphore()
+        for turn in range(1, self.size):
+            pl.semaphore_signal(sem, inc=1, device_id=self.peer(turn), device_id_type=pl.DeviceIdType.MESH)
+        pl.semaphore_wait(sem, self.size - 1)
+
+    def copy(self, source, target, sems, which, turn):
+        if turn == 0:
+            return pltpu.make_async_copy(source, target, sems[1].at[which, 0])
+        return pltpu.make_async_remote_copy(
+            src_ref=source,
+            dst_ref=target,
+            send_sem=sems[0].at[which, turn],
+            recv_sem=sems[1].at[which, turn],
+            device_id=self.peer(turn),
+            device_id_type=pl.DeviceIdType.MESH,
+        )
+
+
+GAIN_ROW = 80
+
+
+def gather_kernel(
+    x_ref, go_ref, dt_ref, rate_ref, vec_ref, xp_ref, wout_ref, win_ref,
+    normed_ref, pack_out, wout_out, win_out, dg_out, both_out,
+    pack, wout, win, dg, both, packed, send, recv, leave, tiles, *, plan
+):
+    f32, bf16 = jnp.float32, jnp.bfloat16
+    rows, model = x_ref.shape
+    deep, wide, share = model // plan.size, both.shape[1], packed.shape[1]
+    me = lax.axis_index("fsdp")
+    sems = (send, recv)
+
+    def copies(which, turn):
+        source = (packed, wout_ref, win_ref)[which]
+        if which == 0:
+            target = pack.at[:, pl.ds(pl.multiple_of(me * share, 128), share)]
+        else:
+            target = (wout, win)[which - 1].at[me]
+        return plan.copy(source, target, sems, which, turn)
+
+    at = 0
+    for ref in (dt_ref, rate_ref, vec_ref):
+        packed[at : at + ref.shape[0], :] = ref[...]
+        at += ref.shape[0]
+    packed[at:, :] = xp_ref[...].astype(f32).T.astype(bf16)
+    plan.barrier()
+    for which in range(3):
+        for turn in range(1, plan.size):
+            copies(which, turn).start()
+    for which in (1, 0, 2):
+        copies(which, 0).start()
+
+    def times_out(turn):
+        at = plan.owner(turn)
+
+        @pl.loop(0, share // 256)
+        def _(k):
+            here = pl.ds(pl.multiple_of(at * share + k * 256, 128), 256)
+            dg[:, here] = lax.dot_general(
+                go_ref[...], wout[at, pl.ds(pl.multiple_of(k * 256, 256), 256), :],
+                (((1,), (1,)), ((), ())), preferred_element_type=f32,
+            )
+        pltpu.make_async_copy(wout.at[at], wout_out.at[at], leave.at[0, turn]).start()
+        part = pl.ds(pl.multiple_of(at * share, 128), share)
+        pltpu.make_async_copy(dg.at[:, part], dg_out.at[:, part], leave.at[2, turn]).start()
+
+    def times_in(turn):
+        at = plan.owner(turn)
+        left = pl.ds(pl.multiple_of(at * deep, 128), deep)
+
+        @pl.loop(0, wide // 256)
+        def _(k):
+            here = pl.ds(pl.multiple_of(k * 256, 256), 256)
+            new = jnp.dot(normed_ref[:, left], win[at, :, here], preferred_element_type=f32)
+            both[:, here] = new if turn == 0 else both[:, here] + new
+            if turn == plan.size - 1:
+                pltpu.make_async_copy(both.at[:, here], both_out.at[:, here], tiles.at[k]).start()
+        pltpu.make_async_copy(win.at[at], win_out.at[at], leave.at[1, turn]).start()
+
+    copies(1, 0).wait()
+    times_out(0)
+    for turn in range(plan.size):
+        copies(0, turn).wait()
+    whole_pack = pltpu.make_async_copy(pack, pack_out, leave.at[3, 0])
+    whole_pack.start()
+    gain = jnp.concatenate(
+        [pack[GAIN_ROW : GAIN_ROW + 16, b * share : b * share + deep] for b in range(plan.size)], axis=1
+    ).astype(f32)[:1]
+
+    @pl.loop(0, rows // 64)
+    def _(k):
+        here = pl.ds(pl.multiple_of(k * 64, 64), 64)
+        x = x_ref[here, :].astype(f32)
+        mean_sq = jnp.mean(x * x, axis=-1, keepdims=True)
+        normed_ref[here, :] = (x * lax.rsqrt(mean_sq + norm_eps) * gain).astype(bf16)
+
+    copies(2, 0).wait()
+    times_in(0)
+    for turn in range(1, plan.size):
+        copies(1, turn).wait()
+        times_out(turn)
+    for turn in range(1, plan.size):
+        copies(2, turn).wait()
+        times_in(turn)
+    whole_pack.wait()
+    for turn in range(plan.size):
+        at = plan.owner(turn)
+        part = pl.ds(pl.multiple_of(at * share, 128), share)
+        pltpu.make_async_copy(wout.at[at], wout_out.at[at], leave.at[0, turn]).wait()
+        pltpu.make_async_copy(win.at[at], win_out.at[at], leave.at[1, turn]).wait()
+        pltpu.make_async_copy(dg.at[:, part], dg_out.at[:, part], leave.at[2, turn]).wait()
+
+    @pl.loop(0, wide // 256)
+    def _(k):
+        here = pl.ds(pl.multiple_of(k * 256, 256), 256)
+        pltpu.make_async_copy(both.at[:, here], both_out.at[:, here], tiles.at[k]).wait()
+
+
+def gather_weights(x, grad_rows, small, w_out, w_in):
+    f32, bf16 = jnp.float32, jnp.bfloat16
+    plan = Exchange(lax.axis_size("fsdp"))
+    n, (rows, model), wide = plan.size, x.shape, w_in.shape[1]
+    depth, share = sum(s.shape[0] for s in small[:3]) + small[3].shape[1], small[0].shape[1]
+    inner = n * share
+    anywhere = pl.BlockSpec(memory_space=pl.ANY)
+    near = pl.BlockSpec(memory_space=pltpu.VMEM)
+    shapes = [
+        ((depth, inner), bf16), ((n,) + w_out.shape, bf16), ((n,) + w_in.shape, bf16), ((rows, inner), f32), ((rows, wide), f32),
+    ]
+    normed, packed, out_all, in_all, d_gated, both = pl.pallas_call(
+        functools.partial(gather_kernel, plan=plan),
+        out_shape=[jax.ShapeDtypeStruct(x.shape, bf16)] + [jax.ShapeDtypeStruct(*s) for s in shapes],
+        in_specs=[near] * 6 + [anywhere] * 2,
+        out_specs=[near] + [anywhere] * 5,
+        scratch_shapes=[pltpu.VMEM(*s) for s in shapes]
+        + [
+            pltpu.VMEM((depth, share), bf16),
+            pltpu.SemaphoreType.DMA((3, n)),
+            pltpu.SemaphoreType.DMA((3, n)),
+            pltpu.SemaphoreType.DMA((4, n)),
+            pltpu.SemaphoreType.DMA((wide // 256,)),
+        ],
+        compiler_params=pltpu.CompilerParams(collective_id=2, has_side_effects=True, vmem_limit_bytes=56 << 20),
+        name="gather_weights",
+    )(x, grad_rows, *small, w_out, w_in)
+    return normed, packed, out_all.reshape(-1, w_out.shape[1]), in_all.reshape(-1, wide), d_gated, both
 
 
 BIG = 1e30
@@ -378,7 +537,7 @@
     rows, inner = u_ref.shape
     states, rank = a_ref.shape[0], dtw_ref.shape[0]
     tiles = inner // 128
-    times = plan.times(total // rows)
+    times = plan.times(total // rows * (tiles // width))
 
     @pl.when(pl.program_id(0) == 0)
     def _():
@@ -388,13 +547,6 @@
         off_ext[pl.ds(rows, 8), :] = jnp.full((8, 128), -1, jnp.int32)
         plan.begin()
 
-    for at in sorted(set(times)):
-        @pl.when(pl.program_id(0) == at)
-        def _():
-            for step in range(plan.steps - 1):
-                if times[step] == at:
-                    plan.finish(step)
-
     proj = proj_ref[0]
     wide_db[...] = jnp.zeros_like(wide_db)
     wide_dc[...] = jnp.zeros_like(wide_dc)
@@ -403,6 +555,13 @@
     def _(cb):
         tile = cb * width
         base = pl.multiple_of(cb * 128 * width, 128 * width)
+        for at in sorted(set(times)):
+            @pl.when(pl.program_id(0) * (tiles // width) + cb == at)
+            def _():
+                for step in range(plan.steps - 1):
+                    if times[step] == at:
+                        plan.finish(step)
+
         for j in range(width):
             lanes = pl.ds(base + 128 * j, 128)
             d, act = dt_ref[:, lanes], u_ref[:, lanes]
@@ -628,36 +787,30 @@
     out_grad,
 ):
     f32, bf16 = jnp.float32, jnp.bfloat16
-    w_in = lax.all_gather(in_proj, "fsdp", axis=0, tiled=True)
-    w_out = lax.all_gather(out_proj, "fsdp", axis=0, tiled=True)
-    w_x = lax.all_gather(x_proj, "fsdp", axis=0, tiled=True)
-    w_gain = lax.all_gather(norm_gain, "fsdp", axis=0, tiled=True)
-    taps = conv_weight.shape[0]
+    taps, share = conv_weight.shape
     rank_dim = dt_proj.shape[0]
     state_dim = a_log.shape[0]
-    packed = jnp.concatenate(
-        [dt_proj, a_log, conv_weight, conv_bias[None], dt_bias[None], skip_gain[None]], axis=0
-    )
-    packed = lax.all_gather(packed, "fsdp", axis=1, tiled=True)
-    w_dt = packed[:rank_dim]
-    w_alog = packed[rank_dim : rank_dim + state_dim].astype(f32)
-    rest = packed[rank_dim + state_dim :].astype(f32)
-
     contexts_here, total_len, model_dim = hidden_in.shape
-    inner_dim = packed.shape[1]
     rows = contexts_here * total_len
+    columns = rank_dim + 2 * state_dim
     offsets = cluster_offsets(cluster_lengths, total_len).reshape(rows)
     offset = jnp.broadcast_to(offsets[:, None], (rows, 128))
+    grad_rows = out_grad.reshape(rows, model_dim)
+    gain_part = jnp.pad(norm_gain, (0, share - norm_gain.shape[0]))
+    vectors = [v[None] for v in (gain_part,)] + [conv_weight] + [v[None] for v in (conv_bias, dt_bias, skip_gain)]
+    spare = columns - rank_dim - state_dim - taps - 4
+    vectors = jnp.concatenate(vectors + [jnp.zeros((spare, share), bf16)], axis=0)
+    normed16, packed, w_out, w_in, d_gated, both = gather_weights(
+        hidden_in.reshape(rows, model_dim), grad_rows, (dt_proj, a_log, vectors, x_proj), out_proj, in_proj
+    )
+    inner_dim = packed.shape[1]
+    decay_rate = -jnp.exp(packed[rank_dim : rank_dim + state_dim].astype(f32))
+    rate2 = decay_rate * LOG2E
+    params = packed[GAIN_ROW + 1 : GAIN_ROW + 9].astype(f32)
+    w_dt, xp = packed[:rank_dim], packed[columns:]
+    parts = lax.axis_size("fsdp")
+    gain_full = packed[GAIN_ROW].reshape(parts, share)[:, : model_dim // parts].reshape(model_dim).astype(f32)
     inputs = hidden_in.reshape(rows, model_dim).astype(f32)
-    grad_rows = out_grad.reshape(rows, model_dim)
-    gain_full = w_gain.astype(f32)
-    normed16 = rms_piece(inputs, gain_full).astype(bf16)
-    both = dot32(normed16, w_in, ((1,), (0,)))
-    decay_rate = -jnp.exp(w_alog)
-    rate2 = decay_rate * LOG2E
-    params = jnp.pad(rest, ((0, 8 - rest.shape[0]), (0, 0)))
-    xp = w_x.T
-    d_gated = dot32(grad_rows, w_out, ((1,), (1,)))
     *saved, gated16, gate16, proj, b_wide, c_wide, boundary, skip_sums = scan_forward(
         both, d_gated, offset, params, xp, w_dt, rate2, CHUNK, WIDTH
     )
@@ -676,7 +829,6 @@
     d_inputs, g_gain = norm_pull(d_normed)
     input_grad = grad_rows.astype(f32) + d_inputs
 
-    parts = lax.axis_size("fsdp")
     gain_row = jnp.pad(
         g_gain.reshape(parts, model_dim // parts), ((0, 0), (0, (inner_dim - model_dim) // parts))
     ).reshape(1, inner_dim)
@@ -691,7 +843,6 @@
     t_small = t_small.astype(f32)
     t_in = jnp.concatenate([t_upper, t_gate], axis=1).astype(f32)
     t_out = t_out.astype(f32)
-    columns = rank_dim + 2 * state_dim
     at = 0
     picked = []
     for size in (columns, rank_dim, state_dim, taps, 1, 1, 1, 1):

time: 368 us -> 335 us (0.910)
  waiting for transfers between devices: 26 us -> 0 us
  matrix products: 56.7 us -> 34.6 us
  Pallas kernels: 241 us -> 262 us
  between operations: 14.6 us -> 1.01 us
  local copies, waits for them, and re-layouts: 9.86 us -> 18.2 us
  blocking collectives: 6.07 us -> 0 us
  other arithmetic: 13.1 us -> 18.6 us
    pallas_call x0 -> x1, Pallas kernels: none -> 25.3 us  [gather_weights(): pl.pallas_call(functools.partial(gather_kernel, plan=plan), out_shape=[ja...]
    all_gather x2 -> x0, waiting for transfers between devices: 24.6 us -> none  [the longest x1 14.3 us: shards(): w_in = lax.all_gather(in_proj, 'fsdp', axis=0, tiled=True)]
    dot_general x8 -> x6, matrix products: 56.7 us -> 34.6 us  [dot32(): lax.dot_general(left, right, (contract, ((), ())), preferred_element_type...]
    all_gather x3 -> x0, blocking collectives: 6.07 us -> none  [the longest x1 2.15 us: shards(): packed = lax.all_gather(packed, 'fsdp', axis=1, tiled=True)]
    pallas_call x1, Pallas kernels: 132 us -> 128 us  [scan_backward(): pl.pallas_call(functools.partial(backward_kernel, width=width, plan=plan,...]
  transfers between devices with their start and end apart: 2 -> 0, of which waited for: 2 -> 0; matrix products, arithmetic and copies ran while one was open for 2% -> 0% of each run, Pallas kernels for 0% -> 0%
where the time goes in v1:
time: 335 us; the launch traced here: 334 us
  Pallas kernels  262 us (78%)
  matrix products  34.6 us (10%)
  other arithmetic  18.6 us (6%)
  local copies, waits for them, and re-layouts  18.2 us (5%)
    pallas_call x1, Pallas kernels, scan_backward(): pl.pallas_call(functools.partial(backward_kernel, width=width, plan=plan,...  128 us
    pallas_call x1, Pallas kernels, reduce_all(): pl.pallas_call(functools.partial(reduce_kernel, plan=plan), out_shape=out...  59.1 us
    pallas_call x1, Pallas kernels, scan_forward(): pl.pallas_call(functools.partial(forward_kernel, width=width), grid=(n,),...  49.4 us
    dot_general x6, matrix products, dot32(): lax.dot_general(left, right, (contract, ((), ())), preferred_element_type...  34.6 us
    pallas_call x1, Pallas kernels, gather_weights(): pl.pallas_call(functools.partial(gather_kernel, plan=plan), out_shape=[ja...  25.3 us

profile of v1, /device:TPU:0, one launch (start us, length us, event | category | flops | bytes accessed | tf_op | source)
XLA Modules:
  0.0 334.2 jit_solution(3318642459286076893)
XLA Ops:
  2.8 1.7 fusion.7
  6.6 1.9 concatenate.13.vec_ref
  8.6 1.8 copy.27.xp_ref
  10.5 25.3 %gather_weights.1 = (bf16[704,1024]{1,0:T(8,128)(2,1)}, bf16[192,2048]{1,0:T(8,128)(2,1)}, bf16[2,1024,1024]{2,1,0:T(8,128)(2,1)}, bf16[2,512,4096]{2,1,0:T(8,12...) custom-call(bf16[704,1024]{1,0:T(8,128)(2,1)} %bitcast.69, bf16[704,1024]{1,0:T(8,128)(2,1)} %bitcast.70, ...), custom_call_target="tpu_custom_call" | custom-call | tf_op jit(solution)/shard_map/gather_weights/pallas_call | solution.py:338
  37.5 0.9 fusion.16.a_ref
  38.4 1.0 slice.61.dtw_ref
  39.4 1.1 slice.60.xp_ref
  40.6 49.4 %scan_forward.1 = (f32[704,2048]{1,0:T(8,128)}, f32[704,2048]{1,0:T(8,128)}, f32[704,2048]{1,0:T(8,128)}, f32[704,2048]{1,0:T(8,128)}, f32[704,2048]{1,0:T(8,128...) custom-call(f32[704,4096]{1,0:T(8,128)} %get-tuple-element.39.upper_, ...), custom_call_target="tpu_custom_call" | custom-call | tf_op jit(solution)/shard_map/scan_forward/pallas_call | solution.py:491
  90.1 4.2 %fusion.14 = bf16[1,704,1024]{2,1,0:T(8,128)(2,1)} fusion(bf16[704,2048]{1,0:T(8,128)(2,1)S(1)} %get-tuple-element.42, bf16[2048,1024]{1,0:T(8,128)(2,1)S(1)} %bitcast.92, bf16[1,704,1024]{2,1,0:T(8,128)(2,1)S(1)} %copy-done.7), kind=kOutput, calls=%fused_computation.23 | convolution fusion | flops 2954952704 | bytes 9961472 | tf_op jit(solution)/shard_map/dot_general | solution.py:766
  94.4 7.0 %fusion = f32[704,1024]{1,0:T(8,128)} fusion(bf16[704,2048]{1,0:T(8,128)(2,1)S(1)} %copy-done.18, bf16[1024,4096]{1,0:T(8,128)(2,1)} %bitcast.90), kind=kOutput, calls=%fused_computation.6 | convolution fusion | flops 2952790016 | bytes 9961472 | tf_op jit(solution)/shard_map/dot_general | solution.py:766
  101.4 5.1 %convolution_convert_fusion.1 = bf16[1024,2048]{1,0:T(8,128)(2,1)} fusion(bf16[704,1024]{1,0:T(8,128)(2,1)S(1)} %copy-done.19, bf16[704,2048]{1,0:T(8,128)(2,1)S(1)} %copy-done.18), kind=kOutput, calls=%fused_computation.12 | convolution fusion | flops 2954887168 | bytes 8519680 | tf_op jit(solution)/shard_map/dot_general | solution.py:766
  106.5 5.0 %convolution_convert_fusion.2 = bf16[2048,1024]{1,0:T(8,128)(2,1)} fusion(bf16[704,2048]{1,0:T(8,128)(2,1)S(1)} %get-tuple-element.42, bf16[1,704,1024]{2,1,0:T(8,128)(2,1)S(1)} %copy-done.8), kind=kOutput, calls=%fused_computation.13 | convolution fusion | flops 2954887168 | bytes 8519680 | tf_op jit(solution)/shard_map/dot_general | solution.py:766
  111.5 127.9 %scan_backward.1 = (bf16[704,2048]{1,0:T(8,128)(2,1)}, f32[16,2048]{1,0:T(8,128)}, f32[64,2048]{1,0:T(8,128)}, f32[96,2048]{1,0:T(8,128)}, f32[48,2048]{1,0:T(8,...) custom-call(f32[704,2048]{1,0:T(8,128)} %get-tuple-element.44.u_ref, ...), custom_call_target="tpu_custom_call" | custom-call | tf_op jit(solution)/shard_map/scan_backward/pallas_call | solution.py:705
  239.4 8.2 %fusion.10 = (bf16[1024]{0:T(1024)(128)(2,1)S(1)}, f32[704]{0:T(1024)S(1)}, f32[704,1024]{1,0:T(8,128)}) fusion(f32[704]{0:T(1024)S(1)} %fusion.18, bf16[1,704,1024]{2,1,0:T(8,128)(2,1)S(1)} %copy-done.7, f32[1024]{0:T(1024)S(1)} %bitcast.84, f32[704,1024]{1,0:T(8,128)S(1)} %copy-done.21, bf16[704,2048]{1,0:T(8,128)(2,1)} %get-tuple-element.55, ...), kind=kOutput, calls=%fused_computation.20 | convolution fusion | flops 2958555392 | bytes 14298624 | tf_op jit(solution)/shard_map/dot_general | solution.py:766
  247.7 4.3 %fusion.5 = f32[1,704,1024]{2,1,0:T(8,128)} fusion(f32[704,1024]{1,0:T(8,128)} %get-tuple-element.71, f32[704]{0:T(1024)S(1)} %multiply_multiply_fusion, f32[704]{0:T(1024)S(1)} %fusion.18, f32[1024]{0:T(1024)S(1)} %bitcast.85, bf16[1,704,1024]{2,1,0:T(8,128)(2,1)S(1)} %copy-done.8, bf16[1,704,1024]{2,1,0:T(8,128)(2,1)S(1)} %copy-done.7), kind=kLoop, calls=%fused_computation.15 | loop fusion | flops 5767168 | bytes 8660480 | tf_op jit(solution)/shard_map/reshape | solution.py:854
  253.5 1.1 copy.33
  254.6 1.3 copy-done.17
  255.8 5.0 %convolution_convert_fusion = bf16[1024,2048]{1,0:T(8,128)(2,1)} fusion(bf16[704,1024]{1,0:T(8,128)(2,1)S(1)} %copy-done.20, bf16[704,2048]{1,0:T(8,128)(2,1)S(1)} %copy-done.17), kind=kOutput, calls=%fused_computation.11 | convolution fusion | flops 2954887168 | bytes 8519680 | tf_op jit(solution)/shard_map/dot_general | solution.py:766
  260.9 59.1 %reduce_all.1 = (bf16[16,32,2048]{2,1,0:T(8,128)(2,1)}, bf16[16,16,1024]{2,1,0:T(8,128)(2,1)}) custom-call(bf16[32,32,2048]{2,1,0:T(8,128)(2,1)} %bitcast.73, bf16[32,16,1024]{2,1,0:T(8,128)(2,1)} %bitcast.74), custom_call_target="tpu_custom_call" | custom-call | tf_op jit(solution)/shard_map/reduce_all/pallas_call | solution.py:186
  320.0 1.8 slice.85
  321.8 1.7 slice.84
  323.5 1.2 convert_element_type.66
  327.1 4.5 %maximum_convert_fusion = f32[512,4096]{1,0:T(8,128)} fusion(bf16[512,2048]{1,0:T(8,128)(2,1)S(1)} %bitcast.76, bf16[512,2048]{1,0:T(8,128)(2,1)S(1)} %bitcast.77), kind=kLoop, calls=%fused_computation.10 | loop fusion | flops 8388608 | bytes 12582912 | tf_op jit(solution)/shard_map/convert_element_type | solution.py:844
  331.6 2.6 bitcast_convert_fusion
  (74 shorter events, 10.0 us)
Async XLA Ops:
  10.5 30.0 %copy-start.1 = (s32[704,128]{1,0:T(8,128)}, s32[704,128]{1,0:T(8,128)S(1)}, u32[]{:S(2)}) copy-start(s32[704,128]{1,0:T(8,128)S(1)} %broadcast_in_dim.65.off_ref) | copy-start | bytes 1081348
  37.4 52.6 %copy-start.5 = (f32[8,2048]{1,0:T(8,128)}, f32[8,2048]{1,0:T(8,128)S(1)}, u32[]{:S(2)}) copy-start(f32[8,2048]{1,0:T(8,128)S(1)} %slice_convert_fusion.par_ref) | copy-start | bytes 196612
  38.4 51.7 %copy-start.4 = (f32[16,2048]{1,0:T(8,128)}, f32[16,2048]{1,0:T(8,128)S(1)}, u32[]{:S(2)}) copy-start(f32[16,2048]{1,0:T(8,128)S(1)} %fusion.16.a_ref) | copy-start | bytes 393220
  39.4 50.6 %copy-start.2 = (bf16[64,2048]{1,0:T(8,128)(2,1)}, bf16[64,2048]{1,0:T(8,128)(2,1)S(1)}, u32[]{:S(2)}) copy-start(bf16[64,2048]{1,0:T(8,128)(2,1)S(1)} %slice.61.dtw_ref) | copy-start | bytes 786436
  40.5 49.5 %copy-start = (bf16[96,2048]{1,0:T(8,128)(2,1)}, bf16[96,2048]{1,0:T(8,128)(2,1)S(1)}, u32[]{:S(2)}) copy-start(bf16[96,2048]{1,0:T(8,128)(2,1)S(1)} %slice.60.xp_ref) | copy-start | bytes 1179652
  40.5 49.5 %copy-start.7 = (bf16[1,704,1024]{2,1,0:T(8,128)(2,1)S(1)}, bf16[1,704,1024]{2,1,0:T(8,128)(2,1)}, u32[]{:S(2)}) copy-start(bf16[1,704,1024]{2,1,0:T(8,128)(2,1)} %param.13) | copy-start | bytes 4325380
  40.5 49.5 %copy-start.16 = (bf16[2,1024,1024]{2,1,0:T(8,128)(2,1)S(1)}, bf16[2,1024,1024]{2,1,0:T(8,128)(2,1)}, u32[]{:S(2)}) copy-start(bf16[2,1024,1024]{2,1,0:T(8,128)(2,1)} %get-tuple-element.43) | copy-start | bytes 12582916
  90.0 4.3 %copy-start.3 = (f32[11,16,2048]{2,1,0:T(8,128)}, f32[11,16,2048]{2,1,0:T(8,128)S(1)}, u32[]{:S(2)}) copy-start(f32[11,16,2048]{2,1,0:T(8,128)S(1)} %get-tuple-element.52.bound_ref) | copy-start | bytes 4325380
  90.0 4.3 %copy-start.6 = (f32[11,96,64]{2,1,0:T(8,128)}, f32[11,96,64]{2,1,0:T(8,128)S(1)}, u32[]{:S(2)}) copy-start(f32[11,96,64]{2,1,0:T(8,128)S(1)} %get-tuple-element.49.proj_ref) | copy-start | bytes 811012
  90.1 4.3 %copy-start.18 = (bf16[704,2048]{1,0:T(8,128)(2,1)S(1)}, bf16[704,2048]{1,0:T(8,128)(2,1)}, u32[]{:S(2)}) copy-start(bf16[704,2048]{1,0:T(8,128)(2,1)} %get-tuple-element.54) | copy-start | bytes 8650756
  94.3 7.1 %copy-start.19 = (bf16[704,1024]{1,0:T(8,128)(2,1)S(1)}, bf16[704,1024]{1,0:T(8,128)(2,1)}, u32[]{:S(2)}) copy-start(bf16[704,1024]{1,0:T(8,128)(2,1)} %get-tuple-element.53) | copy-start | bytes 4325380
  101.4 5.1 %copy-start.8 = (bf16[1,704,1024]{2,1,0:T(8,128)(2,1)S(1)}, bf16[1,704,1024]{2,1,0:T(8,128)(2,1)}, u32[]{:S(2)}) copy-start(bf16[1,704,1024]{2,1,0:T(8,128)(2,1)} %param.25) | copy-start | bytes 4325380
  111.5 127.9 %copy-start.21 = (f32[704,1024]{1,0:T(8,128)S(1)}, f32[704,1024]{1,0:T(8,128)}, u32[]{:S(2)}) copy-start(f32[704,1024]{1,0:T(8,128)} %fusion) | copy-start | bytes 8650756
  247.6 4.4 %copy-start.14 = (f32[48,2048]{1,0:T(8,128)S(1)}, f32[48,2048]{1,0:T(8,128)}, u32[]{:S(2)}) copy-start(f32[48,2048]{1,0:T(8,128)} %get-tuple-element.60) | copy-start | bytes 1179652
  247.6 4.5 %copy-start.15 = (f32[16,2048]{1,0:T(8,128)S(1)}, f32[16,2048]{1,0:T(8,128)}, u32[]{:S(2)}) copy-start(f32[16,2048]{1,0:T(8,128)} %get-tuple-element.59) | copy-start | bytes 393220
  247.6 5.4 %copy-start.12 = (f32[96,2048]{1,0:T(8,128)S(1)}, f32[96,2048]{1,0:T(8,128)}, u32[]{:S(2)}) copy-start(f32[96,2048]{1,0:T(8,128)} %get-tuple-element.57) | copy-start | bytes 2359300
  247.6 5.5 %copy-start.13 = (f32[64,2048]{1,0:T(8,128)S(1)}, f32[64,2048]{1,0:T(8,128)}, u32[]{:S(2)}) copy-start(f32[64,2048]{1,0:T(8,128)} %get-tuple-element.58) | copy-start | bytes 1572868
  253.2 1.4 copy-start.20
  253.4 2.4 copy-start.17
  260.9 66.2 %copy-start.10 = (bf16[16,32,2048]{2,1,0:T(8,128)(2,1)S(1)}, bf16[16,32,2048]{2,1,0:T(8,128)(2,1)}, u32[]{:S(2)}) copy-start(bf16[16,32,2048]{2,1,0:T(8,128)(2,1)} %get-tuple-element.64) | copy-start | bytes 6291460
  320.0 7.1 %copy-start.11 = (bf16[16,32,2048]{2,1,0:T(8,128)(2,1)S(1)}, bf16[16,32,2048]{2,1,0:T(8,128)(2,1)}, u32[]{:S(2)}) copy-start(bf16[16,32,2048]{2,1,0:T(8,128)(2,1)} %get-tuple-element.63) | copy-start | bytes 6291460
  327.1 4.5 %copy-start.9 = (bf16[16,64,1024]{2,1,0:T(8,128)(2,1)S(1)}, bf16[16,64,1024]{2,1,0:T(8,128)(2,1)}, u32[]{:S(2)}) copy-start(bf16[16,64,1024]{2,1,0:T(8,128)(2,1)} %get-tuple-element.65) | copy-start | bytes 6291460

commit v2 on v1

--- a/solution.py
+++ b/solution.py
@@ -132,15 +132,14 @@
             else:
                 work[base + k, :, columns] = new.astype(jnp.bfloat16)
 
-    def begin(self):
-        self.barrier()
-        for p in range(len(self.pieces)):
+    def start(self, pieces):
+        for p in pieces:
             self.copy(p, 0).start()
-        for p in range(len(self.pieces)):
+        for p in pieces:
             self.own(p).start()
 
-    def finish(self, step):
-        for p in range(len(self.pieces)):
+    def advance(self, pieces, step):
+        for p in pieces:
             if step == 0:
                 self.own(p).wait()
             self.copy(p, step).wait()
@@ -150,9 +149,10 @@
                 self.copy(p, step + 1).start()
             else:
                 self.leave(p).start()
-        if step + 1 == self.steps:
-            for p in range(len(self.pieces)):
-                self.leave(p).wait()
+
+    def gone(self, pieces):
+        for p in pieces:
+            self.leave(p).wait()
 
     def times(self, count):
         heavy = (18.0, 10.0, 6.5, 14.0)
@@ -165,34 +165,11 @@
         return out
 
 
-def reduce_kernel(*refs, plan):
-    n = len(plan.shapes)
-    plan.bind(refs[:n], refs[n : 2 * n], refs[2 * n :])
-    plan.begin()
-    for step in range(plan.steps):
-        plan.finish(step)
-
-
 def reduction_of(arrays, parts):
     plan = Reduction(lax.axis_size("fsdp"), lax.axis_size("dp"), [a.shape for a in arrays], parts)
     shaped = [a.reshape(s) for a, s in zip(arrays, plan.shapes)]
     out = [jax.ShapeDtypeStruct((plan.inner,) + s[1:], jnp.bfloat16) for s in plan.shapes]
     return plan, shaped, out
-
-
-def reduce_all(arrays, parts, ident):
-    plan, shaped, out = reduction_of(arrays, parts)
-    anywhere = pl.BlockSpec(memory_space=pl.ANY)
-    out = pl.pallas_call(
-        functools.partial(reduce_kernel, plan=plan),
-        out_shape=out,
-        in_specs=[anywhere] * len(arrays),
-        out_specs=[anywhere] * len(arrays),
-        scratch_shapes=plan.scratch(),
-        compiler_params=pltpu.CompilerParams(collective_id=ident, has_side_effects=True, vmem_limit_bytes=56 << 20),
-        name="reduce_all",
-    )(*shaped)
-    return [o.reshape(-1, o.shape[-1]) for o in out]
 
 
 class Exchange:
@@ -537,6 +514,7 @@
     rows, inner = u_ref.shape
     states, rank = a_ref.shape[0], dtw_ref.shape[0]
     tiles = inner // 128
+    everything = range(len(plan.pieces))
     times = plan.times(total // rows * (tiles // width))
 
     @pl.when(pl.program_id(0) == 0)
@@ -545,7 +523,8 @@
             ref[...] = jnp.zeros_like(ref)
         ext[pl.ds(rows, 8), :] = jnp.zeros((8, inner), f32)
         off_ext[pl.ds(rows, 8), :] = jnp.full((8, 128), -1, jnp.int32)
-        plan.begin()
+        plan.barrier()
+        plan.start(everything)
 
     proj = proj_ref[0]
     wide_db[...] = jnp.zeros_like(wide_db)
@@ -560,7 +539,7 @@
             def _():
                 for step in range(plan.steps - 1):
                     if times[step] == at:
-                        plan.finish(step)
+                        plan.advance(everything, step)
 
         for j in range(width):
             lanes = pl.ds(base + 128 * j, 128)
@@ -687,7 +666,8 @@
 
     @pl.when(pl.program_id(0) == pl.num_programs(0) - 1)
     def _():
-        plan.finish(plan.steps - 1)
+        plan.advance(everything, plan.steps - 1)
+        plan.gone(everything)
 
 
 def scan_backward(saved, both, offset, proj, wide_b, wide_c, bound, params, xp, dtw, rate, chunk, width, grads, parts):
@@ -744,6 +724,129 @@
     return out[:5], [o.reshape(-1, o.shape[-1]) for o in out[5:]]
 
 
+def finish_kernel(
+    grads_ref, small_ref, upper_ref, gate_ref, gated_ref, in_ref, wout_ref, x_ref, go_ref, gain_ref,
+    total_ref, few_ref, layer_ref, left_ref,
+    upper, gate, gated, win, wout, x, go, dn, layer, mine, gain_sum, loads, away, *rest, plan, gain_row
+):
+    f32, bf16 = jnp.float32, jnp.bfloat16
+    rows, model = x.shape
+    inner = upper.shape[1]
+    plan.bind([grads_ref, mine], [total_ref, few_ref], rest)
+    main = [p for p in range(len(plan.pieces)) if plan.pieces[p][0] == 0]
+    late = [p for p in range(len(plan.pieces)) if plan.pieces[p][0] == 1]
+
+    copies = [
+        pltpu.make_async_copy(a, b, loads.at[i])
+        for i, (a, b) in enumerate(
+            (
+                (upper_ref, upper), (in_ref.at[:, pl.ds(0, inner)], win.at[0]), (gate_ref, gate),
+                (in_ref.at[:, pl.ds(inner, inner)], win.at[1]), (x_ref, x), (go_ref, go), (small_ref, mine),
+                (gated_ref, gated), (wout_ref, wout),
+            )
+        )
+    ]
+
+    def product(left, k):
+        @pl.loop(0, model // 256)
+        def _(j):
+            here = pl.ds(pl.multiple_of(j * 256, 256), 256)
+            new = lax.dot_general(left[...], win[k, here, :], (((1,), (1,)), ((), ())), preferred_element_type=f32)
+            dn[:, here] = new if k == 0 else dn[:, here] + new
+
+    plan.barrier()
+    plan.start(main)
+    for c in copies:
+        c.start()
+    copies[0].wait()
+    copies[1].wait()
+    product(upper, 0)
+    plan.advance(main, 0)
+    copies[2].wait()
+    copies[3].wait()
+    product(gate, 1)
+    copies[4].wait()
+    copies[5].wait()
+    gain_sum[...] = jnp.zeros_like(gain_sum)
+
+    @pl.loop(0, rows // 32)
+    def _(k):
+        here = pl.ds(pl.multiple_of(k * 32, 32), 32)
+        value, grad, gain = x[here, :].astype(f32), dn[here, :], gain_ref[...]
+        scale = lax.rsqrt(jnp.mean(value * value, axis=-1, keepdims=True) + norm_eps)
+        through = grad * value
+        gain_sum[...] = gain_sum[...] + folded(through * scale)
+        pull = jnp.mean(through * gain, axis=-1, keepdims=True) * (scale * scale * scale)
+        dn[here, :] = go[here, :].astype(f32) + scale * (grad * gain) - value * pull
+
+    leaving = [pltpu.make_async_copy(dn, left_ref, away.at[0]), pltpu.make_async_copy(layer, layer_ref, away.at[1])]
+    leaving[0].start()
+    copies[6].wait()
+    gain_grad = jnp.sum(gain_sum[...], axis=0, keepdims=True)
+    outer = plan.blocks // plan.inner
+    deep, r = model // outer, mine.shape[1]
+    for f in range(outer):
+        block = f * plan.inner + gain_row // r
+        old = mine[block, :, 0:deep].astype(f32)
+        new = jnp.broadcast_to(gain_grad[:, f * deep : (f + 1) * deep], (r, deep))
+        chosen = lax.broadcasted_iota(jnp.int32, (r, deep), 0) == gain_row % r
+        mine[block, :, 0:deep] = jnp.where(chosen, new, old).astype(bf16)
+    plan.start(late)
+    plan.advance(main, 1)
+    plan.advance(late, 0)
+    copies[7].wait()
+    copies[8].wait()
+
+    @pl.loop(0, model // 256)
+    def _(j):
+        here = pl.ds(pl.multiple_of(j * 256, 256), 256)
+        new = x[:, here].astype(f32) + jnp.dot(gated[...], wout[:, here], preferred_element_type=f32)
+        layer[:, here] = new.astype(bf16)
+
+    leaving[1].start()
+    for step in range(2, plan.steps):
+        plan.advance(main, step)
+        plan.advance(late, step - 1)
+    plan.advance(late, plan.steps - 1)
+    plan.gone(main + late)
+    for c in leaving:
+        c.wait()
+
+
+def finish(grads, small, upper16, gate16, gated16, w_in, w_out, x, go, gain, parts, gain_row):
+    f32, bf16 = jnp.float32, jnp.bfloat16
+    (rows, model), inner = x.shape, upper16.shape[1]
+    plan, shaped, summed = reduction_of([grads, small], parts)
+    anywhere = pl.BlockSpec(memory_space=pl.ANY)
+    flat = pltpu.VMEM((rows, inner), bf16)
+    thin = pltpu.VMEM((rows, model), bf16)
+    total, few, layer_out, input_grad = pl.pallas_call(
+        functools.partial(finish_kernel, plan=plan, gain_row=gain_row),
+        out_shape=summed + [jax.ShapeDtypeStruct((rows, model), bf16), jax.ShapeDtypeStruct((rows, model), f32)],
+        in_specs=[anywhere] * 9 + [pl.BlockSpec(memory_space=pltpu.VMEM)],
+        out_specs=[anywhere] * 4,
+        scratch_shapes=[
+            flat,
+            flat,
+            flat,
+            pltpu.VMEM((2, model, inner), bf16),
+            pltpu.VMEM((inner, model), bf16),
+            thin,
+            thin,
+            pltpu.VMEM((rows, model), f32),
+            thin,
+            pltpu.VMEM(plan.shapes[1], bf16),
+            pltpu.VMEM((8, model), f32),
+            pltpu.SemaphoreType.DMA((9,)),
+            pltpu.SemaphoreType.DMA((2,)),
+        ]
+        + plan.scratch(),
+        compiler_params=pltpu.CompilerParams(collective_id=1, has_side_effects=True, vmem_limit_bytes=56 << 20),
+        name="finish",
+    )(*shaped, upper16, gate16, gated16, w_in, w_out, x, go, gain)
+    return total.reshape(-1, total.shape[-1]), few.reshape(-1, few.shape[-1]), layer_out, input_grad
+
+
 def cluster_offsets(lengths, total_len):
     count = lengths.shape[1]
     ahead = jnp.arange(count)[:, None] < jnp.arange(count)[None, :]
@@ -755,11 +858,6 @@
     )
     first_spot = jnp.sum(jnp.where(inside, start_points[:, :, None], 0), axis=1, dtype=jnp.int32)
     return where_at[None, :] - first_spot
-
-
-def rms_piece(inputs, gain_vec):
-    mean_sq = jnp.mean(inputs * inputs, axis=-1, keepdims=True)
-    return inputs * lax.rsqrt(mean_sq + norm_eps) * gain_vec
 
 
 def dot32(left, right, contract):
@@ -810,7 +908,6 @@
     w_dt, xp = packed[:rank_dim], packed[columns:]
     parts = lax.axis_size("fsdp")
     gain_full = packed[GAIN_ROW].reshape(parts, share)[:, : model_dim // parts].reshape(model_dim).astype(f32)
-    inputs = hidden_in.reshape(rows, model_dim).astype(f32)
     *saved, gated16, gate16, proj, b_wide, c_wide, boundary, skip_sums = scan_forward(
         both, d_gated, offset, params, xp, w_dt, rate2, CHUNK, WIDTH
     )
@@ -820,25 +917,16 @@
         saved, both, offset, proj, b_wide, c_wide, boundary, params, xp, w_dt, rate2, CHUNK, WIDTH,
         [g_w_out, g_w_gate], [thirds(model_dim), thirds(inner_dim)],
     )
-    layer_out = (inputs + dot32(gated16, w_out, ((1,), (0,)))).astype(bf16)
     g_w_upper = dot32(normed16, upper16, ((0,), (0,))).astype(bf16)
-    d_normed = dot32(upper16, w_in[:, :inner_dim], ((1,), (1,))) + dot32(
-        gate16, w_in[:, inner_dim:], ((1,), (1,))
-    )
-    _, norm_pull = jax.vjp(rms_piece, inputs, gain_full)
-    d_inputs, g_gain = norm_pull(d_normed)
-    input_grad = grad_rows.astype(f32) + d_inputs
-
-    gain_row = jnp.pad(
-        g_gain.reshape(parts, model_dim // parts), ((0, 0), (0, (inner_dim - model_dim) // parts))
-    ).reshape(1, inner_dim)
     row_sums = jnp.concatenate([sums, skip_sums]).reshape(7, 8, inner_dim).sum(axis=1)
-    small = jnp.concatenate([g_w_x, g_w_dt, rate_sum * decay_rate, row_sums, gain_row], axis=0)
-    spare = -small.shape[0] % (16 * lax.axis_size("dp"))
+    small = jnp.concatenate([g_w_x, g_w_dt, rate_sum * decay_rate, row_sums], axis=0)
+    gain_row = small.shape[0]
+    spare = -(gain_row + 1) % (16 * lax.axis_size("dp")) + 1
     small = jnp.pad(small, ((0, spare), (0, 0))).astype(bf16)
     small = small.reshape(-1, parts, inner_dim // parts).transpose(1, 0, 2).reshape(-1, inner_dim // parts)
-    t_upper, t_small = reduce_all(
-        [g_w_upper, small], [thirds(inner_dim, 2), [(inner_dim // parts, ORDERS[2])]], 1
+    t_upper, t_small, layer_out, input_grad = finish(
+        g_w_upper, small, upper16, gate16, gated16, w_in, w_out, hidden_in.reshape(rows, model_dim), grad_rows,
+        gain_full[None], [thirds(inner_dim, 2), [(inner_dim // parts, ORDERS[2])]], gain_row,
     )
     t_small = t_small.astype(f32)
     t_in = jnp.concatenate([t_upper, t_gate], axis=1).astype(f32)

time: 335 us -> 322 us (0.961)
  matrix products: 34.6 us -> 18.6 us
  Pallas kernels: 262 us -> 267 us
    dot_general x6 -> x3, matrix products: 34.6 us -> 18.6 us  [dot32(): lax.dot_general(left, right, (contract, ((), ())), preferred_element_type...]
    pallas_call x1, Pallas kernels: 59.1 us -> 65.4 us  [finish(): pl.pallas_call(functools.partial(finish_kernel, plan=plan, gain_row=gain_...]
    reshape x1 -> x0, other arithmetic: 4.35 us -> none  [shards(): input_grad.reshape(hidden_in.shape)]
where the time goes in v2:
time: 322 us; the launch traced here: 321 us
  Pallas kernels  267 us (83%)
  local copies, waits for them, and re-layouts  19.1 us (6%)
  matrix products  18.6 us (6%)
  other arithmetic  15.4 us (5%)
    pallas_call x1, Pallas kernels, scan_backward(): pl.pallas_call(functools.partial(backward_kernel, width=width, plan=plan,...  127 us
    pallas_call x1, Pallas kernels, finish(): pl.pallas_call(functools.partial(finish_kernel, plan=plan, gain_row=gain_...  65.4 us
    pallas_call x1, Pallas kernels, scan_forward(): pl.pallas_call(functools.partial(forward_kernel, width=width), grid=(n,),...  49.3 us
    pallas_call x1, Pallas kernels, gather_weights(): pl.pallas_call(functools.partial(gather_kernel, plan=plan), out_shape=[ja...  25.1 us
    dot_general x3, matrix products, dot32(): lax.dot_general(left, right, (contract, ((), ())), preferred_element_type...  18.6 us

profile of v2, /device:TPU:0, one launch (start us, length us, event | category | flops | bytes accessed | tf_op | source)
XLA Modules:
  0.0 321.4 jit_solution(14117539864197359175)
XLA Ops:
  0.6 1.8 copy.27.xp_ref
  5.2 1.9 concatenate.13.vec_ref
  7.1 25.1 %gather_weights.1 = (bf16[704,1024]{1,0:T(8,128)(2,1)}, bf16[192,2048]{1,0:T(8,128)(2,1)}, bf16[2,1024,1024]{2,1,0:T(8,128)(2,1)}, bf16[2,512,4096]{2,1,0:T(8,12...) custom-call(bf16[704,1024]{1,0:T(8,128)(2,1)} %bitcast.55, bf16[704,1024]{1,0:T(8,128)(2,1)} %bitcast.57, ...), custom_call_target="tpu_custom_call" | custom-call | tf_op jit(solution)/shard_map/gather_weights/pallas_call | solution.py:315
  32.3 1.0 slice.54.xp_ref
  33.3 1.1 slice.55.dtw_ref
  34.4 0.9 fusion.8.a_ref
  35.4 0.9 slice_convert_fusion.par_ref
  36.7 49.3 %scan_forward.1 = (f32[704,2048]{1,0:T(8,128)}, f32[704,2048]{1,0:T(8,128)}, f32[704,2048]{1,0:T(8,128)}, f32[704,2048]{1,0:T(8,128)}, f32[704,2048]{1,0:T(8,128...) custom-call(f32[704,4096]{1,0:T(8,128)} %get-tuple-element.42.upper_, ...), custom_call_target="tpu_custom_call" | custom-call | tf_op jit(solution)/shard_map/scan_forward/pallas_call | solution.py:468
  86.1 8.6 %convolution_convert_fusion.1 = bf16[1024,2048]{1,0:T(8,128)(2,1)} fusion(bf16[704,1024]{1,0:T(8,128)(2,1)S(1)} %copy-done.15, bf16[704,2048]{1,0:T(8,128)(2,1)} %get-tuple-element.55.gate_ref), kind=kOutput, calls=%fused_computation.2 | convolution fusion | flops 2954887168 | bytes 8519680 | tf_op jit(solution)/shard_map/dot_general | solution.py:864
  94.7 5.0 %convolution_convert_fusion.2 = bf16[2048,1024]{1,0:T(8,128)(2,1)} fusion(bf16[704,2048]{1,0:T(8,128)(2,1)S(1)} %get-tuple-element.54.gated_ref, bf16[1,704,1024]{2,1,0:T(8,128)(2,1)S(1)} %copy-done.8), kind=kOutput, calls=%fused_computation.3 | convolution fusion | flops 2954887168 | bytes 8519680 | tf_op jit(solution)/shard_map/dot_general | solution.py:864
  99.7 127.5 %scan_backward.1 = (bf16[704,2048]{1,0:T(8,128)(2,1)}, f32[16,2048]{1,0:T(8,128)}, f32[64,2048]{1,0:T(8,128)}, f32[96,2048]{1,0:T(8,128)}, f32[48,2048]{1,0:T(8,...) custom-call(f32[704,2048]{1,0:T(8,128)} %get-tuple-element.45.u_ref, ...), custom_call_target="tpu_custom_call" | custom-call | tf_op jit(solution)/shard_map/scan_backward/pallas_call | solution.py:685
  227.2 0.9 multiply_convert_fusion
  228.2 1.1 fusion.7
  229.3 1.3 convert.16
  230.6 1.1 convert.17
  231.8 1.1 copy.32
  232.9 5.0 %convolution_convert_fusion = bf16[1024,2048]{1,0:T(8,128)(2,1)} fusion(bf16[704,1024]{1,0:T(8,128)(2,1)S(1)} %copy-done.15, bf16[704,2048]{1,0:T(8,128)(2,1)S(1)} %copy-done.10), kind=kOutput, calls=%fused_computation.1 | convolution fusion | flops 2954887168 | bytes 8519680 | tf_op jit(solution)/shard_map/dot_general | solution.py:864
  237.9 0.8 slice_reduce_fusion
  239.3 65.4 %finish.1 = (bf16[16,32,2048]{2,1,0:T(8,128)(2,1)}, bf16[16,16,1024]{2,1,0:T(8,128)(2,1)}, bf16[704,1024]{1,0:T(8,128)(2,1)}, f32[704,1024]{1,0:T(8,128)}) custom-call(bf16[32,32,2048]{2,1,0:T(8,128)(2,1)} %bitcast.64, bf16[32,16,1024]{2,1,0:T(8,128)(2,1)} %bitcast.61, bf16[704,2048]{1,0:T(8,128)(2,1)} %get-tuple-element.56.upper_ref, ...), custom_call_target="tpu_custom_call" | custom-call | tf_op jit(solution)/shard_map/finish/pallas_call | solution.py:823
  304.7 6.1 %maximum_convert_fusion = f32[512,4096]{1,0:T(8,128)} fusion(bf16[512,2048]{1,0:T(8,128)(2,1)S(1)} %bitcast.66, bf16[512,2048]{1,0:T(8,128)(2,1)} %bitcast.67), kind=kLoop, calls=%fused_computation | loop fusion | flops 8388608 | bytes 12582912 | tf_op jit(solution)/shard_map/convert_element_type | solution.py:932
  314.9 2.6 bitcast_convert_fusion
  317.5 1.1 copy.35
  318.6 1.2 copy-done.9
  319.8 1.6 copy.36
  (55 shorter events, 7.9 us)
Async XLA Ops:
  7.1 29.2 %copy-start.16 = (s32[1,8]{1,0:T(1,128)S(1)}, s32[1,8]{1,0:T(1,128)}, u32[]{:S(2)}) copy-start(s32[1,8]{1,0:T(1,128)} %param.14) | copy-start | bytes 100
  33.3 52.7 %copy-start = (bf16[96,2048]{1,0:T(8,128)(2,1)}, bf16[96,2048]{1,0:T(8,128)(2,1)S(1)}, u32[]{:S(2)}) copy-start(bf16[96,2048]{1,0:T(8,128)(2,1)S(1)} %slice.54.xp_ref) | copy-start | bytes 1179652
  34.4 51.6 %copy-start.3 = (bf16[64,2048]{1,0:T(8,128)(2,1)}, bf16[64,2048]{1,0:T(8,128)(2,1)S(1)}, u32[]{:S(2)}) copy-start(bf16[64,2048]{1,0:T(8,128)(2,1)S(1)} %slice.55.dtw_ref) | copy-start | bytes 786436
  35.4 50.7 %copy-start.5 = (f32[16,2048]{1,0:T(8,128)}, f32[16,2048]{1,0:T(8,128)S(1)}, u32[]{:S(2)}) copy-start(f32[16,2048]{1,0:T(8,128)S(1)} %fusion.8.a_ref) | copy-start | bytes 393220
  36.3 49.8 %copy-start.6 = (f32[8,2048]{1,0:T(8,128)}, f32[8,2048]{1,0:T(8,128)S(1)}, u32[]{:S(2)}) copy-start(f32[8,2048]{1,0:T(8,128)S(1)} %slice_convert_fusion.par_ref) | copy-start | bytes 196612
  36.7 49.4 %copy-start.1 = (s32[704,128]{1,0:T(8,128)}, s32[704,128]{1,0:T(8,128)S(1)}, u32[]{:S(2)}) copy-start(s32[704,128]{1,0:T(8,128)S(1)} %broadcast_in_dim.61.off_ref) | copy-start | bytes 1081348
  36.7 49.4 %copy-start.15 = (bf16[704,1024]{1,0:T(8,128)(2,1)S(1)}, bf16[704,1024]{1,0:T(8,128)(2,1)}, u32[]{:S(2)}) copy-start(bf16[704,1024]{1,0:T(8,128)(2,1)} %get-tuple-element.41) | copy-start | bytes 4325380
  86.1 8.6 %copy-start.4 = (f32[11,16,2048]{2,1,0:T(8,128)}, f32[11,16,2048]{2,1,0:T(8,128)S(1)}, u32[]{:S(2)}) copy-start(f32[11,16,2048]{2,1,0:T(8,128)S(1)} %get-tuple-element.53.bound_ref) | copy-start | bytes 4325380
  86.1 8.6 %copy-start.7 = (f32[11,96,64]{2,1,0:T(8,128)}, f32[11,96,64]{2,1,0:T(8,128)S(1)}, u32[]{:S(2)}) copy-start(f32[11,96,64]{2,1,0:T(8,128)S(1)} %get-tuple-element.50.proj_ref) | copy-start | bytes 811012
  86.1 8.6 %copy-start.2 = (bf16[704,2048]{1,0:T(8,128)(2,1)}, bf16[704,2048]{1,0:T(8,128)(2,1)S(1)}, u32[]{:S(2)}) copy-start(bf16[704,2048]{1,0:T(8,128)(2,1)S(1)} %get-tuple-element.54.gated_ref) | copy-start | bytes 8650756
  86.1 8.6 %copy-start.8 = (bf16[1,704,1024]{2,1,0:T(8,128)(2,1)S(1)}, bf16[1,704,1024]{2,1,0:T(8,128)(2,1)}, u32[]{:S(2)}) copy-start(bf16[1,704,1024]{2,1,0:T(8,128)(2,1)} %param.25) | copy-start | bytes 4325380
  229.3 3.6 %copy-start.10 = (bf16[704,2048]{1,0:T(8,128)(2,1)S(1)}, bf16[704,2048]{1,0:T(8,128)(2,1)}, u32[]{:S(2)}) copy-start(bf16[704,2048]{1,0:T(8,128)(2,1)} %get-tuple-element.56.upper_ref) | copy-start | bytes 8650756
  239.3 65.4 %copy-start.13 = (bf16[16,32,2048]{2,1,0:T(8,128)(2,1)S(1)}, bf16[16,32,2048]{2,1,0:T(8,128)(2,1)}, u32[]{:S(2)}) copy-start(bf16[16,32,2048]{2,1,0:T(8,128)(2,1)} %get-tuple-element.68) | copy-start | bytes 6291460
  304.7 6.1 %copy-start.11 = (bf16[16,16,1024]{2,1,0:T(8,128)(2,1)S(1)}, bf16[16,16,1024]{2,1,0:T(8,128)(2,1)}, u32[]{:S(2)}) copy-start(bf16[16,16,1024]{2,1,0:T(8,128)(2,1)} %get-tuple-element.66) | copy-start | bytes 1572868
  310.8 4.0 %copy-start.12 = (bf16[16,64,1024]{2,1,0:T(8,128)(2,1)S(1)}, bf16[16,64,1024]{2,1,0:T(8,128)(2,1)}, u32[]{:S(2)}) copy-start(bf16[16,64,1024]{2,1,0:T(8,128)(2,1)} %get-tuple-element.69) | copy-start | bytes 6291460
  314.9 2.6 copy-start.14
  317.5 2.3 copy-start.9

commit v3 on v2

--- a/solution.py
+++ b/solution.py
@@ -11,6 +11,9 @@
 CHUNK = 64
 WIDTH = 4
 norm_eps = 1e-05
+BIG = 1e30
+LN2 = math.log(2.0)
+LOG2E = 1.0 / LN2
 
 def bits_of(size):
     return size.bit_length() - 1
@@ -201,12 +204,9 @@
         )
 
 
-GAIN_ROW = 80
-
-
 def gather_kernel(
-    x_ref, go_ref, dt_ref, rate_ref, vec_ref, xp_ref, wout_ref, win_ref,
-    normed_ref, pack_out, wout_out, win_out, dg_out, both_out,
+    x_ref, go_ref, dt_ref, rate_ref, taps_ref, vec_ref, xp_ref, wout_ref, win_ref,
+    normed_ref, dtw_ref, xpw_ref, decay_ref, par_ref, gain_ref, wout_out, win_out, dg_out, both_out,
     pack, wout, win, dg, both, packed, send, recv, leave, tiles, *, plan
 ):
     f32, bf16 = jnp.float32, jnp.bfloat16
@@ -223,11 +223,18 @@
             target = (wout, win)[which - 1].at[me]
         return plan.copy(source, target, sems, which, turn)
 
-    at = 0
-    for ref in (dt_ref, rate_ref, vec_ref):
-        packed[at : at + ref.shape[0], :] = ref[...]
-        at += ref.shape[0]
-    packed[at:, :] = xp_ref[...].astype(f32).T.astype(bf16)
+    lines = share // 128
+    vectors = vec_ref[...].astype(f32)
+    line = [
+        jnp.concatenate([vectors[k : k + 1] for k in range(v * lines, (v + 1) * lines)], axis=1) for v in range(4)
+    ]
+    few = [line[0], taps_ref[...].astype(f32)] + line[1:]
+    depth, states, taps = dt_ref.shape[0], rate_ref.shape[0], taps_ref.shape[0]
+    few.append(jnp.zeros((16 - 4 - taps, share), f32))
+    packed[0:depth, :] = dt_ref[...]
+    packed[depth : depth + states, :] = rate_ref[...]
+    packed[depth + states : depth + states + 16, :] = jnp.concatenate(few, axis=0).astype(bf16)
+    packed[depth + states + 16 :, :] = xp_ref[...]
     plan.barrier()
     for which in range(3):
         for turn in range(1, plan.size):
@@ -266,11 +273,13 @@
     times_out(0)
     for turn in range(plan.size):
         copies(0, turn).wait()
-    whole_pack = pltpu.make_async_copy(pack, pack_out, leave.at[3, 0])
-    whole_pack.start()
-    gain = jnp.concatenate(
-        [pack[GAIN_ROW : GAIN_ROW + 16, b * share : b * share + deep] for b in range(plan.size)], axis=1
-    ).astype(f32)[:1]
+    dtw_ref[...] = pack[0:depth, :]
+    xpw_ref[...] = pack[depth + states + 16 :, :]
+    decay_ref[...] = -jnp.exp(pack[depth : depth + states, :].astype(f32)) * LOG2E
+    few = pack[depth + states : depth + states + 16, :].astype(f32)
+    par_ref[...] = few[1:9]
+    gain = jnp.concatenate([few[:1, b * share : b * share + deep] for b in range(plan.size)], axis=1)
+    gain_ref[...] = jnp.broadcast_to(gain, gain_ref.shape)
 
     @pl.loop(0, rows // 64)
     def _(k):
@@ -287,7 +296,6 @@
     for turn in range(1, plan.size):
         copies(2, turn).wait()
         times_in(turn)
-    whole_pack.wait()
     for turn in range(plan.size):
         at = plan.owner(turn)
         part = pl.ds(pl.multiple_of(at * share, 128), share)
@@ -305,35 +313,35 @@
     f32, bf16 = jnp.float32, jnp.bfloat16
     plan = Exchange(lax.axis_size("fsdp"))
     n, (rows, model), wide = plan.size, x.shape, w_in.shape[1]
-    depth, share = sum(s.shape[0] for s in small[:3]) + small[3].shape[1], small[0].shape[1]
+    (rank, share), states, cols = small[0].shape, small[1].shape[0], small[4].shape[0]
     inner = n * share
     anywhere = pl.BlockSpec(memory_space=pl.ANY)
     near = pl.BlockSpec(memory_space=pltpu.VMEM)
     shapes = [
-        ((depth, inner), bf16), ((n,) + w_out.shape, bf16), ((n,) + w_in.shape, bf16), ((rows, inner), f32), ((rows, wide), f32),
+        ((rank + states + 16 + cols, inner), bf16), ((n,) + w_out.shape, bf16), ((n,) + w_in.shape, bf16), ((rows, inner), f32), ((rows, wide), f32),
     ]
-    normed, packed, out_all, in_all, d_gated, both = pl.pallas_call(
+    outs = [
+        (x.shape, bf16), ((rank, inner), bf16), ((cols, inner), bf16), ((states, inner), f32), ((8, inner), f32), ((8, model), f32),
+    ]
+    *made, out_all, in_all, d_gated, both = pl.pallas_call(
         functools.partial(gather_kernel, plan=plan),
-        out_shape=[jax.ShapeDtypeStruct(x.shape, bf16)] + [jax.ShapeDtypeStruct(*s) for s in shapes],
-        in_specs=[near] * 6 + [anywhere] * 2,
-        out_specs=[near] + [anywhere] * 5,
+        out_shape=[jax.ShapeDtypeStruct(*s) for s in outs + shapes[1:]],
+        in_specs=[near] * 7 + [anywhere] * 2,
+        out_specs=[near] * 6 + [anywhere] * 4,
         scratch_shapes=[pltpu.VMEM(*s) for s in shapes]
         + [
-            pltpu.VMEM((depth, share), bf16),
+            pltpu.VMEM((shapes[0][0][0], share), bf16),
             pltpu.SemaphoreType.DMA((3, n)),
             pltpu.SemaphoreType.DMA((3, n)),
-            pltpu.SemaphoreType.DMA((4, n)),
+            pltpu.SemaphoreType.DMA((3, n)),
             pltpu.SemaphoreType.DMA((wide // 256,)),
         ],
         compiler_params=pltpu.CompilerParams(collective_id=2, has_side_effects=True, vmem_limit_bytes=56 << 20),
         name="gather_weights",
     )(x, grad_rows, *small, w_out, w_in)
-    return normed, packed, out_all.reshape(-1, w_out.shape[1]), in_all.reshape(-1, wide), d_gated, both
-
-
-BIG = 1e30
-LN2 = math.log(2.0)
-LOG2E = 1.0 / LN2
+    return made, out_all.reshape(-1, w_out.shape[1]), in_all.reshape(-1, wide), d_gated, both
+
+
 TAPS, SHIFT, DT_BIAS, SKIP = 0, 4, 5, 6
 
 
@@ -496,19 +504,20 @@
             tile(f32),
             pltpu.VMEM((width, 64, 128), f32),
         ],
-        compiler_params=pltpu.CompilerParams(dimension_semantics=("arbitrary",), vmem_limit_bytes=48 << 20),
+        compiler_params=pltpu.CompilerParams(dimension_semantics=("arbitrary",), vmem_limit_bytes=62 << 20),
         name="scan_forward",
     )(both, both, d_gated, offset, params, xp, dtw, rate)
 
 
 def backward_kernel(
-    u_ref, ds_ref, dt_ref, sg_ref, dy_ref, upper_ref, off_ref, proj_ref, wide_b, wide_c, bound_ref, par_ref, xp_ref, dtw_ref, a_ref,
+    u_ref, ds_ref, dt_ref, sg_ref, dy_ref, upper_ref, off_ref, proj_ref, wide_b, wide_c, bound_ref, par_ref, xp_ref, dtw_ref, a_ref, skip_ref,
     *rest, width, plan, total
 ):
     f32, bf16 = jnp.float32, jnp.bfloat16
     n = len(plan.shapes)
     given, rest = rest[:n], rest[n:]
-    (du_ref, ga_ref, gdt_ref, gx_ref, sum_ref), out, rest = rest[:5], rest[5 : 5 + n], rest[5 + n :]
+    (du_ref, small_ref), out, rest = rest[:2], rest[2 : 2 + n], rest[2 + n :]
+    ga_ref, gdt_ref, gx_ref, sum_ref, *rest = rest
     ws, dtm, dtu, dyb, hbuf, sbuf, qbuf, dd, di, u16, dt16, ext, off_ext, wide_db, wide_dc, cols_ref = rest[:16]
     plan.bind(given, out, rest[16:])
     rows, inner = u_ref.shape
@@ -666,11 +675,22 @@
 
     @pl.when(pl.program_id(0) == pl.num_programs(0) - 1)
     def _():
+        share = small_ref.shape[1]
+        deep = small_ref.shape[0] // (inner // share)
+        sums = [jnp.sum(sum_ref[pl.ds(8 * k, 8), :], axis=0, keepdims=True) for k in range(6)]
+        sums += [jnp.sum(skip_ref[...], axis=0, keepdims=True), jnp.zeros((9, inner), f32)]
+        blocks = [gx_ref[...], gdt_ref[...], ga_ref[...] * a_ref[...] * LN2, jnp.concatenate(sums, axis=0)]
+        for f in range(inner // share):
+            at = f * deep
+            for block in blocks:
+                small_ref[at : at + block.shape[0], :] = block[:, f * share : (f + 1) * share].astype(bf16)
+                at += block.shape[0]
+            small_ref[at : (f + 1) * deep, :] = jnp.zeros(((f + 1) * deep - at, share), bf16)
         plan.advance(everything, plan.steps - 1)
         plan.gone(everything)
 
 
-def scan_backward(saved, both, offset, proj, wide_b, wide_c, bound, params, xp, dtw, rate, chunk, width, grads, parts):
+def scan_backward(saved, both, offset, proj, wide_b, wide_c, bound, params, xp, dtw, rate, skip, chunk, width, grads, parts):
     T, DI = saved[0].shape
     n, states, cols, rank = T // chunk, rate.shape[0], xp.shape[0], dtw.shape[0]
     f32, bf16 = jnp.float32, jnp.bfloat16
@@ -678,7 +698,9 @@
     whole = lambda a: pl.BlockSpec(a.shape, lambda i: (0, 0))
     anywhere = pl.BlockSpec(memory_space=pl.ANY)
     plan, shaped, summed = reduction_of(grads, parts)
-    sums = [jax.ShapeDtypeStruct((r, DI), f32) for r in (states, rank, cols, 48)]
+    outer, inner = lax.axis_size("fsdp"), lax.axis_size("dp")
+    deep = -(-(states + rank + cols + 16) // (16 * inner)) * 16 * inner
+    small = jax.ShapeDtypeStruct((outer * deep, DI // outer), bf16)
     pieces = pltpu.VMEM((width, chunk, 128), f32)
     eights = pltpu.VMEM((width, 64, 128), f32)
     tall = pltpu.VMEM((chunk * states, 128), f32)
@@ -693,11 +715,12 @@
             pl.BlockSpec((chunk * states, 128), lambda i: (n - 1 - i, 0)),
             pl.BlockSpec((1, states, DI), lambda i: (n - 1 - i, 0, 0)),
         ]
-        + [whole(a) for a in (params, xp, dtw, rate)]
+        + [whole(a) for a in (params, xp, dtw, rate, skip)]
         + [anywhere] * len(grads),
-        out_specs=[row] + [whole(a) for a in sums] + [anywhere] * len(grads),
-        out_shape=[jax.ShapeDtypeStruct((T, DI), bf16)] + sums + summed,
-        scratch_shapes=[
+        out_specs=[row, whole(small)] + [anywhere] * len(grads),
+        out_shape=[jax.ShapeDtypeStruct((T, DI), bf16), small] + summed,
+        scratch_shapes=[pltpu.VMEM((r, DI), f32) for r in (states, rank, cols, 48)]
+        + [
             pltpu.VMEM((states, DI), f32),
             pieces,
             pieces,
@@ -720,8 +743,8 @@
             dimension_semantics=("arbitrary",), collective_id=0, has_side_effects=True, vmem_limit_bytes=56 << 20
         ),
         name="scan_backward",
-    )(*saved, both, offset, proj, wide_b, wide_c, bound, params, xp, dtw, rate, *shaped)
-    return out[:5], [o.reshape(-1, o.shape[-1]) for o in out[5:]]
+    )(*saved, both, offset, proj, wide_b, wide_c, bound, params, xp, dtw, rate, skip, *shaped)
+    return out[:2], [o.reshape(-1, o.shape[-1]) for o in out[2:]]
 
 
 def finish_kernel(
@@ -772,7 +795,7 @@
     @pl.loop(0, rows // 32)
     def _(k):
         here = pl.ds(pl.multiple_of(k * 32, 32), 32)
-        value, grad, gain = x[here, :].astype(f32), dn[here, :], gain_ref[...]
+        value, grad, gain = x[here, :].astype(f32), dn[here, :], gain_ref[0:1, :]
         scale = lax.rsqrt(jnp.mean(value * value, axis=-1, keepdims=True) + norm_eps)
         through = grad * value
         gain_sum[...] = gain_sum[...] + folded(through * scale)
@@ -847,6 +870,50 @@
     return total.reshape(-1, total.shape[-1]), few.reshape(-1, few.shape[-1]), layer_out, input_grad
 
 
+def write_kernel(
+    upper_ref, gate_ref, out_ref, small_ref, layer_ref, left_ref,
+    in_to, out_to, x_to, dt_to, rate_to, taps_to, shift_to, bias_to, skip_to, gain_to, layer_to, left_to,
+):
+    f32 = jnp.float32
+    wide = upper_ref.shape[1]
+    in_to[:, 0:wide] = upper_ref[...].astype(f32)
+    in_to[:, wide:] = gate_ref[...].astype(f32)
+    out_to[...] = out_ref[...].astype(f32)
+    layer_to[...] = layer_ref[...]
+    left_to[...] = left_ref[...]
+
+    @pl.when(pl.program_id(0) == 0)
+    def _():
+        at = 0
+        for ref in (x_to, dt_to, rate_to):
+            ref[...] = small_ref[at : at + ref.shape[0], :].astype(f32)
+            at += ref.shape[0]
+        few = small_ref[at : at + 16, :].astype(f32)
+        at = 0
+        for ref in (taps_to, shift_to, bias_to, skip_to, gain_to):
+            ref[...] = few[at : at + ref.shape[0], : ref.shape[1]]
+            at += ref.shape[0]
+
+
+def write_outputs(upper, gate, out, small, layer, left, sizes):
+    f32, share, steps = jnp.float32, small.shape[1], 4
+    few = [(r, share) for r in sizes[:-1]] + [(1, sizes[-1])]
+    part = lambda a: pl.BlockSpec((a.shape[0] // steps, a.shape[1]), lambda i: (i, 0))
+    whole = lambda a: pl.BlockSpec(a.shape, lambda i: (0, 0))
+    big = [jax.ShapeDtypeStruct((upper.shape[0], upper.shape[1] + gate.shape[1]), f32), jax.ShapeDtypeStruct(out.shape, f32)]
+    few = [jax.ShapeDtypeStruct(a, f32) for a in few]
+    last = [jax.ShapeDtypeStruct(a.shape, a.dtype) for a in (layer, left)]
+    return pl.pallas_call(
+        write_kernel,
+        grid=(steps,),
+        in_specs=[part(upper), part(gate), part(out), whole(small), part(layer), part(left)],
+        out_specs=[part(a) for a in big] + [whole(a) for a in few] + [part(a) for a in last],
+        out_shape=big + few + last,
+        compiler_params=pltpu.CompilerParams(dimension_semantics=("arbitrary",), vmem_limit_bytes=62 << 20),
+        name="write_outputs",
+    )(upper, gate, out, small, layer, left)
+
+
 def cluster_offsets(lengths, total_len):
     count = lengths.shape[1]
     ahead = jnp.arange(count)[:, None] < jnp.arange(count)[None, :]
@@ -895,52 +962,36 @@
     offset = jnp.broadcast_to(offsets[:, None], (rows, 128))
     grad_rows = out_grad.reshape(rows, model_dim)
     gain_part = jnp.pad(norm_gain, (0, share - norm_gain.shape[0]))
-    vectors = [v[None] for v in (gain_part,)] + [conv_weight] + [v[None] for v in (conv_bias, dt_bias, skip_gain)]
-    spare = columns - rank_dim - state_dim - taps - 4
-    vectors = jnp.concatenate(vectors + [jnp.zeros((spare, share), bf16)], axis=0)
-    normed16, packed, w_out, w_in, d_gated, both = gather_weights(
-        hidden_in.reshape(rows, model_dim), grad_rows, (dt_proj, a_log, vectors, x_proj), out_proj, in_proj
+    vectors = jnp.concatenate([gain_part, conv_bias, dt_bias, skip_gain]).reshape(-1, 128)
+    x = hidden_in.reshape(rows, model_dim)
+    (normed16, w_dt, xp, rate2, params, gain), w_out, w_in, d_gated, both = gather_weights(
+        x, grad_rows, (dt_proj, a_log, conv_weight, vectors, x_proj.T), out_proj, in_proj
     )
-    inner_dim = packed.shape[1]
-    decay_rate = -jnp.exp(packed[rank_dim : rank_dim + state_dim].astype(f32))
-    rate2 = decay_rate * LOG2E
-    params = packed[GAIN_ROW + 1 : GAIN_ROW + 9].astype(f32)
-    w_dt, xp = packed[:rank_dim], packed[columns:]
+    inner_dim = params.shape[1]
     parts = lax.axis_size("fsdp")
-    gain_full = packed[GAIN_ROW].reshape(parts, share)[:, : model_dim // parts].reshape(model_dim).astype(f32)
     *saved, gated16, gate16, proj, b_wide, c_wide, boundary, skip_sums = scan_forward(
         both, d_gated, offset, params, xp, w_dt, rate2, CHUNK, WIDTH
     )
     g_w_out = dot32(gated16, grad_rows, ((0,), (0,))).astype(bf16)
     g_w_gate = dot32(normed16, gate16, ((0,), (0,))).astype(bf16)
-    (upper16, rate_sum, g_w_dt, g_w_x, sums), (t_out, t_gate) = scan_backward(
-        saved, both, offset, proj, b_wide, c_wide, boundary, params, xp, w_dt, rate2, CHUNK, WIDTH,
+    (upper16, small), (t_out, t_gate) = scan_backward(
+        saved, both, offset, proj, b_wide, c_wide, boundary, params, xp, w_dt, rate2, skip_sums, CHUNK, WIDTH,
         [g_w_out, g_w_gate], [thirds(model_dim), thirds(inner_dim)],
     )
     g_w_upper = dot32(normed16, upper16, ((0,), (0,))).astype(bf16)
-    row_sums = jnp.concatenate([sums, skip_sums]).reshape(7, 8, inner_dim).sum(axis=1)
-    small = jnp.concatenate([g_w_x, g_w_dt, rate_sum * decay_rate, row_sums], axis=0)
-    gain_row = small.shape[0]
-    spare = -(gain_row + 1) % (16 * lax.axis_size("dp")) + 1
-    small = jnp.pad(small, ((0, spare), (0, 0))).astype(bf16)
-    small = small.reshape(-1, parts, inner_dim // parts).transpose(1, 0, 2).reshape(-1, inner_dim // parts)
+    gain_row = columns + rank_dim + state_dim + taps + 3
     t_upper, t_small, layer_out, input_grad = finish(
-        g_w_upper, small, upper16, gate16, gated16, w_in, w_out, hidden_in.reshape(rows, model_dim), grad_rows,
-        gain_full[None], [thirds(inner_dim, 2), [(inner_dim // parts, ORDERS[2])]], gain_row,
+        g_w_upper, small, upper16, gate16, gated16, w_in, w_out, x, grad_rows,
+        gain, [thirds(inner_dim, 2), [(inner_dim // parts, ORDERS[2])]], gain_row,
     )
-    t_small = t_small.astype(f32)
-    t_in = jnp.concatenate([t_upper, t_gate], axis=1).astype(f32)
-    t_out = t_out.astype(f32)
-    at = 0
-    picked = []
-    for size in (columns, rank_dim, state_dim, taps, 1, 1, 1, 1):
-        picked.append(t_small[at : at + size])
-        at += size
-    t_x, t_dt, t_alog, t_conv, t_b_conv, t_b_dt, t_skip, t_gain = picked
+    t_in, t_out, t_x, t_dt, t_alog, t_conv, t_b_conv, t_b_dt, t_skip, t_gain, layer_out, input_grad = write_outputs(
+        t_upper, t_gate, t_out, t_small, layer_out, input_grad,
+        (columns, rank_dim, state_dim, taps, 1, 1, 1, model_dim // parts),
+    )
     return (
         layer_out.reshape(hidden_in.shape),
         input_grad.reshape(hidden_in.shape),
-        t_gain[0, : model_dim // parts],
+        t_gain[0],
         t_in,
         t_conv,
         t_b_conv[0],

time: 322 us -> 304 us (0.944)
  local copies, waits for them, and re-layouts: 19.1 us -> 1.59 us
  other arithmetic: 15.4 us -> 2.8 us
  Pallas kernels: 267 us -> 279 us
    pallas_call x0 -> x1, Pallas kernels: none -> 11.5 us  [write_outputs(): pl.pallas_call(write_kernel, grid=(steps,), in_specs=[part(upper), part(g...]
    convert_element_type x4 -> x0, other arithmetic: 9.75 us -> none  [the longest x1 6.13 us: shards(): t_in = jnp.concatenate([t_upper, t_gate], axis=1).astype(f32)]
    slice x9 -> x0, local copies, waits for them, and re-layouts: 6.85 us -> none  [the longest x5 3.35 us: shards(): picked.append(t_small[at:at + size])]
    unnamed x38 -> x6, local copies, waits for them, and re-layouts: 6.35 us -> 0.01 us
    another operation x3 -> x0, other arithmetic: 3.34 us -> none
where the time goes in v3:
time: 304 us
  Pallas kernels  279 us (92%)
  matrix products  19.1 us (6%)
    pallas_call x1, Pallas kernels, scan_backward(): pl.pallas_call(functools.partial(backward_kernel, width=width, plan=plan,...  127 us
    pallas_call x1, Pallas kernels, finish(): pl.pallas_call(functools.partial(finish_kernel, plan=plan, gain_row=gain_...  65.5 us
    pallas_call x1, Pallas kernels, scan_forward(): pl.pallas_call(functools.partial(forward_kernel, width=width), grid=(n,),...  49.6 us
    pallas_call x1, Pallas kernels, gather_weights(): pl.pallas_call(functools.partial(gather_kernel, plan=plan), out_shape=[ja...  25.3 us
    dot_general x3, matrix products, dot32(): lax.dot_general(left, right, (contract, ((), ())), preferred_element_type...  19.1 us
    pallas_call x1, Pallas kernels, write_outputs(): pl.pallas_call(write_kernel, grid=(steps,), in_specs=[part(upper), part(g...  11.5 us

profile of v3, /device:TPU:0, one launch (start us, length us, event | category | flops | bytes accessed | tf_op | source)
XLA Modules:
  0.0 303.5 jit_solution(4856265086382396496)
XLA Ops:
  0.6 0.7 select_reduce_fusion.1
  1.4 0.7 fusion.1
  2.0 0.7 pad_bitcast_fusion
  2.7 0.1 select_reduce_fusion
  2.8 1.3 pad_maximum_fusion.vec_ref
  4.1 0.9 broadcast_in_dim.27.off_ref
  5.0 25.3 %gather_weights.1 = (bf16[704,1024]{1,0:T(8,128)(2,1)}, bf16[64,2048]{1,0:T(8,128)(2,1)}, bf16[96,2048]{1,0:T(8,128)(2,1)}, f32[16,2048]{1,0:T(8,128)}, f32[8,20...) custom-call(bf16[704,1024]{1,0:T(8,128)(2,1)} %bitcast.40, ...), custom_call_target="tpu_custom_call" | custom-call | tf_op jit(solution)/shard_map/gather_weights/pallas_call | solution.py:326
  30.4 0.0 copy-start
  30.4 49.6 %scan_forward.1 = (f32[704,2048]{1,0:T(8,128)}, f32[704,2048]{1,0:T(8,128)}, f32[704,2048]{1,0:T(8,128)}, f32[704,2048]{1,0:T(8,128)}, f32[704,2048]{1,0:T(8,128...) custom-call(f32[704,4096]{1,0:T(8,128)} %get-tuple-element.55.upper_, ...), custom_call_target="tpu_custom_call" | custom-call | tf_op jit(solution)/shard_map/scan_forward/pallas_call | solution.py:476
  80.0 0.0 copy-done
  80.0 0.0 copy-start.1
  80.0 0.0 copy-start.2
  80.0 7.0 %convolution_convert_fusion.2 = bf16[2048,1024]{1,0:T(8,128)(2,1)} fusion(bf16[704,2048]{1,0:T(8,128)(2,1)} %get-tuple-element.71.gated_ref, bf16[1,704,1024]{2,1,0:T(8,128)(2,1)S(1)} %copy-done), kind=kOutput, calls=%fused_computation.2 | convolution fusion | flops 2954887168 | bytes 8519680 | tf_op jit(solution)/shard_map/dot_general | solution.py:931
  87.0 0.0 copy-done.1
  87.0 0.0 copy-done.2
  87.0 5.0 %convolution_convert_fusion.1 = bf16[1024,2048]{1,0:T(8,128)(2,1)} fusion(bf16[704,1024]{1,0:T(8,128)(2,1)S(1)} %copy-done.2, bf16[704,2048]{1,0:T(8,128)(2,1)S(1)} %copy-done.1), kind=kOutput, calls=%fused_computation.1 | convolution fusion | flops 2954887168 | bytes 8519680 | tf_op jit(solution)/shard_map/dot_general | solution.py:931
  92.1 127.2 %scan_backward.1 = (bf16[704,2048]{1,0:T(8,128)(2,1)}, bf16[512,1024]{1,0:T(8,128)(2,1)}, bf16[16,64,1024]{2,1,0:T(8,128)(2,1)}, bf16[16,32,2048]{2,1,0:T(8,128)(2,1)}) custom-call(f32[704,2048]{1,0:T(8,128)} %get-tuple-element.61.u_ref, f32[704,2048]{1,0:T(8,128)} %get-tuple-element.62.ds_ref, f32[704,2048]{1,0:T(8,128)} %get-tuple-element.63.dt_ref, ...), custom_call_target="tpu_custom_call" | custom-call | tf_op jit(solution)/shard_map/scan_backward/pallas_call | solution.py:707
  219.3 7.0 %convolution_convert_fusion = bf16[1024,2048]{1,0:T(8,128)(2,1)} fusion(bf16[704,1024]{1,0:T(8,128)(2,1)S(1)} %copy-done.2, bf16[704,2048]{1,0:T(8,128)(2,1)} %get-tuple-element.73.upper_ref), kind=kOutput, calls=%fused_computation | convolution fusion | flops 2954887168 | bytes 8519680 | tf_op jit(solution)/shard_map/dot_general | solution.py:931
  226.3 65.5 %finish.1 = (bf16[16,32,2048]{2,1,0:T(8,128)(2,1)}, bf16[16,16,1024]{2,1,0:T(8,128)(2,1)}, bf16[704,1024]{1,0:T(8,128)(2,1)}, f32[704,1024]{1,0:T(8,128)}) custom-call(bf16[32,32,2048]{2,1,0:T(8,128)(2,1)} %bitcast.47, bf16[32,16,1024]{2,1,0:T(8,128)(2,1)} %bitcast.51, bf16[704,2048]{1,0:T(8,128)(2,1)} %get-tuple-element.73.upper_ref, ...), custom_call_target="tpu_custom_call" | custom-call | tf_op jit(solution)/shard_map/finish/pallas_call | solution.py:846
  291.8 11.5 %write_outputs.1 = (f32[512,4096]{1,0:T(8,128)}, f32[1024,1024]{1,0:T(8,128)}, f32[96,1024]{1,0:T(8,128)}, f32[64,1024]{1,0:T(8,128)}, f32[16,1024]{1,0:T(8,128)...) custom-call(bf16[512,2048]{1,0:T(8,128)(2,1)} %bitcast.50, ...), custom_call_target="tpu_custom_call" | custom-call | tf_op jit(solution)/shard_map/write_outputs/pallas_call | solution.py:906
  (1 shorter events, 0.0 us)
Async XLA Ops:
  30.4 49.6 %copy-start = (bf16[1,704,1024]{2,1,0:T(8,128)(2,1)S(1)}, bf16[1,704,1024]{2,1,0:T(8,128)(2,1)}, u32[]{:S(2)}) copy-start(bf16[1,704,1024]{2,1,0:T(8,128)(2,1)} %param.25) | copy-start | bytes 4325380
  80.0 7.0 %copy-start.1 = (bf16[704,2048]{1,0:T(8,128)(2,1)S(1)}, bf16[704,2048]{1,0:T(8,128)(2,1)}, u32[]{:S(2)}) copy-start(bf16[704,2048]{1,0:T(8,128)(2,1)} %get-tuple-element.72.gate_ref) | copy-start | bytes 8650756
  80.0 7.0 %copy-start.2 = (bf16[704,1024]{1,0:T(8,128)(2,1)S(1)}, bf16[704,1024]{1,0:T(8,128)(2,1)}, u32[]{:S(2)}) copy-start(bf16[704,1024]{1,0:T(8,128)(2,1)} %get-tuple-element.54) | copy-start | bytes 4325380

commit v4 on v3

--- a/solution.py
+++ b/solution.py
@@ -370,7 +370,7 @@
 
 def forward_kernel(
     upper_ref, z_ref, dg_ref, off_ref, par_ref, xp_ref, dtw_ref, a_ref,
-    u_ref, ds_ref, dt_ref, sg_ref, dy_ref, gated_ref, gate_ref, proj_ref, wide_b, wide_c, bound_ref, skip_ref,
+    u_ref, ds_ref, dt_ref, sg_ref, dy_ref, gated_ref, gate_ref, proj_ref, wide_b, wide_c, kept_ref, end_ref, skip_ref,
     hs, ext, u16, dtm, dtu, ys, ybuf, *, width
 ):
     f32, bf16 = jnp.float32, jnp.bfloat16
@@ -383,8 +383,6 @@
         hs[...] = jnp.zeros_like(hs)
         skip_ref[...] = jnp.zeros_like(skip_ref)
         ext[pl.ds(0, 8), :] = jnp.zeros((8, inner), f32)
-
-    bound_ref[0] = hs[...]
 
     @pl.loop(0, tiles, unroll=True)
     def _(k):
@@ -438,6 +436,7 @@
                 bt = [wide_b[pl.ds((r0 + t) * 16 + 8 * s, 8), :] for s in range(2)]
                 ct = [wide_c[pl.ds((r0 + t) * 16 + 8 * s, 8), :] for s in range(2)]
                 for j in range(width):
+                    kept_ref[tile + j, pl.ds((r0 + t) * 16, 16), :] = jnp.concatenate(h[j], axis=0).astype(bf16)
                     for s in range(2):
                         h[j][s] = jnp.exp2(d[j] * rate[j][s]) * h[j][s] + x[j] * bt[s]
                     ybuf[j, pl.ds(t * 8, 8), :] = ct[0] * h[j][0] + ct[1] * h[j][1]
@@ -450,6 +449,7 @@
         for s in range(2):
             for j in range(width):
                 hs[pl.ds(8 * s, 8), pl.ds(base + 128 * j, 128)] = h[s * width + j]
+    end_ref[...] = hs[...]
 
     @pl.loop(0, tiles, unroll=True)
     def _(k):
@@ -483,7 +483,8 @@
             pl.BlockSpec((1, cols, chunk), lambda i: (i, 0, 0)),
             pl.BlockSpec((chunk * states, 128), lambda i: (i, 0)),
             pl.BlockSpec((chunk * states, 128), lambda i: (i, 0)),
-            pl.BlockSpec((1, states, DI), lambda i: (i, 0, 0)),
+            pl.BlockSpec((DI // 128, chunk * states, 128), lambda i: (0, i, 0)),
+            pl.BlockSpec((states, DI), lambda i: (0, 0)),
             pl.BlockSpec((8, DI), lambda i: (0, 0)),
         ],
         out_shape=[flat(f32)] * 5
@@ -492,7 +493,8 @@
             jax.ShapeDtypeStruct((n, cols, chunk), f32),
             jax.ShapeDtypeStruct((T * states, 128), f32),
             jax.ShapeDtypeStruct((T * states, 128), f32),
-            jax.ShapeDtypeStruct((n, states, DI), f32),
+            jax.ShapeDtypeStruct((DI // 128, T * states, 128), bf16),
+            jax.ShapeDtypeStruct((states, DI), f32),
             jax.ShapeDtypeStruct((8, DI), f32),
         ],
         scratch_shapes=[
@@ -510,7 +512,7 @@
 
 
 def backward_kernel(
-    u_ref, ds_ref, dt_ref, sg_ref, dy_ref, upper_ref, off_ref, proj_ref, wide_b, wide_c, bound_ref, par_ref, xp_ref, dtw_ref, a_ref, skip_ref,
+    u_ref, ds_ref, dt_ref, sg_ref, dy_ref, upper_ref, off_ref, proj_ref, wide_b, wide_c, kept_ref, end_ref, par_ref, xp_ref, dtw_ref, a_ref, skip_ref,
     *rest, width, plan, total
 ):
     f32, bf16 = jnp.float32, jnp.bfloat16
@@ -518,7 +520,7 @@
     given, rest = rest[:n], rest[n:]
     (du_ref, small_ref), out, rest = rest[:2], rest[2 : 2 + n], rest[2 + n :]
     ga_ref, gdt_ref, gx_ref, sum_ref, *rest = rest
-    ws, dtm, dtu, dyb, hbuf, sbuf, qbuf, dd, di, u16, dt16, ext, off_ext, wide_db, wide_dc, cols_ref = rest[:16]
+    ws, ns, dtm, dtu, dyb, sbuf, qbuf, dd, di, u16, dt16, ext, off_ext, wide_db, wide_dc, cols_ref = rest[:16]
     plan.bind(given, out, rest[16:])
     rows, inner = u_ref.shape
     states, rank = a_ref.shape[0], dtw_ref.shape[0]
@@ -530,6 +532,7 @@
     def _():
         for ref in (ws, ga_ref, gdt_ref, gx_ref, sum_ref):
             ref[...] = jnp.zeros_like(ref)
+        ns[...] = end_ref[...]
         ext[pl.ds(rows, 8), :] = jnp.zeros((8, inner), f32)
         off_ext[pl.ds(rows, 8), :] = jnp.full((8, 128), -1, jnp.int32)
         plan.barrier()
@@ -559,30 +562,11 @@
             u16[:, lanes] = act.astype(bf16)
         rate = [[a_ref[pl.ds(8 * s, 8), pl.ds(base + 128 * j, 128)] for s in range(2)] for j in range(width)]
 
-        def again(g, h):
-            h = [list(p) for p in zip(h[:width], h[width:])]
-            r0 = pl.multiple_of(g * 8, 8)
-            for t in range(8):
-                d = rows_of(dtm, 0, r0 + t, width)
-                x = rows_of(dtu, 0, r0 + t, width)
-                bt = [wide_b[pl.ds((r0 + t) * 16 + 8 * s, 8), :] for s in range(2)]
-                for j in range(width):
-                    for s in range(2):
-                        hbuf[pl.ds((r0 + t) * 16 + 8 * s, 8), pl.ds(128 * j, 128)] = h[j][s]
-                        h[j][s] = jnp.exp2(d[j] * rate[j][s]) * h[j][s] + x[j] * bt[s]
-            return tuple(p[0] for p in h) + tuple(p[1] for p in h)
-
-        h = tuple(bound_ref[0, pl.ds(8 * s, 8), pl.ds(base + 128 * j, 128)] for s in range(2) for j in range(width))
-        h = lax.fori_loop(0, rows // 8, again, h)
-        for s in range(2):
-            for j in range(width):
-                hbuf[pl.ds(rows * 16 + 8 * s, 8), pl.ds(128 * j, 128)] = h[s * width + j]
-
         def body(k, carry):
             r0 = pl.multiple_of((rows // 8 - 1 - k) * 8, 8)
             w = [[carry[s * width + j] for s in range(2)] for j in range(width)]
             ga = [[carry[2 * width + s * width + j] for s in range(2)] for j in range(width)]
-            newer = [[hbuf[pl.ds((r0 + 8) * 16 + 8 * s, 8), pl.ds(128 * j, 128)] for s in range(2)] for j in range(width)]
+            newer = [[carry[4 * width + s * width + j] for s in range(2)] for j in range(width)]
             for t in range(7, -1, -1):
                 d = rows_of(dtm, 0, r0 + t, width)
                 x = rows_of(dtu, 0, r0 + t, width)
@@ -593,9 +577,10 @@
                 dc = [None, None]
                 for j in range(width):
                     qs, ss = None, None
+                    both = kept_ref[tile + j, pl.ds((r0 + t) * 16, 16), :].astype(f32)
                     for s in range(2):
                         later = newer[j][s]
-                        prior = hbuf[pl.ds((r0 + t) * 16 + 8 * s, 8), pl.ds(128 * j, 128)]
+                        prior = both[8 * s : 8 * s + 8]
                         newer[j][s] = prior
                         g = ct[s] * v[j] + w[j][s]
                         w[j][s] = jnp.exp2(d[j] * rate[j][s]) * g
@@ -621,11 +606,9 @@
                 s8 = by_eights(sbuf, j)
                 dd[here, lanes] = LN2 * by_eights(qbuf, j) + u_ref[here, lanes] * s8
                 di[here, lanes] = dt_ref[here, lanes] * s8
-            return tuple(w[j][s] for s in range(2) for j in range(width)) + tuple(
-                ga[j][s] for s in range(2) for j in range(width)
-            )
-
-        held = [(r, pl.ds(8 * s, 8), pl.ds(base + 128 * j, 128)) for r in (ws, ga_ref) for s in range(2) for j in range(width)]
+            return tuple(v[j][s] for v in (w, ga, newer) for s in range(2) for j in range(width))
+
+        held = [(r, pl.ds(8 * s, 8), pl.ds(base + 128 * j, 128)) for r in (ws, ga_ref, ns) for s in range(2) for j in range(width)]
         end = lax.fori_loop(0, rows // 8, body, tuple(r[a, b] for r, a, b in held))
         for (r, a, b), value in zip(held, end):
             r[a, b] = value
@@ -690,7 +673,7 @@
         plan.gone(everything)
 
 
-def scan_backward(saved, both, offset, proj, wide_b, wide_c, bound, params, xp, dtw, rate, skip, chunk, width, grads, parts):
+def scan_backward(saved, both, offset, proj, wide_b, wide_c, kept, end, params, xp, dtw, rate, skip, chunk, width, grads, parts):
     T, DI = saved[0].shape
     n, states, cols, rank = T // chunk, rate.shape[0], xp.shape[0], dtw.shape[0]
     f32, bf16 = jnp.float32, jnp.bfloat16
@@ -713,7 +696,8 @@
             pl.BlockSpec((1, cols, chunk), lambda i: (n - 1 - i, 0, 0)),
             pl.BlockSpec((chunk * states, 128), lambda i: (n - 1 - i, 0)),
             pl.BlockSpec((chunk * states, 128), lambda i: (n - 1 - i, 0)),
-            pl.BlockSpec((1, states, DI), lambda i: (n - 1 - i, 0, 0)),
+            pl.BlockSpec((DI // 128, chunk * states, 128), lambda i: (0, n - 1 - i, 0)),
+            whole(end),
         ]
         + [whole(a) for a in (params, xp, dtw, rate, skip)]
         + [anywhere] * len(grads),
@@ -722,10 +706,10 @@
         scratch_shapes=[pltpu.VMEM((r, DI), f32) for r in (states, rank, cols, 48)]
         + [
             pltpu.VMEM((states, DI), f32),
+            pltpu.VMEM((states, DI), f32),
             pieces,
             pieces,
             pieces,
-            pltpu.VMEM((chunk * states + states, 128 * width), f32),
             eights,
             eights,
             pltpu.VMEM((chunk, DI), f32),
@@ -743,7 +727,7 @@
             dimension_semantics=("arbitrary",), collective_id=0, has_side_effects=True, vmem_limit_bytes=56 << 20
         ),
         name="scan_backward",
-    )(*saved, both, offset, proj, wide_b, wide_c, bound, params, xp, dtw, rate, skip, *shaped)
+    )(*saved, both, offset, proj, wide_b, wide_c, kept, end, params, xp, dtw, rate, skip, *shaped)
     return out[:2], [o.reshape(-1, o.shape[-1]) for o in out[2:]]
 
 
@@ -969,13 +953,13 @@
     )
     inner_dim = params.shape[1]
     parts = lax.axis_size("fsdp")
-    *saved, gated16, gate16, proj, b_wide, c_wide, boundary, skip_sums = scan_forward(
+    *saved, gated16, gate16, proj, b_wide, c_wide, kept, end, skip_sums = scan_forward(
         both, d_gated, offset, params, xp, w_dt, rate2, CHUNK, WIDTH
     )
     g_w_out = dot32(gated16, grad_rows, ((0,), (0,))).astype(bf16)
     g_w_gate = dot32(normed16, gate16, ((0,), (0,))).astype(bf16)
     (upper16, small), (t_out, t_gate) = scan_backward(
-        saved, both, offset, proj, b_wide, c_wide, boundary, params, xp, w_dt, rate2, skip_sums, CHUNK, WIDTH,
+        saved, both, offset, proj, b_wide, c_wide, kept, end, params, xp, w_dt, rate2, skip_sums, CHUNK, WIDTH,
         [g_w_out, g_w_gate], [thirds(model_dim), thirds(inner_dim)],
     )
     g_w_upper = dot32(normed16, upper16, ((0,), (0,))).astype(bf16)

time: 304 us -> 293 us (0.964)
  Pallas kernels: 279 us -> 269 us
    pallas_call x1, Pallas kernels: 127 us -> 114 us  [scan_backward(): pl.pallas_call(functools.partial(backward_kernel, width=width, plan=plan,...]
    pallas_call x1, Pallas kernels: 49.6 us -> 52.8 us  [scan_forward(): pl.pallas_call(functools.partial(forward_kernel, width=width), grid=(n,),...]
where the time goes in v4:
time: 293 us
  Pallas kernels  269 us (92%)
  matrix products  19.1 us (7%)
    pallas_call x1, Pallas kernels, scan_backward(): pl.pallas_call(functools.partial(backward_kernel, width=width, plan=plan,...  114 us
    pallas_call x1, Pallas kernels, finish(): pl.pallas_call(functools.partial(finish_kernel, plan=plan, gain_row=gain_...  65.5 us
    pallas_call x1, Pallas kernels, scan_forward(): pl.pallas_call(functools.partial(forward_kernel, width=width), grid=(n,),...  52.8 us
    pallas_call x1, Pallas kernels, gather_weights(): pl.pallas_call(functools.partial(gather_kernel, plan=plan), out_shape=[ja...  25.3 us
    dot_general x3, matrix products, dot32(): lax.dot_general(left, right, (contract, ((), ())), preferred_element_type...  19.1 us
    pallas_call x1, Pallas kernels, write_outputs(): pl.pallas_call(write_kernel, grid=(steps,), in_specs=[part(upper), part(g...  11.5 us

profile of v4, /device:TPU:0, one launch (start us, length us, event | category | flops | bytes accessed | tf_op | source)
XLA Modules:
  0.0 293.1 jit_solution(6471028904001247726)
XLA Ops:
  0.6 0.7 select_reduce_fusion.1
  1.4 0.7 fusion.1
  2.0 0.7 pad_bitcast_fusion
  2.7 0.1 select_reduce_fusion
  2.8 1.3 pad_maximum_fusion.vec_ref
  4.1 0.9 broadcast_in_dim.27.off_ref
  5.0 25.3 %gather_weights.1 = (bf16[704,1024]{1,0:T(8,128)(2,1)}, bf16[64,2048]{1,0:T(8,128)(2,1)}, bf16[96,2048]{1,0:T(8,128)(2,1)}, f32[16,2048]{1,0:T(8,128)}, f32[8,20...) custom-call(bf16[704,1024]{1,0:T(8,128)(2,1)} %bitcast.40, ...), custom_call_target="tpu_custom_call" | custom-call | tf_op jit(solution)/shard_map/gather_weights/pallas_call | solution.py:326
  30.4 0.0 copy-start
  30.4 52.8 %scan_forward.1 = (f32[704,2048]{1,0:T(8,128)}, f32[704,2048]{1,0:T(8,128)}, f32[704,2048]{1,0:T(8,128)}, f32[704,2048]{1,0:T(8,128)}, f32[704,2048]{1,0:T(8,128...) custom-call(f32[704,4096]{1,0:T(8,128)} %get-tuple-element.56.upper_, ...), custom_call_target="tpu_custom_call" | custom-call | tf_op jit(solution)/shard_map/scan_forward/pallas_call | solution.py:476
  83.2 0.0 copy-done
  83.2 0.0 copy-start.1
  83.2 0.0 copy-start.2
  83.2 7.0 %convolution_convert_fusion.2 = bf16[2048,1024]{1,0:T(8,128)(2,1)} fusion(bf16[704,2048]{1,0:T(8,128)(2,1)} %get-tuple-element.73.gated_ref, bf16[1,704,1024]{2,1,0:T(8,128)(2,1)S(1)} %copy-done), kind=kOutput, calls=%fused_computation.2 | convolution fusion | flops 2954887168 | bytes 8519680 | tf_op jit(solution)/shard_map/dot_general | solution.py:915
  90.2 0.0 copy-done.1
  90.2 0.0 copy-done.2
  90.2 5.0 %convolution_convert_fusion.1 = bf16[1024,2048]{1,0:T(8,128)(2,1)} fusion(bf16[704,1024]{1,0:T(8,128)(2,1)S(1)} %copy-done.2, bf16[704,2048]{1,0:T(8,128)(2,1)S(1)} %copy-done.1), kind=kOutput, calls=%fused_computation.1 | convolution fusion | flops 2954887168 | bytes 8519680 | tf_op jit(solution)/shard_map/dot_general | solution.py:915
  95.2 113.7 %scan_backward.1 = (bf16[704,2048]{1,0:T(8,128)(2,1)}, bf16[512,1024]{1,0:T(8,128)(2,1)}, bf16[16,64,1024]{2,1,0:T(8,128)(2,1)}, bf16[16,32,2048]{2,1,0:T(8,128)(2,1)}) custom-call(f32[704,2048]{1,0:T(8,128)} %get-tuple-element.62.u_ref, f32[704,2048]{1,0:T(8,128)} %get-tuple-element.63.ds_ref, f32[704,2048]{1,0:T(8,128)} %get-tuple-element.64.dt_ref, ...), custom_call_target="tpu_custom_call" | custom-call | tf_op jit(solution)/shard_map/scan_backward/pallas_call | solution.py:690
  208.9 7.0 %convolution_convert_fusion = bf16[1024,2048]{1,0:T(8,128)(2,1)} fusion(bf16[704,1024]{1,0:T(8,128)(2,1)S(1)} %copy-done.2, bf16[704,2048]{1,0:T(8,128)(2,1)} %get-tuple-element.75.upper_ref), kind=kOutput, calls=%fused_computation | convolution fusion | flops 2954887168 | bytes 8519680 | tf_op jit(solution)/shard_map/dot_general | solution.py:915
  216.0 65.5 %finish.1 = (bf16[16,32,2048]{2,1,0:T(8,128)(2,1)}, bf16[16,16,1024]{2,1,0:T(8,128)(2,1)}, bf16[704,1024]{1,0:T(8,128)(2,1)}, f32[704,1024]{1,0:T(8,128)}) custom-call(bf16[32,32,2048]{2,1,0:T(8,128)(2,1)} %bitcast.47, bf16[32,16,1024]{2,1,0:T(8,128)(2,1)} %bitcast.51, bf16[704,2048]{1,0:T(8,128)(2,1)} %get-tuple-element.75.upper_ref, ...), custom_call_target="tpu_custom_call" | custom-call | tf_op jit(solution)/shard_map/finish/pallas_call | solution.py:830
  281.4 11.5 %write_outputs.1 = (f32[512,4096]{1,0:T(8,128)}, f32[1024,1024]{1,0:T(8,128)}, f32[96,1024]{1,0:T(8,128)}, f32[64,1024]{1,0:T(8,128)}, f32[16,1024]{1,0:T(8,128)...) custom-call(bf16[512,2048]{1,0:T(8,128)(2,1)} %bitcast.50, ...), custom_call_target="tpu_custom_call" | custom-call | tf_op jit(solution)/shard_map/write_outputs/pallas_call | solution.py:890
  (1 shorter events, 0.0 us)
Async XLA Ops:
  30.4 52.8 %copy-start = (bf16[1,704,1024]{2,1,0:T(8,128)(2,1)S(1)}, bf16[1,704,1024]{2,1,0:T(8,128)(2,1)}, u32[]{:S(2)}) copy-start(bf16[1,704,1024]{2,1,0:T(8,128)(2,1)} %param.25) | copy-start | bytes 4325380
  83.2 7.0 %copy-start.1 = (bf16[704,2048]{1,0:T(8,128)(2,1)S(1)}, bf16[704,2048]{1,0:T(8,128)(2,1)}, u32[]{:S(2)}) copy-start(bf16[704,2048]{1,0:T(8,128)(2,1)} %get-tuple-element.74.gate_ref) | copy-start | bytes 8650756
  83.2 7.0 %copy-start.2 = (bf16[704,1024]{1,0:T(8,128)(2,1)S(1)}, bf16[704,1024]{1,0:T(8,128)(2,1)}, u32[]{:S(2)}) copy-start(bf16[704,1024]{1,0:T(8,128)(2,1)} %get-tuple-element.55) | copy-start | bytes 4325380

commit v5 on v4

--- a/solution.py
+++ b/solution.py
@@ -732,27 +732,40 @@
 
 
 def finish_kernel(
-    grads_ref, small_ref, upper_ref, gate_ref, gated_ref, in_ref, wout_ref, x_ref, go_ref, gain_ref,
-    total_ref, few_ref, layer_ref, left_ref,
-    upper, gate, gated, win, wout, x, go, dn, layer, mine, gain_sum, loads, away, *rest, plan, gain_row
+    small_ref, normed_ref, upper_ref, gate_ref, gated_ref, in_ref, wout_ref, x_ref, go_ref, gain_ref,
+    total_ref, few_ref, layer_ref, left_ref, gain_out,
+    normed, upper, gate, gated, win, wout, x, go, dn, layer, grads, gain_sum, gain_in, loads, away, gain_send, gain_recv,
+    *rest, plan
 ):
     f32, bf16 = jnp.float32, jnp.bfloat16
     rows, model = x.shape
     inner = upper.shape[1]
-    plan.bind([grads_ref, mine], [total_ref, few_ref], rest)
-    main = [p for p in range(len(plan.pieces)) if plan.pieces[p][0] == 0]
-    late = [p for p in range(len(plan.pieces)) if plan.pieces[p][0] == 1]
+    plan.bind([grads, small_ref], [total_ref, few_ref], rest)
+    everything = range(len(plan.pieces))
+    few = [p for p in everything if plan.pieces[p][0] == 1]
+    main = [p for p in everything if plan.pieces[p][0] == 0]
+    halves = [main[: len(main) // 2], main[len(main) // 2 :]]
 
     copies = [
         pltpu.make_async_copy(a, b, loads.at[i])
         for i, (a, b) in enumerate(
             (
-                (upper_ref, upper), (in_ref.at[:, pl.ds(0, inner)], win.at[0]), (gate_ref, gate),
-                (in_ref.at[:, pl.ds(inner, inner)], win.at[1]), (x_ref, x), (go_ref, go), (small_ref, mine),
-                (gated_ref, gated), (wout_ref, wout),
+                (normed_ref, normed), (upper_ref, upper), (in_ref.at[:, pl.ds(0, inner)], win.at[0]), (gate_ref, gate),
+                (in_ref.at[:, pl.ds(inner, inner)], win.at[1]), (x_ref, x), (go_ref, go), (gated_ref, gated), (wout_ref, wout),
             )
         )
     ]
+
+    def gradient(half):
+        columns = pl.ds(half * (inner // 2), inner // 2)
+        deep = grads.shape[1]
+
+        @pl.loop(0, model // 256)
+        def _(k):
+            part = normed[:, pl.ds(pl.multiple_of(k * 256, 256), 256)]
+            new = lax.dot_general(part, upper[:, columns], (((0,), (0,)), ((), ())), preferred_element_type=f32).astype(bf16)
+            for b in range(256 // deep):
+                grads[k * (256 // deep) + b, :, columns] = new[b * deep : (b + 1) * deep]
 
     def product(left, k):
         @pl.loop(0, model // 256)
@@ -761,20 +774,47 @@
             new = lax.dot_general(left[...], win[k, here, :], (((1,), (1,)), ((), ())), preferred_element_type=f32)
             dn[:, here] = new if k == 0 else dn[:, here] + new
 
-    plan.barrier()
-    plan.start(main)
+    def gain_copy(stage):
+        axis, bit = ("fsdp", stage) if stage < plan.outer_bits else ("dp", stage - plan.outer_bits)
+        return pltpu.make_async_remote_copy(
+            src_ref=gain_sum.at[stage],
+            dst_ref=gain_in.at[stage],
+            send_sem=gain_send.at[stage],
+            recv_sem=gain_recv.at[stage],
+            device_id=plan.partner(axis, bit),
+            device_id_type=pl.DeviceIdType.MESH,
+        )
+
+    def gain_step(stage):
+        gain_copy(stage).wait()
+        gain_sum[stage + 1] = gain_sum[stage] + gain_in[stage]
+        if stage + 1 < plan.stages:
+            gain_copy(stage + 1).start()
+
     for c in copies:
         c.start()
+    plan.barrier()
+    plan.start(few)
     copies[0].wait()
     copies[1].wait()
+    gradient(0)
+    plan.start(halves[0])
+    gradient(1)
+    plan.start(halves[1])
+    copies[2].wait()
+    plan.advance(halves[0], 0)
+    plan.advance(few, 0)
     product(upper, 0)
-    plan.advance(main, 0)
-    copies[2].wait()
+    plan.advance(halves[1], 0)
     copies[3].wait()
+    copies[4].wait()
     product(gate, 1)
-    copies[4].wait()
     copies[5].wait()
-    gain_sum[...] = jnp.zeros_like(gain_sum)
+    copies[6].wait()
+    plan.advance(halves[0], 1)
+    plan.advance(halves[1], 1)
+    plan.advance(few, 1)
+    gain_sum[0] = jnp.zeros(gain_sum.shape[1:], f32)
 
     @pl.loop(0, rows // 32)
     def _(k):
@@ -782,25 +822,14 @@
         value, grad, gain = x[here, :].astype(f32), dn[here, :], gain_ref[0:1, :]
         scale = lax.rsqrt(jnp.mean(value * value, axis=-1, keepdims=True) + norm_eps)
         through = grad * value
-        gain_sum[...] = gain_sum[...] + folded(through * scale)
+        gain_sum[0] = gain_sum[0] + folded(through * scale)
         pull = jnp.mean(through * gain, axis=-1, keepdims=True) * (scale * scale * scale)
         dn[here, :] = go[here, :].astype(f32) + scale * (grad * gain) - value * pull
 
+    gain_copy(0).start()
     leaving = [pltpu.make_async_copy(dn, left_ref, away.at[0]), pltpu.make_async_copy(layer, layer_ref, away.at[1])]
     leaving[0].start()
-    copies[6].wait()
-    gain_grad = jnp.sum(gain_sum[...], axis=0, keepdims=True)
-    outer = plan.blocks // plan.inner
-    deep, r = model // outer, mine.shape[1]
-    for f in range(outer):
-        block = f * plan.inner + gain_row // r
-        old = mine[block, :, 0:deep].astype(f32)
-        new = jnp.broadcast_to(gain_grad[:, f * deep : (f + 1) * deep], (r, deep))
-        chosen = lax.broadcasted_iota(jnp.int32, (r, deep), 0) == gain_row % r
-        mine[block, :, 0:deep] = jnp.where(chosen, new, old).astype(bf16)
-    plan.start(late)
-    plan.advance(main, 1)
-    plan.advance(late, 0)
+    plan.advance(everything, 2)
     copies[7].wait()
     copies[8].wait()
 
@@ -811,28 +840,46 @@
         layer[:, here] = new.astype(bf16)
 
     leaving[1].start()
-    for step in range(2, plan.steps):
-        plan.advance(main, step)
-        plan.advance(late, step - 1)
-    plan.advance(late, plan.steps - 1)
-    plan.gone(main + late)
+    stage = 0
+    for step in range(3, plan.steps):
+        plan.advance(everything, step)
+        if stage < plan.stages:
+            gain_step(stage)
+            stage += 1
+    while stage < plan.stages:
+        gain_step(stage)
+        stage += 1
+    deep = gain_out.shape[1]
+    own = pl.ds(pl.multiple_of(lax.axis_index("fsdp") * deep, 128), deep)
+    gain_out[...] = jnp.broadcast_to(jnp.sum(gain_sum[plan.stages, :, own], axis=0, keepdims=True), gain_out.shape)
+    plan.gone(everything)
     for c in leaving:
         c.wait()
 
 
-def finish(grads, small, upper16, gate16, gated16, w_in, w_out, x, go, gain, parts, gain_row):
+def finish(small, normed16, upper16, gate16, gated16, w_in, w_out, x, go, gain, parts):
     f32, bf16 = jnp.float32, jnp.bfloat16
     (rows, model), inner = x.shape, upper16.shape[1]
-    plan, shaped, summed = reduction_of([grads, small], parts)
+    grads = jax.ShapeDtypeStruct((model, inner), bf16)
+    outer = lax.axis_size("fsdp")
+    plan = Reduction(outer, lax.axis_size("dp"), [grads.shape, small.shape], parts)
+    summed = [jax.ShapeDtypeStruct((plan.inner,) + s[1:], bf16) for s in plan.shapes]
     anywhere = pl.BlockSpec(memory_space=pl.ANY)
+    near = pl.BlockSpec(memory_space=pltpu.VMEM)
     flat = pltpu.VMEM((rows, inner), bf16)
     thin = pltpu.VMEM((rows, model), bf16)
-    total, few, layer_out, input_grad = pl.pallas_call(
-        functools.partial(finish_kernel, plan=plan, gain_row=gain_row),
-        out_shape=summed + [jax.ShapeDtypeStruct((rows, model), bf16), jax.ShapeDtypeStruct((rows, model), f32)],
-        in_specs=[anywhere] * 9 + [pl.BlockSpec(memory_space=pltpu.VMEM)],
-        out_specs=[anywhere] * 4,
+    total, few, layer_out, input_grad, gain_total = pl.pallas_call(
+        functools.partial(finish_kernel, plan=plan),
+        out_shape=summed
+        + [
+            jax.ShapeDtypeStruct((rows, model), bf16),
+            jax.ShapeDtypeStruct((rows, model), f32),
+            jax.ShapeDtypeStruct((8, model // outer), f32),
+        ],
+        in_specs=[anywhere] * 9 + [near],
+        out_specs=[anywhere] * 4 + [near],
         scratch_shapes=[
+            thin,
             flat,
             flat,
             flat,
@@ -842,20 +889,23 @@
             thin,
             pltpu.VMEM((rows, model), f32),
             thin,
-            pltpu.VMEM(plan.shapes[1], bf16),
-            pltpu.VMEM((8, model), f32),
+            pltpu.VMEM(plan.shapes[0], bf16),
+            pltpu.VMEM((plan.stages + 1, 8, model), f32),
+            pltpu.VMEM((plan.stages, 8, model), f32),
             pltpu.SemaphoreType.DMA((9,)),
             pltpu.SemaphoreType.DMA((2,)),
+            pltpu.SemaphoreType.DMA((plan.stages,)),
+            pltpu.SemaphoreType.DMA((plan.stages,)),
         ]
         + plan.scratch(),
-        compiler_params=pltpu.CompilerParams(collective_id=1, has_side_effects=True, vmem_limit_bytes=56 << 20),
+        compiler_params=pltpu.CompilerParams(collective_id=1, has_side_effects=True, vmem_limit_bytes=60 << 20),
         name="finish",
-    )(*shaped, upper16, gate16, gated16, w_in, w_out, x, go, gain)
-    return total.reshape(-1, total.shape[-1]), few.reshape(-1, few.shape[-1]), layer_out, input_grad
+    )(small.reshape(plan.shapes[1]), normed16, upper16, gate16, gated16, w_in, w_out, x, go, gain)
+    return total.reshape(-1, total.shape[-1]), few.reshape(-1, few.shape[-1]), layer_out, input_grad, gain_total
 
 
 def write_kernel(
-    upper_ref, gate_ref, out_ref, small_ref, layer_ref, left_ref,
+    upper_ref, gate_ref, out_ref, small_ref, layer_ref, left_ref, gain_ref,
     in_to, out_to, x_to, dt_to, rate_to, taps_to, shift_to, bias_to, skip_to, gain_to, layer_to, left_to,
 ):
     f32 = jnp.float32
@@ -874,12 +924,13 @@
             at += ref.shape[0]
         few = small_ref[at : at + 16, :].astype(f32)
         at = 0
-        for ref in (taps_to, shift_to, bias_to, skip_to, gain_to):
+        gain_to[...] = gain_ref[0:1, :]
+        for ref in (taps_to, shift_to, bias_to, skip_to):
             ref[...] = few[at : at + ref.shape[0], : ref.shape[1]]
             at += ref.shape[0]
 
 
-def write_outputs(upper, gate, out, small, layer, left, sizes):
+def write_outputs(upper, gate, out, small, layer, left, gain, sizes):
     f32, share, steps = jnp.float32, small.shape[1], 4
     few = [(r, share) for r in sizes[:-1]] + [(1, sizes[-1])]
     part = lambda a: pl.BlockSpec((a.shape[0] // steps, a.shape[1]), lambda i: (i, 0))
@@ -890,12 +941,12 @@
     return pl.pallas_call(
         write_kernel,
         grid=(steps,),
-        in_specs=[part(upper), part(gate), part(out), whole(small), part(layer), part(left)],
+        in_specs=[part(upper), part(gate), part(out), whole(small), part(layer), part(left), whole(gain)],
         out_specs=[part(a) for a in big] + [whole(a) for a in few] + [part(a) for a in last],
         out_shape=big + few + last,
         compiler_params=pltpu.CompilerParams(dimension_semantics=("arbitrary",), vmem_limit_bytes=62 << 20),
         name="write_outputs",
-    )(upper, gate, out, small, layer, left)
+    )(upper, gate, out, small, layer, left, gain)
 
 
 def cluster_offsets(lengths, total_len):
@@ -962,14 +1013,12 @@
         saved, both, offset, proj, b_wide, c_wide, kept, end, params, xp, w_dt, rate2, skip_sums, CHUNK, WIDTH,
         [g_w_out, g_w_gate], [thirds(model_dim), thirds(inner_dim)],
     )
-    g_w_upper = dot32(normed16, upper16, ((0,), (0,))).astype(bf16)
-    gain_row = columns + rank_dim + state_dim + taps + 3
-    t_upper, t_small, layer_out, input_grad = finish(
-        g_w_upper, small, upper16, gate16, gated16, w_in, w_out, x, grad_rows,
-        gain, [thirds(inner_dim, 2), [(inner_dim // parts, ORDERS[2])]], gain_row,
+    t_upper, t_small, layer_out, input_grad, t_gain = finish(
+        small, normed16, upper16, gate16, gated16, w_in, w_out, x, grad_rows, gain,
+        [thirds(inner_dim, 2), [(inner_dim // parts, ORDERS[2])]],
     )
     t_in, t_out, t_x, t_dt, t_alog, t_conv, t_b_conv, t_b_dt, t_skip, t_gain, layer_out, input_grad = write_outputs(
-        t_upper, t_gate, t_out, t_small, layer_out, input_grad,
+        t_upper, t_gate, t_out, t_small, layer_out, input_grad, t_gain,
         (columns, rank_dim, state_dim, taps, 1, 1, 1, model_dim // parts),
     )
     return (

time: 293 us -> 286 us (0.976)
  matrix products: 19.1 us -> 12 us
    dot_general x3 -> x2, matrix products: 19.1 us -> 12 us  [dot32(): lax.dot_general(left, right, (contract, ((), ())), preferred_element_type...]
where the time goes in v5:
time: 286 us; the launch traced here: 285 us
  Pallas kernels  268 us (94%)
  matrix products  12 us (4%)
    pallas_call x1, Pallas kernels, scan_backward(): pl.pallas_call(functools.partial(backward_kernel, width=width, plan=plan,...  114 us
    pallas_call x1, Pallas kernels, finish(): pl.pallas_call(functools.partial(finish_kernel, plan=plan), out_shape=sum...  64.4 us
    pallas_call x1, Pallas kernels, scan_forward(): pl.pallas_call(functools.partial(forward_kernel, width=width), grid=(n,),...  52.8 us
    pallas_call x1, Pallas kernels, gather_weights(): pl.pallas_call(functools.partial(gather_kernel, plan=plan), out_shape=[ja...  25.4 us
    dot_general x2, matrix products, dot32(): lax.dot_general(left, right, (contract, ((), ())), preferred_element_type...  12 us
    pallas_call x1, Pallas kernels, write_outputs(): pl.pallas_call(write_kernel, grid=(steps,), in_specs=[part(upper), part(g...  11.7 us

profile of v5, /device:TPU:0, one launch (start us, length us, event | category | flops | bytes accessed | tf_op | source)
XLA Modules:
  0.0 285.3 jit_solution(4141776200160756240)
XLA Ops:
  0.6 0.7 select_reduce_fusion.1
  1.4 0.7 fusion.1
  2.0 0.7 pad_bitcast_fusion
  2.7 0.1 select_reduce_fusion
  2.8 1.3 pad_maximum_fusion.vec_ref
  4.1 0.9 broadcast_in_dim.27.off_ref
  5.0 25.4 %gather_weights.1 = (bf16[704,1024]{1,0:T(8,128)(2,1)}, bf16[64,2048]{1,0:T(8,128)(2,1)}, bf16[96,2048]{1,0:T(8,128)(2,1)}, f32[16,2048]{1,0:T(8,128)}, f32[8,20...) custom-call(bf16[704,1024]{1,0:T(8,128)(2,1)} %bitcast.37, ...), custom_call_target="tpu_custom_call" | custom-call | tf_op jit(solution)/shard_map/gather_weights/pallas_call | solution.py:326
  30.4 0.0 copy-start
  30.4 52.8 %scan_forward.1 = (f32[704,2048]{1,0:T(8,128)}, f32[704,2048]{1,0:T(8,128)}, f32[704,2048]{1,0:T(8,128)}, f32[704,2048]{1,0:T(8,128)}, f32[704,2048]{1,0:T(8,128...) custom-call(f32[704,4096]{1,0:T(8,128)} %get-tuple-element.56.upper_, ...), custom_call_target="tpu_custom_call" | custom-call | tf_op jit(solution)/shard_map/scan_forward/pallas_call | solution.py:476
  83.2 0.0 copy-done
  83.2 0.0 copy-start.1
  83.2 0.0 copy-start.2
  83.2 7.0 %convolution_convert_fusion.1 = bf16[2048,1024]{1,0:T(8,128)(2,1)} fusion(bf16[704,2048]{1,0:T(8,128)(2,1)} %get-tuple-element.73.gated_ref, bf16[1,704,1024]{2,1,0:T(8,128)(2,1)S(1)} %copy-done), kind=kOutput, calls=%fused_computation.1 | convolution fusion | flops 2954887168 | bytes 8519680 | tf_op jit(solution)/shard_map/dot_general | solution.py:966
  90.2 0.0 copy-done.1
  90.2 0.0 copy-done.2
  90.2 5.0 %convolution_convert_fusion = bf16[1024,2048]{1,0:T(8,128)(2,1)} fusion(bf16[704,1024]{1,0:T(8,128)(2,1)S(1)} %copy-done.2, bf16[704,2048]{1,0:T(8,128)(2,1)S(1)} %copy-done.1), kind=kOutput, calls=%fused_computation | convolution fusion | flops 2954887168 | bytes 8519680 | tf_op jit(solution)/shard_map/dot_general | solution.py:966
  95.3 113.7 %scan_backward.1 = (bf16[704,2048]{1,0:T(8,128)(2,1)}, bf16[512,1024]{1,0:T(8,128)(2,1)}, bf16[16,64,1024]{2,1,0:T(8,128)(2,1)}, bf16[16,32,2048]{2,1,0:T(8,128)(2,1)}) custom-call(f32[704,2048]{1,0:T(8,128)} %get-tuple-element.62.u_ref, f32[704,2048]{1,0:T(8,128)} %get-tuple-element.63.ds_ref, f32[704,2048]{1,0:T(8,128)} %get-tuple-element.64.dt_ref, ...), custom_call_target="tpu_custom_call" | custom-call | tf_op jit(solution)/shard_map/scan_backward/pallas_call | solution.py:690
  209.0 64.4 %finish.1 = (bf16[16,32,2048]{2,1,0:T(8,128)(2,1)}, bf16[16,16,1024]{2,1,0:T(8,128)(2,1)}, bf16[704,1024]{1,0:T(8,128)(2,1)}, f32[704,1024]{1,0:T(8,128)}, f32[8,512]{1,0:T(8,128)}) custom-call(bf16[32,16,1024]{2,1,0:T(8,128)(2,1)} %bitcast.47, bf16[704,1024]{1,0:T(8,128)(2,1)} %get-tuple-element.74.normed_ref, ...), custom_call_target="tpu_custom_call" | custom-call | tf_op jit(solution)/shard_map/finish/pallas_call | solution.py:871
  273.4 11.7 %write_outputs.1 = (f32[512,4096]{1,0:T(8,128)}, f32[1024,1024]{1,0:T(8,128)}, f32[96,1024]{1,0:T(8,128)}, f32[64,1024]{1,0:T(8,128)}, f32[16,1024]{1,0:T(8,128)...) custom-call(bf16[512,2048]{1,0:T(8,128)(2,1)} %bitcast.46, ...), custom_call_target="tpu_custom_call" | custom-call | tf_op jit(solution)/shard_map/write_outputs/pallas_call | solution.py:941
  (1 shorter events, 0.0 us)
Async XLA Ops:
  30.4 52.8 %copy-start = (bf16[1,704,1024]{2,1,0:T(8,128)(2,1)S(1)}, bf16[1,704,1024]{2,1,0:T(8,128)(2,1)}, u32[]{:S(2)}) copy-start(bf16[1,704,1024]{2,1,0:T(8,128)(2,1)} %param.25) | copy-start | bytes 4325380
  83.2 7.0 %copy-start.1 = (bf16[704,2048]{1,0:T(8,128)(2,1)S(1)}, bf16[704,2048]{1,0:T(8,128)(2,1)}, u32[]{:S(2)}) copy-start(bf16[704,2048]{1,0:T(8,128)(2,1)} %get-tuple-element.75.gate_ref) | copy-start | bytes 8650756
  83.2 7.0 %copy-start.2 = (bf16[704,1024]{1,0:T(8,128)(2,1)S(1)}, bf16[704,1024]{1,0:T(8,128)(2,1)}, u32[]{:S(2)}) copy-start(bf16[704,1024]{1,0:T(8,128)(2,1)} %get-tuple-element.74.normed_ref) | copy-start | bytes 4325380

commit v6 on v5

--- a/solution.py
+++ b/solution.py
@@ -371,7 +371,7 @@
 def forward_kernel(
     upper_ref, z_ref, dg_ref, off_ref, par_ref, xp_ref, dtw_ref, a_ref,
     u_ref, ds_ref, dt_ref, sg_ref, dy_ref, gated_ref, gate_ref, proj_ref, wide_b, wide_c, kept_ref, end_ref, skip_ref,
-    hs, ext, u16, dtm, dtu, ys, ybuf, *, width
+    hs, ext, u16, dtm, dtu, ys, mix, *, width
 ):
     f32, bf16 = jnp.float32, jnp.bfloat16
     rows, inner = upper_ref.shape
@@ -405,6 +405,14 @@
     spread(proj, rank, wide_b, states)
     spread(proj, rank + states, wide_c, states)
     rank16 = proj[:rank].astype(bf16)
+    column = lax.broadcasted_iota(jnp.int32, (states, 8 * states), 1) % states
+    tiled = jnp.where(column == lax.broadcasted_iota(jnp.int32, (states, 8 * states), 0), 1.0, 0.0).astype(bf16)
+    many = lax.dot_general(
+        proj[rank + states :].astype(bf16), tiled, (((0,), (0,)), ((), ())), preferred_element_type=f32
+    )
+    token = lax.broadcasted_iota(jnp.int32, (rows, 8 * states), 0) % 8
+    mine = lax.broadcasted_iota(jnp.int32, (rows, 8 * states), 1) // states == token
+    mix[...] = jnp.where(mine, many, 0.0)
 
     @pl.loop(0, tiles // 2, unroll=True)
     def _(k):
@@ -430,22 +438,28 @@
         def body(g, h):
             h = [list(p) for p in zip(h[:width], h[width:])]
             r0 = pl.multiple_of(g * 8, 8)
+            low = [jnp.concatenate(h[j], axis=0).astype(bf16) for j in range(width)]
+            seen = [[] for _ in range(width)]
             for t in range(8):
                 d = rows_of(dtm, tile, r0 + t, width)
                 x = rows_of(dtu, tile, r0 + t, width)
                 bt = [wide_b[pl.ds((r0 + t) * 16 + 8 * s, 8), :] for s in range(2)]
-                ct = [wide_c[pl.ds((r0 + t) * 16 + 8 * s, 8), :] for s in range(2)]
                 for j in range(width):
-                    kept_ref[tile + j, pl.ds((r0 + t) * 16, 16), :] = jnp.concatenate(h[j], axis=0).astype(bf16)
+                    kept_ref[tile + j, pl.ds((r0 + t) * 16, 16), :] = low[j]
                     for s in range(2):
                         h[j][s] = jnp.exp2(d[j] * rate[j][s]) * h[j][s] + x[j] * bt[s]
-                    ybuf[j, pl.ds(t * 8, 8), :] = ct[0] * h[j][0] + ct[1] * h[j][1]
-            for j in range(width):
-                ys[tile + j, pl.ds(r0, 8), :] = by_eights(ybuf, j)
+                    low[j] = jnp.concatenate(h[j], axis=0).astype(bf16)
+                    seen[j].append(low[j])
+            left = mix[pl.ds(r0, 8), :].astype(bf16)
+            for j in range(0, width, 2):
+                right = jnp.concatenate([jnp.concatenate(seen[j + k], axis=0) for k in range(2)], axis=1)
+                part = jnp.dot(left, right, preferred_element_type=f32)
+                for k in range(2):
+                    ys[tile + j + k, pl.ds(r0, 8), :] = part[:, 128 * k : 128 * k + 128]
             return tuple(p[0] for p in h) + tuple(p[1] for p in h)
 
         h = tuple(hs[pl.ds(8 * s, 8), pl.ds(base + 128 * j, 128)] for s in range(2) for j in range(width))
-        h = lax.fori_loop(0, rows // 8, body, h, unroll=4)
+        h = lax.fori_loop(0, rows // 8, body, h, unroll=8)
         for s in range(2):
             for j in range(width):
                 hs[pl.ds(8 * s, 8), pl.ds(base + 128 * j, 128)] = h[s * width + j]
@@ -504,7 +518,7 @@
             tile(f32),
             tile(f32),
             tile(f32),
-            pltpu.VMEM((width, 64, 128), f32),
+            pltpu.VMEM((chunk, 8 * states), f32),
         ],
         compiler_params=pltpu.CompilerParams(dimension_semantics=("arbitrary",), vmem_limit_bytes=62 << 20),
         name="scan_forward",
@@ -767,8 +781,8 @@
             for b in range(256 // deep):
                 grads[k * (256 // deep) + b, :, columns] = new[b * deep : (b + 1) * deep]
 
-    def product(left, k):
-        @pl.loop(0, model // 256)
+    def product(left, k, start=0, stop=model // 256):
+        @pl.loop(start, stop)
         def _(j):
             here = pl.ds(pl.multiple_of(j * 256, 256), 256)
             new = lax.dot_general(left[...], win[k, here, :], (((1,), (1,)), ((), ())), preferred_element_type=f32)
@@ -804,8 +818,9 @@
     copies[2].wait()
     plan.advance(halves[0], 0)
     plan.advance(few, 0)
-    product(upper, 0)
+    product(upper, 0, 0, model // 512)
     plan.advance(halves[1], 0)
+    product(upper, 0, model // 512, model // 256)
     copies[3].wait()
     copies[4].wait()
     product(gate, 1)

time: 286 us -> 281 us (0.983)
  Pallas kernels: 268 us -> 263 us
    pallas_call x1, Pallas kernels: 52.8 us -> 47.7 us  [scan_forward(): pl.pallas_call(functools.partial(forward_kernel, width=width), grid=(n,),...]
where the time goes in v6:
time: 281 us; the launch traced here: 280 us
  Pallas kernels  263 us (94%)
  matrix products  12.1 us (4%)
    pallas_call x1, Pallas kernels, scan_backward(): pl.pallas_call(functools.partial(backward_kernel, width=width, plan=plan,...  114 us
    pallas_call x1, Pallas kernels, finish(): pl.pallas_call(functools.partial(finish_kernel, plan=plan), out_shape=sum...  64.3 us
    pallas_call x1, Pallas kernels, scan_forward(): pl.pallas_call(functools.partial(forward_kernel, width=width), grid=(n,),...  47.7 us
    pallas_call x1, Pallas kernels, gather_weights(): pl.pallas_call(functools.partial(gather_kernel, plan=plan), out_shape=[ja...  25.4 us
    dot_general x2, matrix products, dot32(): lax.dot_general(left, right, (contract, ((), ())), preferred_element_type...  12.1 us
    pallas_call x1, Pallas kernels, write_outputs(): pl.pallas_call(write_kernel, grid=(steps,), in_specs=[part(upper), part(g...  11.7 us

profile of v6, /device:TPU:0, one launch (start us, length us, event | category | flops | bytes accessed | tf_op | source)
XLA Modules:
  0.0 280.2 jit_solution(9692382860409509850)
XLA Ops:
  0.6 0.7 select_reduce_fusion.1
  1.4 0.7 fusion.1
  2.0 0.7 pad_bitcast_fusion
  2.7 0.1 select_reduce_fusion
  2.8 1.3 pad_maximum_fusion.vec_ref
  4.1 0.9 broadcast_in_dim.27.off_ref
  5.0 25.4 %gather_weights.1 = (bf16[704,1024]{1,0:T(8,128)(2,1)}, bf16[64,2048]{1,0:T(8,128)(2,1)}, bf16[96,2048]{1,0:T(8,128)(2,1)}, f32[16,2048]{1,0:T(8,128)}, f32[8,20...) custom-call(bf16[704,1024]{1,0:T(8,128)(2,1)} %bitcast.37, ...), custom_call_target="tpu_custom_call" | custom-call | tf_op jit(solution)/shard_map/gather_weights/pallas_call | solution.py:326
  30.4 0.0 copy-start
  30.4 47.7 %scan_forward.1 = (f32[704,2048]{1,0:T(8,128)}, f32[704,2048]{1,0:T(8,128)}, f32[704,2048]{1,0:T(8,128)}, f32[704,2048]{1,0:T(8,128)}, f32[704,2048]{1,0:T(8,128...) custom-call(f32[704,4096]{1,0:T(8,128)} %get-tuple-element.56.upper_, ...), custom_call_target="tpu_custom_call" | custom-call | tf_op jit(solution)/shard_map/scan_forward/pallas_call | solution.py:490
  78.2 0.0 copy-done
  78.2 0.0 copy-start.1
  78.2 0.0 copy-start.2
  78.2 7.0 %convolution_convert_fusion.1 = bf16[2048,1024]{1,0:T(8,128)(2,1)} fusion(bf16[704,2048]{1,0:T(8,128)(2,1)} %get-tuple-element.73.gated_ref, bf16[1,704,1024]{2,1,0:T(8,128)(2,1)S(1)} %copy-done), kind=kOutput, calls=%fused_computation.1 | convolution fusion | flops 2954887168 | bytes 8519680 | tf_op jit(solution)/shard_map/dot_general | solution.py:981
  85.2 0.0 copy-done.1
  85.2 0.0 copy-done.2
  85.2 5.0 %convolution_convert_fusion = bf16[1024,2048]{1,0:T(8,128)(2,1)} fusion(bf16[704,1024]{1,0:T(8,128)(2,1)S(1)} %copy-done.2, bf16[704,2048]{1,0:T(8,128)(2,1)S(1)} %copy-done.1), kind=kOutput, calls=%fused_computation | convolution fusion | flops 2954887168 | bytes 8519680 | tf_op jit(solution)/shard_map/dot_general | solution.py:981
  90.3 113.8 %scan_backward.1 = (bf16[704,2048]{1,0:T(8,128)(2,1)}, bf16[512,1024]{1,0:T(8,128)(2,1)}, bf16[16,64,1024]{2,1,0:T(8,128)(2,1)}, bf16[16,32,2048]{2,1,0:T(8,128)(2,1)}) custom-call(f32[704,2048]{1,0:T(8,128)} %get-tuple-element.62.u_ref, f32[704,2048]{1,0:T(8,128)} %get-tuple-element.63.ds_ref, f32[704,2048]{1,0:T(8,128)} %get-tuple-element.64.dt_ref, ...), custom_call_target="tpu_custom_call" | custom-call | tf_op jit(solution)/shard_map/scan_backward/pallas_call | solution.py:704
  204.0 64.3 %finish.1 = (bf16[16,32,2048]{2,1,0:T(8,128)(2,1)}, bf16[16,16,1024]{2,1,0:T(8,128)(2,1)}, bf16[704,1024]{1,0:T(8,128)(2,1)}, f32[704,1024]{1,0:T(8,128)}, f32[8,512]{1,0:T(8,128)}) custom-call(bf16[32,16,1024]{2,1,0:T(8,128)(2,1)} %bitcast.47, bf16[704,1024]{1,0:T(8,128)(2,1)} %get-tuple-element.74.normed_ref, ...), custom_call_target="tpu_custom_call" | custom-call | tf_op jit(solution)/shard_map/finish/pallas_call | solution.py:886
  268.4 11.7 %write_outputs.1 = (f32[512,4096]{1,0:T(8,128)}, f32[1024,1024]{1,0:T(8,128)}, f32[96,1024]{1,0:T(8,128)}, f32[64,1024]{1,0:T(8,128)}, f32[16,1024]{1,0:T(8,128)...) custom-call(bf16[512,2048]{1,0:T(8,128)(2,1)} %bitcast.46, ...), custom_call_target="tpu_custom_call" | custom-call | tf_op jit(solution)/shard_map/write_outputs/pallas_call | solution.py:956
  (1 shorter events, 0.0 us)
Async XLA Ops:
  30.4 47.8 %copy-start = (bf16[1,704,1024]{2,1,0:T(8,128)(2,1)S(1)}, bf16[1,704,1024]{2,1,0:T(8,128)(2,1)}, u32[]{:S(2)}) copy-start(bf16[1,704,1024]{2,1,0:T(8,128)(2,1)} %param.25) | copy-start | bytes 4325380
  78.2 7.0 %copy-start.1 = (bf16[704,2048]{1,0:T(8,128)(2,1)S(1)}, bf16[704,2048]{1,0:T(8,128)(2,1)}, u32[]{:S(2)}) copy-start(bf16[704,2048]{1,0:T(8,128)(2,1)} %get-tuple-element.75.gate_ref) | copy-start | bytes 8650756
  78.2 7.0 %copy-start.2 = (bf16[704,1024]{1,0:T(8,128)(2,1)S(1)}, bf16[704,1024]{1,0:T(8,128)(2,1)}, u32[]{:S(2)}) copy-start(bf16[704,1024]{1,0:T(8,128)(2,1)} %get-tuple-element.74.normed_ref) | copy-start | bytes 4325380

commit v7 on v6

--- a/solution.py
+++ b/solution.py
@@ -205,8 +205,8 @@
 
 
 def gather_kernel(
-    x_ref, go_ref, dt_ref, rate_ref, taps_ref, vec_ref, xp_ref, wout_ref, win_ref,
-    normed_ref, dtw_ref, xpw_ref, decay_ref, par_ref, gain_ref, wout_out, win_out, dg_out, both_out,
+    x_ref, go_ref, dt_ref, rate_ref, taps_ref, vec_ref, xp_ref, len_ref, wout_ref, win_ref,
+    normed_ref, dtw_ref, xpw_ref, decay_ref, par_ref, gain_ref, off_ref, wout_out, win_out, dg_out, both_out,
     pack, wout, win, dg, both, packed, send, recv, leave, tiles, *, plan
 ):
     f32, bf16 = jnp.float32, jnp.bfloat16
@@ -269,6 +269,21 @@
                 pltpu.make_async_copy(both.at[:, here], both_out.at[:, here], tiles.at[k]).start()
         pltpu.make_async_copy(win.at[at], win_out.at[at], leave.at[1, turn]).start()
 
+    contexts, clusters = len_ref.shape
+    span = rows // contexts
+    for c in range(contexts):
+        starts = [jnp.int32(0)]
+        for k in range(clusters - 1):
+            starts.append(starts[-1] + len_ref[c, k])
+
+        @pl.loop(0, span // 64)
+        def _(k):
+            spot = lax.broadcasted_iota(jnp.int32, (64, 128), 0) + k * 64
+            value = spot
+            for first in starts[1:]:
+                value = jnp.where(spot >= first, spot - first, value)
+            off_ref[pl.ds(pl.multiple_of(c * span + k * 64, 64), 64), :] = value
+
     copies(1, 0).wait()
     times_out(0)
     for turn in range(plan.size):
@@ -309,7 +324,7 @@
         pltpu.make_async_copy(both.at[:, here], both_out.at[:, here], tiles.at[k]).wait()
 
 
-def gather_weights(x, grad_rows, small, w_out, w_in):
+def gather_weights(x, grad_rows, small, lengths, w_out, w_in):
     f32, bf16 = jnp.float32, jnp.bfloat16
     plan = Exchange(lax.axis_size("fsdp"))
     n, (rows, model), wide = plan.size, x.shape, w_in.shape[1]
@@ -321,13 +336,13 @@
         ((rank + states + 16 + cols, inner), bf16), ((n,) + w_out.shape, bf16), ((n,) + w_in.shape, bf16), ((rows, inner), f32), ((rows, wide), f32),
     ]
     outs = [
-        (x.shape, bf16), ((rank, inner), bf16), ((cols, inner), bf16), ((states, inner), f32), ((8, inner), f32), ((8, model), f32),
+        (x.shape, bf16), ((rank, inner), bf16), ((cols, inner), bf16), ((states, inner), f32), ((8, inner), f32), ((8, model), f32), ((rows, 128), jnp.int32),
     ]
     *made, out_all, in_all, d_gated, both = pl.pallas_call(
         functools.partial(gather_kernel, plan=plan),
         out_shape=[jax.ShapeDtypeStruct(*s) for s in outs + shapes[1:]],
-        in_specs=[near] * 7 + [anywhere] * 2,
-        out_specs=[near] * 6 + [anywhere] * 4,
+        in_specs=[near] * 7 + [pl.BlockSpec(memory_space=pltpu.SMEM)] + [anywhere] * 2,
+        out_specs=[near] * 7 + [anywhere] * 4,
         scratch_shapes=[pltpu.VMEM(*s) for s in shapes]
         + [
             pltpu.VMEM((shapes[0][0][0], share), bf16),
@@ -338,7 +353,7 @@
         ],
         compiler_params=pltpu.CompilerParams(collective_id=2, has_side_effects=True, vmem_limit_bytes=56 << 20),
         name="gather_weights",
-    )(x, grad_rows, *small, w_out, w_in)
+    )(x, grad_rows, *small, lengths, w_out, w_in)
     return made, out_all.reshape(-1, w_out.shape[1]), in_all.reshape(-1, wide), d_gated, both
 
 
@@ -429,7 +444,7 @@
             dtm[2 * k + j] = jnp.where(off_ref[...] > 0, delta[:, part], BIG)
             dtu[2 * k + j] = grown[:, part]
 
-    @pl.loop(0, tiles // width)
+    @pl.loop(0, tiles // width, unroll=2)
     def _(cb):
         tile = cb * width
         base = pl.multiple_of(cb * 128 * width, 128 * width)
@@ -964,19 +979,6 @@
     )(upper, gate, out, small, layer, left, gain)
 
 
-def cluster_offsets(lengths, total_len):
-    count = lengths.shape[1]
-    ahead = jnp.arange(count)[:, None] < jnp.arange(count)[None, :]
-    start_points = jnp.sum(jnp.where(ahead[None], lengths[:, :, None], 0), axis=1, dtype=jnp.int32)
-    end_points = start_points + lengths
-    where_at = jnp.arange(total_len, dtype=jnp.int32)
-    inside = (where_at[None, None, :] >= start_points[:, :, None]) & (
-        where_at[None, None, :] < end_points[:, :, None]
-    )
-    first_spot = jnp.sum(jnp.where(inside, start_points[:, :, None], 0), axis=1, dtype=jnp.int32)
-    return where_at[None, :] - first_spot
-
-
 def dot32(left, right, contract):
     return lax.dot_general(left, right, (contract, ((), ())), preferred_element_type=jnp.float32)
 
@@ -1008,14 +1010,12 @@
     contexts_here, total_len, model_dim = hidden_in.shape
     rows = contexts_here * total_len
     columns = rank_dim + 2 * state_dim
-    offsets = cluster_offsets(cluster_lengths, total_len).reshape(rows)
-    offset = jnp.broadcast_to(offsets[:, None], (rows, 128))
     grad_rows = out_grad.reshape(rows, model_dim)
     gain_part = jnp.pad(norm_gain, (0, share - norm_gain.shape[0]))
     vectors = jnp.concatenate([gain_part, conv_bias, dt_bias, skip_gain]).reshape(-1, 128)
     x = hidden_in.reshape(rows, model_dim)
-    (normed16, w_dt, xp, rate2, params, gain), w_out, w_in, d_gated, both = gather_weights(
-        x, grad_rows, (dt_proj, a_log, conv_weight, vectors, x_proj.T), out_proj, in_proj
+    (normed16, w_dt, xp, rate2, params, gain, offset), w_out, w_in, d_gated, both = gather_weights(
+        x, grad_rows, (dt_proj, a_log, conv_weight, vectors, x_proj.T), cluster_lengths, out_proj, in_proj
     )
     inner_dim = params.shape[1]
     parts = lax.axis_size("fsdp")

time: 281 us -> 276 us (0.982)
  no operation moved by 1% of the time
where the time goes in v7:
time: 276 us
  Pallas kernels  261 us (95%)
  matrix products  12 us (4%)
    pallas_call x1, Pallas kernels, scan_backward(): pl.pallas_call(functools.partial(backward_kernel, width=width, plan=plan,...  114 us
    pallas_call x1, Pallas kernels, finish(): pl.pallas_call(functools.partial(finish_kernel, plan=plan), out_shape=sum...  64.5 us
    pallas_call x1, Pallas kernels, scan_forward(): pl.pallas_call(functools.partial(forward_kernel, width=width), grid=(n,),...  45.2 us
    pallas_call x1, Pallas kernels, gather_weights(): pl.pallas_call(functools.partial(gather_kernel, plan=plan), out_shape=[ja...  25.6 us
    dot_general x2, matrix products, dot32(): lax.dot_general(left, right, (contract, ((), ())), preferred_element_type...  12 us
    pallas_call x1, Pallas kernels, write_outputs(): pl.pallas_call(write_kernel, grid=(steps,), in_specs=[part(upper), part(g...  11.7 us

profile of v7, /device:TPU:0, one launch (start us, length us, event | category | flops | bytes accessed | tf_op | source)
XLA Modules:
  0.0 275.5 jit_solution(1178978172943713736)
XLA Ops:
  0.6 0.7 pad_bitcast_fusion
  1.3 1.3 pad_maximum_fusion.vec_ref
  2.6 25.6 %gather_weights.1 = (bf16[704,1024]{1,0:T(8,128)(2,1)}, bf16[64,2048]{1,0:T(8,128)(2,1)}, bf16[96,2048]{1,0:T(8,128)(2,1)}, f32[16,2048]{1,0:T(8,128)}, f32[8,20...) custom-call(bf16[704,1024]{1,0:T(8,128)(2,1)} %bitcast.30, ...), custom_call_target="tpu_custom_call" | custom-call | tf_op jit(solution)/shard_map/gather_weights/pallas_call | solution.py:341
  28.3 0.0 copy-start
  28.3 45.2 %scan_forward.1 = (f32[704,2048]{1,0:T(8,128)}, f32[704,2048]{1,0:T(8,128)}, f32[704,2048]{1,0:T(8,128)}, f32[704,2048]{1,0:T(8,128)}, f32[704,2048]{1,0:T(8,128...) custom-call(f32[704,4096]{1,0:T(8,128)} %get-tuple-element.57.upper_, ...), custom_call_target="tpu_custom_call" | custom-call | tf_op jit(solution)/shard_map/scan_forward/pallas_call | solution.py:505
  73.5 0.0 copy-done
  73.5 0.0 copy-start.1
  73.5 0.0 copy-start.2
  73.5 7.0 %convolution_convert_fusion.1 = bf16[2048,1024]{1,0:T(8,128)(2,1)} fusion(bf16[704,2048]{1,0:T(8,128)(2,1)} %get-tuple-element.75.gated_ref, bf16[1,704,1024]{2,1,0:T(8,128)(2,1)S(1)} %copy-done), kind=kOutput, calls=%fused_computation.1 | convolution fusion | flops 2954887168 | bytes 8519680 | tf_op jit(solution)/shard_map/dot_general | solution.py:983
  80.5 0.0 copy-done.1
  80.5 0.0 copy-done.2
  80.5 5.0 %convolution_convert_fusion = bf16[1024,2048]{1,0:T(8,128)(2,1)} fusion(bf16[704,1024]{1,0:T(8,128)(2,1)S(1)} %copy-done.2, bf16[704,2048]{1,0:T(8,128)(2,1)S(1)} %copy-done.1), kind=kOutput, calls=%fused_computation | convolution fusion | flops 2954887168 | bytes 8519680 | tf_op jit(solution)/shard_map/dot_general | solution.py:983
  85.5 113.6 %scan_backward.1 = (bf16[704,2048]{1,0:T(8,128)(2,1)}, bf16[512,1024]{1,0:T(8,128)(2,1)}, bf16[16,64,1024]{2,1,0:T(8,128)(2,1)}, bf16[16,32,2048]{2,1,0:T(8,128)(2,1)}) custom-call(f32[704,2048]{1,0:T(8,128)} %get-tuple-element.64.u_ref, f32[704,2048]{1,0:T(8,128)} %get-tuple-element.65.ds_ref, f32[704,2048]{1,0:T(8,128)} %get-tuple-element.66.dt_ref, ...), custom_call_target="tpu_custom_call" | custom-call | tf_op jit(solution)/shard_map/scan_backward/pallas_call | solution.py:719
  199.1 64.5 %finish.1 = (bf16[16,32,2048]{2,1,0:T(8,128)(2,1)}, bf16[16,16,1024]{2,1,0:T(8,128)(2,1)}, bf16[704,1024]{1,0:T(8,128)(2,1)}, f32[704,1024]{1,0:T(8,128)}, f32[8,512]{1,0:T(8,128)}) custom-call(bf16[32,16,1024]{2,1,0:T(8,128)(2,1)} %bitcast.40, bf16[704,1024]{1,0:T(8,128)(2,1)} %get-tuple-element.76.normed_ref, ...), custom_call_target="tpu_custom_call" | custom-call | tf_op jit(solution)/shard_map/finish/pallas_call | solution.py:901
  263.7 11.7 %write_outputs.1 = (f32[512,4096]{1,0:T(8,128)}, f32[1024,1024]{1,0:T(8,128)}, f32[96,1024]{1,0:T(8,128)}, f32[64,1024]{1,0:T(8,128)}, f32[16,1024]{1,0:T(8,128)...) custom-call(bf16[512,2048]{1,0:T(8,128)(2,1)} %bitcast.39, ...), custom_call_target="tpu_custom_call" | custom-call | tf_op jit(solution)/shard_map/write_outputs/pallas_call | solution.py:971
Async XLA Ops:
  28.3 45.2 %copy-start = (bf16[1,704,1024]{2,1,0:T(8,128)(2,1)S(1)}, bf16[1,704,1024]{2,1,0:T(8,128)(2,1)}, u32[]{:S(2)}) copy-start(bf16[1,704,1024]{2,1,0:T(8,128)(2,1)} %param.25) | copy-start | bytes 4325380
  73.5 7.0 %copy-start.1 = (bf16[704,2048]{1,0:T(8,128)(2,1)S(1)}, bf16[704,2048]{1,0:T(8,128)(2,1)}, u32[]{:S(2)}) copy-start(bf16[704,2048]{1,0:T(8,128)(2,1)} %get-tuple-element.77.gate_ref) | copy-start | bytes 8650756
  73.5 7.0 %copy-start.2 = (bf16[704,1024]{1,0:T(8,128)(2,1)S(1)}, bf16[704,1024]{1,0:T(8,128)(2,1)}, u32[]{:S(2)}) copy-start(bf16[704,1024]{1,0:T(8,128)(2,1)} %get-tuple-element.76.normed_ref) | copy-start | bytes 4325380
